TPU v7x, 512 devices: a whole 4x4x16 slice. The times are simulated.
512 devices in a mesh: wide: 128 (over z, x, core), narrow: 4 (over y).
Axes of the slice: x: 4, y: 4, z: 16, core: 2. Of those that a mesh axis runs over, the one named last changes fastest.
Arguments:
- tokens_in: bfloat16 [16384, 2560], P('wide', 'narrow'), may hold values from -6 to 6
- norm_gain: bfloat16 [2560], replicated, may hold values from 0.099609375 to 1.8984375
- query_weight: bfloat16 [2560, 2560], P('wide', 'narrow'), may hold values from -0.25 to 0.25
- key_weight: bfloat16 [2560, 640], P('wide', 'narrow'), may hold values from -0.125 to 0.125
- value_weight: bfloat16 [2560, 640], P('wide', 'narrow'), may hold values from -0.5 to 0.5
- out_weight: bfloat16 [2560, 2560], P('wide', 'narrow'), may hold values from -0.125 to 0.125
- cache_keys: bfloat16 [640, 131072], P('narrow', 'wide'), may hold values from -64 to 64
- cache_values: bfloat16 [640, 131072], P('narrow', 'wide'), may hold values from -24 to 24
- cached_len: int32 [32], replicated, may hold values from 1 to 4096, as said below
- append_slot: int32 [32], replicated, may hold values from 0 to 4095
- shard_owner: int32 [32], replicated, may hold values from 0 to 3
Outputs:
- attention_update: bfloat16 [16384, 2560], P('wide', 'narrow')
- appended_keys: bfloat16 [640, 131072], P('narrow', 'wide')
- appended_values: bfloat16 [640, 131072], P('narrow', 'wide')
Inputs may be any that keep to these rules, and one draw needn't show every extreme that they name: `cached_len`: each request's number of cached keys; some request holds 4096.
All inputs are finite; a program needn't handle non-finite values.
Results may differ from a plain program's by a relative error of at most 0.012.
The roundings to bfloat16 on the way count: a program that leaves them out, or rounds other values in their place, can miss the bound.
Values may be sent and summed in bfloat16 or wider, within the bound.
A program may use at most 64 MiB of HBM per device.

v0:
```python
import math

import jax
import jax.numpy as jnp
from jax import lax
from jax.sharding import PartitionSpec as P

HEAD_DIM = 80
WIN = 4096
GROUP_BITS = 2
GROUP = 4


EPSILON = 1e-05
ROPE_BASE = 10000.0
LOWEST = -1e30


def from_partner(block, axis, bit):
    count = lax.axis_size(axis)
    route = []
    for low in range(count):
        high = low | 1 << bit
        if high != low and high < count:
            route += [(low, high), (high, low)]
    return lax.ppermute(block, axis, route)


def rms_normed(rows_in, gain):
    values = rows_in.astype(jnp.float32)
    scaling = lax.rsqrt(jnp.mean(values * values, axis=-1, keepdims=True) + EPSILON)
    return (values * scaling * gain.astype(jnp.float32)).astype(jnp.bfloat16)


def rotate(values, positions):
    half_dim = values.shape[-1] // 2
    inverse = ROPE_BASE ** (-(jnp.arange(half_dim, dtype=jnp.float32) * (2.0 / values.shape[-1])))
    angles = positions.astype(jnp.float32)[:, None] * inverse[None, :]
    cos_part = jnp.cos(angles)[:, None, :]
    sin_part = jnp.sin(angles)[:, None, :]
    lower = values[..., :half_dim]
    higher = values[..., half_dim:]
    return jnp.concatenate(
        [lower * cos_part - higher * sin_part, higher * cos_part + lower * sin_part], axis=-1
    )


def ordered(mine, other, upper, along):
    first_half = jnp.where(upper, other, mine)
    second_half = jnp.where(upper, mine, other)
    return jnp.concatenate([first_half, second_half], axis=along)


def empty_state(row_count, groups, repeats):
    return (
        jnp.zeros((row_count, groups, repeats, HEAD_DIM), jnp.float32),
        jnp.full((row_count, groups, repeats), LOWEST, jnp.float32),
        jnp.zeros((row_count, groups, repeats), jnp.float32),
    )


def fold_keys(state, queries, query_pos, keys, values, key_pos, key_ok, widest):
    key_count = keys.shape[1]
    groups = queries.shape[1]
    block = math.gcd(key_count, widest)
    keys_split = keys.reshape(groups, HEAD_DIM, key_count)
    values_split = values.reshape(groups, HEAD_DIM, key_count)
    scale = HEAD_DIM ** (-0.5)

    def step(index, carry):
        accum, top_old, sum_old = carry
        start = index * block
        block_keys = lax.dynamic_slice_in_dim(keys_split, start, block, 2)
        block_values = lax.dynamic_slice_in_dim(values_split, start, block, 2)
        block_pos = lax.dynamic_slice_in_dim(key_pos, start, block, 0)
        block_ok = lax.dynamic_slice_in_dim(key_ok, start, block, 0)
        scores = (
            jnp.einsum("tgrd,gdk->tgrk", queries, block_keys, preferred_element_type=jnp.float32)
            * scale
        )
        allowed = (
            block_ok[None, :]
            & (block_pos[None, :] <= query_pos[:, None])
            & (query_pos[:, None] - block_pos[None, :] < WIN)
        )
        allowed = allowed[:, None, None, :]
        top_new = jnp.maximum(top_old, jnp.max(jnp.where(allowed, scores, LOWEST), axis=-1))
        weights = jnp.where(allowed, jnp.exp(scores - top_new[..., None]), 0.0)
        rescale = jnp.exp(top_old - top_new)
        sum_new = sum_old * rescale + jnp.sum(weights, axis=-1)
        mixed = jnp.einsum(
            "tgrk,gdk->tgrd",
            weights.astype(jnp.bfloat16),
            block_values,
            preferred_element_type=jnp.float32,
        )
        return (accum * rescale[..., None] + mixed, top_new, sum_new)

    return lax.fori_loop(0, key_count // block, step, state)


def shards(
    tokens_in,
    norm_gain,
    query_weight,
    key_weight,
    value_weight,
    out_weight,
    cache_keys,
    cache_values,
    cached_len,
    append_slot,
    shard_owner,
):
    whole = lax.all_gather(tokens_in, "narrow", axis=1, tiled=True)
    normed = rms_normed(whole, norm_gain)
    tok_rows = whole.shape[0]
    query_width = query_weight.shape[1]
    kv_width = key_weight.shape[1]
    local_heads = query_width // HEAD_DIM
    local_groups = kv_width // HEAD_DIM
    repeats = local_heads // local_groups
    columns = normed
    query_sum = jnp.dot(
        columns,
        lax.all_gather(query_weight, "wide", axis=0, tiled=True),
        preferred_element_type=jnp.float32,
    )
    key_sum = jnp.dot(
        columns,
        lax.all_gather(key_weight, "wide", axis=0, tiled=True),
        preferred_element_type=jnp.float32,
    )
    value_sum = jnp.dot(
        columns,
        lax.all_gather(value_weight, "wide", axis=0, tiled=True),
        preferred_element_type=jnp.float32,
    )
    position = lax.axis_index("wide")
    request = position // GROUP
    place = position % GROUP
    length = cached_len[request]
    offset = append_slot[request]
    owner = shard_owner[request]
    query_pos = length + place * tok_rows + jnp.arange(tok_rows, dtype=jnp.int32)
    queries = rotate(query_sum.reshape(tok_rows, local_heads, HEAD_DIM), query_pos).astype(
        jnp.bfloat16
    )
    queries = queries.reshape(tok_rows, local_groups, repeats, HEAD_DIM)
    new_keys = (
        rotate(key_sum.reshape(tok_rows, local_groups, HEAD_DIM), query_pos)
        .astype(jnp.bfloat16)
        .reshape(tok_rows, kv_width)
    )
    new_values = value_sum.astype(jnp.bfloat16)
    shard_rows = cache_keys.shape[1]
    within = jnp.arange(shard_rows, dtype=jnp.int32)
    cycle_mine = (place - owner) % GROUP * shard_rows + within
    old_keys, old_values = (cache_keys, cache_values)
    for bit in range(GROUP_BITS):
        upper = place // 2**bit % 2 == 1
        other_keys, other_values, other_old_keys, other_old_values = from_partner(
            (new_keys, new_values, old_keys, old_values), "wide", bit
        )
        new_keys = ordered(new_keys, other_keys, upper, 0)
        new_values = ordered(new_values, other_values, upper, 0)
        old_keys = ordered(old_keys, other_old_keys, upper, 1)
        old_values = ordered(old_values, other_old_values, upper, 1)
    slot_index = jnp.arange(old_keys.shape[1], dtype=jnp.int32)
    cycle = (slot_index // shard_rows - owner) % GROUP * shard_rows + slot_index % shard_rows
    cached_pos = (cycle - offset + length) % WIN
    state = fold_keys(
        empty_state(tok_rows, local_groups, repeats),
        queries,
        query_pos,
        old_keys,
        old_values,
        cached_pos,
        cached_pos < length,
        512,
    )
    key_cols = new_keys.T
    value_cols = new_values.T
    new_count = key_cols.shape[1]
    new_pos = length + jnp.arange(new_count, dtype=jnp.int32)
    state = fold_keys(
        state,
        queries,
        query_pos,
        key_cols,
        value_cols,
        new_pos,
        jnp.ones((new_count,), dtype=bool),
        512,
    )
    accum, top_score, total = state
    attended = (accum / total[..., None]).astype(jnp.bfloat16).reshape(tok_rows, query_width)
    all_heads = lax.all_gather(attended, "narrow", axis=1, tiled=True)
    columns = all_heads
    update = jnp.dot(
        columns,
        lax.all_gather(out_weight, "wide", axis=0, tiled=True),
        preferred_element_type=jnp.float32,
    ).astype(jnp.bfloat16)
    new_index = (cycle_mine - offset) % WIN
    written = new_index < new_count
    take_rows = jnp.minimum(new_index, new_count - 1)
    put_keys = jnp.where(written[None, :], jnp.take(key_cols, take_rows, axis=1), cache_keys)
    put_values = jnp.where(written[None, :], jnp.take(value_cols, take_rows, axis=1), cache_values)
    return (update, put_keys, put_values)


def solution(mesh):
    in_specs = (
        P("wide", "narrow"),
        P(),
        P("wide", "narrow"),
        P("wide", "narrow"),
        P("wide", "narrow"),
        P("wide", "narrow"),
        P("narrow", "wide"),
        P("narrow", "wide"),
        P(),
        P(),
        P(),
    )
    out_specs = (P("wide", "narrow"), P("narrow", "wide"), P("narrow", "wide"))
    return jax.shard_map(shards, mesh=mesh, in_specs=in_specs, out_specs=out_specs, check_vma=False)
```

profile of v0, /device:TPU:1, one launch (start us, length us, event | category | flops | bytes accessed | tf_op | source)
XLA Modules:
  0.0 399.1 jit_solution(11105308332598685223)
XLA Ops:
  8.0 109.3 %all-gather.2 = bf16[128,20,160]{2,1,0:T(8,128)(2,1)S(1)} all-gather(bf16[1,20,160]{2,1,0:T(8,128)(2,1)} %bitcast.135), channel_id=1, replica_groups=mesh['wide'=128,'narrow'=4] {'wide'}, dimensions={0}, use_global_device_ids=true | all-gather | bytes 825600 | tf_op jit(solution)/shard_map/all_gather | solution.py:136
  117.9 12.4 %all_gather.18 = bf16[128,2560]{1,0:T(8,128)(2,1)S(1)} all-gather(bf16[128,640]{1,0:T(8,128)(2,1)} %param.15), channel_id=1, replica_groups=mesh['wide'=128,'narrow'=4] {'narrow'}, dimensions={1}, use_global_device_ids=true | all-gather | bytes 819200 | tf_op jit(solution)/shard_map/all_gather | solution.py:115
  131.8 4.1 %collective-permute-start.6 = (bf16[128,160]{0,1:T(8,128)(2,1)}, bf16[128,160]{0,1:T(8,128)(2,1)}, u32[]{:S(2)}, u32[]{:S(2)}) collective-permute-start(bf16[128,160]{0,1:T(8,128)(2,1)} %convolution_convert_fusion.1), channel_id=1, source_target_pairs={{0,4},{4,0},{8,12},{12,8},{16,20},{20,16},{24,28},{28,24},{32,36},... | collective-permute-start | bytes 122888 | tf_op jit(solution)/shard_map/ppermute | solution.py:26
  135.9 100.1 %all-gather.1 = bf16[128,20,160]{2,1,0:T(8,128)(2,1)S(1)} all-gather(bf16[1,20,160]{2,1,0:T(8,128)(2,1)} %bitcast.136), channel_id=1, replica_groups=mesh['wide'=128,'narrow'=4] {'wide'}, dimensions={0}, use_global_device_ids=true | all-gather | bytes 825600 | tf_op jit(solution)/shard_map/all_gather | solution.py:131
  239.4 2.1 collective-permute-start.4
  241.5 2.3 collective-permute-start.2
  243.8 2.3 collective-permute-start
  248.0 2.5 broadcast_compare_fusion
  250.5 2.5 add_select_fusion
  259.2 1.9 collective-permute-start.7
  261.2 3.4 collective-permute-start.5
  270.1 2.8 collective-permute-start.1
  274.7 5.3 %gather_fusion.1 = bf16[1024,160]{1,0:T(8,128)(2,1)} fusion(bf16[160,512]{0,1:T(8,128)(2,1)S(1)} %copy.40, s32[1024]{0:T(1024)} %fusion.54), kind=kCustom, calls=%fused_computation.1.clone | custom fusion | bytes 659456 | tf_op jit(solution)/shard_map/jit(_take)/gather | solution.py:209
  280.0 5.3 %gather_fusion = bf16[1024,160]{1,0:T(8,128)(2,1)} fusion(bf16[160,512]{0,1:T(8,128)(2,1)S(1)} %copy.38, s32[1024]{0:T(1024)} %fusion.54), kind=kCustom, calls=%fused_computation.clone | custom fusion | bytes 659456 | tf_op jit(solution)/shard_map/jit(_take)/gather | solution.py:208
  285.3 2.5 bitcast_select_fusion.2
  287.8 1.9 copy.42
  290.7 2.4 collective-permute-start.3
  295.8 11.1 %collective-permute-done.3 = bf16[160,2048]{1,0:T(8,128)(2,1)S(1)} collective-permute-done((bf16[160,2048]{1,0:T(8,128)(2,1)S(1)}, bf16[160,2048]{1,0:T(8,128)(2,1)S(1)}, u32[]{:S(2)}, u32[]{:S(2)}) %collective-permute-start.3) | collective-permute-done | bytes 655392 | tf_op jit(solution)/shard_map/ppermute | solution.py:26
  308.4 6.1 %reshape.265 = bf16[2560,640]{1,0:T(8,128)(2,1)} reshape(bf16[128,20,640]{2,1,0:T(8,128)(2,1)} %all-gather.7.cloned.1.call-done) | data formatting | bytes 6553600
  314.5 3.4 fusion.64
  318.1 41.1 %while.5 = (s32[]{:T(128)}, f32[128,2,4,80]{0,3,2,1:T(8,128)S(1)}, f32[128,2,4]{0,2,1:T(4,128)S(1)}, f32[128,2,4]{0,2,1:T(4,128)S(1)}, pred[4096]{0:T(1024)(128)...) while((s32[]{:T(128)}, f32[128,2,4,80]{0,3,2,1:T(8,128)S(1)}, ...), condition=%wide.region_4.5_spmd.clone, body=%wide.region_1.4_spmd.clone.sunk | while | flops 174118016 | bytes 7774939 | solution.py:99
  321.7 1.5 fusion.89
  326.8 1.5 fusion.89
  331.9 1.5 fusion.89
  337.0 1.5 fusion.89
  342.1 1.5 fusion.89
  347.3 1.5 fusion.89
  357.6 1.5 fusion.89
  360.7 11.0 %all_gather.22 = bf16[128,2560]{0,1:T(8,128)(2,1)S(1)} all-gather(bf16[128,640]{0,1:T(8,128)(2,1)S(1)} %bitcast.129), channel_id=1, replica_groups=mesh['wide'=128,'narrow'=4] {'narrow'}, dimensions={1}, use_global_device_ids=true | all-gather | bytes 819200 | tf_op jit(solution)/shard_map/all_gather | solution.py:198
  371.7 11.2 %all-gather.9.cloned.1.call-done = bf16[128,20,640]{2,1,0:T(8,128)(2,1)} async-done(((bf16[1,20,640]{2,1,0:T(8,128)(2,1)}), bf16[128,20,640]{2,1,0:T(8,128)(2,1)}) %all-gather.9.cloned.1.call-update) | async-done | bytes 3276816 | tf_op jit(solution)/shard_map/all_gather | solution.py:202
  382.9 6.1 %reshape.271 = bf16[2560,640]{1,0:T(8,128)(2,1)} reshape(bf16[128,20,640]{2,1,0:T(8,128)(2,1)} %all-gather.9.cloned.1.call-done) | data formatting | bytes 6553600
  389.0 3.3 convolution_convert_fusion
  (166 shorter events, 57.0 us)
Async XLA Ops:
  7.2 301.2 %all-gather.7.cloned.1.call-start = ((), (), s32[]{:S(2)}) async-start(), calls=%async_computation | async-start | bytes 3962880 | tf_op jit(solution)/shard_map/all_gather | solution.py:126
  7.9 375.0 %all-gather.9.cloned.1.call-start = ((), (), s32[]{:S(2)}) async-start(), calls=%async_computation.1 | async-start | bytes 3962880 | tf_op jit(solution)/shard_map/all_gather | solution.py:202
  7.9 109.9 %copy-start.10 = (bf16[2560]{0:T(1024)(128)(2,1)S(1)}, bf16[2560]{0:T(1024)(128)(2,1)}, u32[]{:S(2)}) copy-start(bf16[2560]{0:T(1024)(128)(2,1)} %param.16) | copy-start | bytes 15364
  130.5 108.2 %copy-start.11 = (f32[128]{0:T(128)}, f32[128]{0:T(128)S(1)}, u32[]{:S(2)}) copy-start(f32[128]{0:T(128)S(1)} %add_rsqrt_fusion) | copy-start | bytes 1540
  131.8 126.6 %collective-permute-start.6 = (bf16[128,160]{0,1:T(8,128)(2,1)}, bf16[128,160]{0,1:T(8,128)(2,1)}, u32[]{:S(2)}, u32[]{:S(2)}) collective-permute-start(bf16[128,160]{0,1:T(8,128)(2,1)} %convolution_convert_fusion.1), channel_id=1, source_target_pairs={{0,4},{4,0},{8,12},{12,8},{16,20},{20,16},{24,28},{28,24},{32,36},... | collective-permute-start | bytes 122888 | tf_op jit(solution)/shard_map/ppermute | solution.py:26
  236.6 4.9 %copy-start = (bf16[160,1024]{1,0:T(8,128)(2,1)S(1)}, bf16[160,1024]{1,0:T(8,128)(2,1)}, u32[]{:S(2)}) copy-start(bf16[160,1024]{1,0:T(8,128)(2,1)} %param.22) | copy-start | bytes 983044
  236.6 10.1 %copy-start.13 = (s32[32]{0:T(128)S(1)}, s32[32]{0:T(128)}, u32[]{:S(2)}) copy-start(s32[32]{0:T(128)} %param.24) | copy-start | bytes 388
  236.6 10.8 %copy-start.14 = (s32[32]{0:T(128)S(1)}, s32[32]{0:T(128)}, u32[]{:S(2)}) copy-start(s32[32]{0:T(128)} %param.25) | copy-start | bytes 388
  238.8 19.6 %copy-start.4 = (f32[128,40]{0,1:T(8,128)}, f32[128,40]{0,1:T(8,128)S(1)}, u32[]{:S(2)}) copy-start(f32[128,40]{0,1:T(8,128)S(1)} %get-tuple-element.305) | copy-start | bytes 61444
  238.8 19.6 %copy-start.6 = (f32[128,40]{0,1:T(8,128)}, f32[128,40]{0,1:T(8,128)S(1)}, u32[]{:S(2)}) copy-start(f32[128,40]{0,1:T(8,128)S(1)} %get-tuple-element.306) | copy-start | bytes 61444
  239.4 18.9 %collective-permute-start.4 = (bf16[128,160]{0,1:T(8,128)(2,1)S(1)}, bf16[128,160]{0,1:T(8,128)(2,1)S(1)}, u32[]{:S(2)}, u32[]{:S(2)}) collective-permute-start(bf16[128,160]{0,1:T(8,128)(2,1)S(1)} %bitcast.127), channel_id=1, source_target_pairs={{0,4},{4,0},{8,12},{12,8},{16,20},{20,16},{24,28},{28,24},{32,36},... | collective-permute-start | bytes 122888 | tf_op jit(solution)/shard_map/ppermute | solution.py:26
  241.5 25.5 %collective-permute-start.2 = (bf16[160,1024]{1,0:T(8,128)(2,1)S(1)}, bf16[160,1024]{1,0:T(8,128)(2,1)S(1)}, u32[]{:S(2)}, u32[]{:S(2)}) collective-permute-start(bf16[160,1024]{1,0:T(8,128)(2,1)S(1)} %copy-done), channel_id=1, source_target_pairs={{0,4},{4,0},{8,12},{12,8},{16,20},{20,16},{24,28},{28,24},{32,36},... | collective-permute-start | bytes 983048 | tf_op jit(solution)/shard_map/ppermute | solution.py:26
  243.8 24.0 %collective-permute-start = (bf16[160,1024]{1,0:T(8,128)(2,1)}, bf16[160,1024]{1,0:T(8,128)(2,1)}, u32[]{:S(2)}, u32[]{:S(2)}) collective-permute-start(bf16[160,1024]{1,0:T(8,128)(2,1)} %param.21), channel_id=1, source_target_pairs={{0,4},{4,0},{8,12},{12,8},{16,20},{20,16},{24,28},{28,24},{32,36},... | collective-permute-start | bytes 983048 | tf_op jit(solution)/shard_map/ppermute | solution.py:26
  259.2 5.7 %collective-permute-start.7 = (bf16[256,160]{0,1:T(8,128)(2,1)S(1)}, bf16[256,160]{0,1:T(8,128)(2,1)S(1)}, u32[]{:S(2)}, u32[]{:S(2)}) collective-permute-start(bf16[256,160]{0,1:T(8,128)(2,1)S(1)} %pad_maximum_fusion.8), channel_id=1, source_target_pairs={{0,8},{8,0},{4,12},{12,4},{16,24},{24,16},{20,28},{28,20},{32,40},... | collective-permute-start | bytes 245768 | tf_op jit(solution)/shard_map/ppermute | solution.py:26
  261.2 5.8 %collective-permute-start.5 = (bf16[256,160]{0,1:T(8,128)(2,1)S(1)}, bf16[256,160]{0,1:T(8,128)(2,1)S(1)}, u32[]{:S(2)}, u32[]{:S(2)}) collective-permute-start(bf16[256,160]{0,1:T(8,128)(2,1)S(1)} %pad_maximum_fusion.7), channel_id=1, source_target_pairs={{0,8},{8,0},{4,12},{12,4},{16,24},{24,16},{20,28},{28,20},{32,40},... | collective-permute-start | bytes 245768 | tf_op jit(solution)/shard_map/ppermute | solution.py:26
  267.0 0.7 copy-start.3
  270.1 23.1 %collective-permute-start.1 = (bf16[160,2048]{1,0:T(8,128)(2,1)}, bf16[160,2048]{1,0:T(8,128)(2,1)}, u32[]{:S(2)}, u32[]{:S(2)}) collective-permute-start(bf16[160,2048]{1,0:T(8,128)(2,1)} %pad_maximum_fusion.2), channel_id=1, source_target_pairs={{0,8},{8,0},{4,12},{12,4},{16,24},{24,16},{20,28},{28,20},{32,40},... | collective-permute-start | bytes 1966088 | tf_op jit(solution)/shard_map/ppermute | solution.py:26
  290.7 16.2 %collective-permute-start.3 = (bf16[160,2048]{1,0:T(8,128)(2,1)S(1)}, bf16[160,2048]{1,0:T(8,128)(2,1)S(1)}, u32[]{:S(2)}, u32[]{:S(2)}) collective-permute-start(bf16[160,2048]{1,0:T(8,128)(2,1)S(1)} %pad_maximum_fusion.3), channel_id=1, source_target_pairs={{0,8},{8,0},{4,12},{12,4},{16,24},{24,16},{20,28},{28,20},{32,40},... | collective-permute-start | bytes 1966088 | tf_op jit(solution)/shard_map/ppermute | solution.py:26
  308.4 6.1 %copy-start.12 = (f32[128]{0:T(128)S(1)}, f32[128]{0:T(128)}, u32[]{:S(2)}) copy-start(f32[128]{0:T(128)} %copy-done.11) | copy-start | bytes 1540
  314.5 3.4 copy-start.5
  314.5 3.4 copy-start.7
  314.5 3.5 copy-start.9
  314.5 3.5 copy-start.15
  318.0 41.1 %copy-start.1 = (bf16[512,160]{0,1:T(8,128)(2,1)S(1)}, bf16[512,160]{0,1:T(8,128)(2,1)}, u32[]{:S(2)}) copy-start(bf16[512,160]{0,1:T(8,128)(2,1)} %get-tuple-element.292) | copy-start | bytes 491524
  318.0 41.1 %copy-start.2 = (pred[128,512]{0,1:T(8,128)(4,1)S(1)}, pred[128,512]{0,1:T(8,128)(4,1)}, u32[]{:S(2)}) copy-start(pred[128,512]{0,1:T(8,128)(4,1)} %fusion.38) | copy-start | bytes 196612
  359.2 1.0 copy-start.8
Sparse Core Ops, SparseCore 0:
  11.0 147.4 all-gather.6
  246.2 136.6 all-gather.8
where the time goes:
time: 401 us; the launch traced here: 399 us
  blocking collectives  233 us (58%)
  local copies, waits for them, and re-layouts  44.6 us (11%)
  matrix products  32.8 us (8%)
  other arithmetic  26.6 us (7%)
  waiting for transfers between devices  24.6 us (6%)
  starting transfers between devices  21.3 us (5%)
  between operations  15.9 us (4%)
    all_gather x1, blocking collectives, shards(): lax.all_gather(value_weight, 'wide', axis=0, tiled=True)  109 us
    all_gather x1, blocking collectives, shards(): lax.all_gather(key_weight, 'wide', axis=0, tiled=True)  100 us
    ppermute x8, starting transfers between devices, from_partner(): return lax.ppermute(block, axis, route)  21.2 us
    unnamed x40, local copies, waits for them, and re-layouts  18.5 us
    ppermute x8, waiting for transfers between devices, from_partner(): return lax.ppermute(block, axis, route)  12.7 us
    all_gather x1, blocking collectives, shards(): whole = lax.all_gather(tokens_in, 'narrow', axis=1, tiled=True)  12.4 us
    dot_general x9, matrix products, step(): jnp.einsum('tgrk,gdk->tgrd', weights.astype(jnp.bfloat16), block_values,...  12.2 us
    dot_general x9, matrix products, step(): jnp.einsum('tgrd,gdk->tgrk', queries, block_keys, preferred_element_type=...  12 us
  transfers between devices with their start and end apart: 10, of which 4 were waited for; matrix products, arithmetic and copies ran while one was open for 23% of the time, Pallas kernels for 0%

commit v1 on v0

--- a/solution.py
+++ b/solution.py
@@ -1,9 +1,10 @@
 import math
 
+import numpy as np
 import jax
 import jax.numpy as jnp
 from jax import lax
-from jax.sharding import PartitionSpec as P
+from jax.sharding import Mesh, PartitionSpec as P
 
 HEAD_DIM = 80
 WIN = 4096
@@ -17,13 +18,24 @@
 
 
 def from_partner(block, axis, bit):
-    count = lax.axis_size(axis)
+    count = lax.psum(1, axis)
     route = []
     for low in range(count):
         high = low | 1 << bit
         if high != low and high < count:
             route += [(low, high), (high, low)]
     return lax.ppermute(block, axis, route)
+
+
+WIDE = ("z", "x", "c")
+
+
+def gather_rows(block):
+    rows = block.shape[0]
+    plane = lax.all_gather(block, ("z", "x"), axis=0, tiled=False)
+    both = lax.all_gather(plane, "c", axis=0, tiled=False)
+    both = jnp.transpose(both, (1, 0, 2, 3))
+    return both.reshape(-1, block.shape[1])
 
 
 def rms_normed(rows_in, gain):
@@ -121,22 +133,12 @@
     local_groups = kv_width // HEAD_DIM
     repeats = local_heads // local_groups
     columns = normed
-    query_sum = jnp.dot(
-        columns,
-        lax.all_gather(query_weight, "wide", axis=0, tiled=True),
-        preferred_element_type=jnp.float32,
-    )
-    key_sum = jnp.dot(
-        columns,
-        lax.all_gather(key_weight, "wide", axis=0, tiled=True),
-        preferred_element_type=jnp.float32,
-    )
-    value_sum = jnp.dot(
-        columns,
-        lax.all_gather(value_weight, "wide", axis=0, tiled=True),
-        preferred_element_type=jnp.float32,
-    )
-    position = lax.axis_index("wide")
+    qkv = gather_rows(jnp.concatenate([query_weight, key_weight, value_weight], axis=1))
+    qkv_sum = jnp.dot(columns, qkv, preferred_element_type=jnp.float32)
+    query_sum = qkv_sum[:, :query_width]
+    key_sum = qkv_sum[:, query_width : query_width + kv_width]
+    value_sum = qkv_sum[:, query_width + kv_width :]
+    position = lax.axis_index(WIDE)
     request = position // GROUP
     place = position % GROUP
     length = cached_len[request]
@@ -160,7 +162,7 @@
     for bit in range(GROUP_BITS):
         upper = place // 2**bit % 2 == 1
         other_keys, other_values, other_old_keys, other_old_values = from_partner(
-            (new_keys, new_values, old_keys, old_values), "wide", bit
+            (new_keys, new_values, old_keys, old_values), WIDE, bit
         )
         new_keys = ordered(new_keys, other_keys, upper, 0)
         new_values = ordered(new_values, other_values, upper, 0)
@@ -199,7 +201,7 @@
     columns = all_heads
     update = jnp.dot(
         columns,
-        lax.all_gather(out_weight, "wide", axis=0, tiled=True),
+        gather_rows(out_weight),
         preferred_element_type=jnp.float32,
     ).astype(jnp.bfloat16)
     new_index = (cycle_mine - offset) % WIN
@@ -211,18 +213,15 @@
 
 
 def solution(mesh):
-    in_specs = (
-        P("wide", "narrow"),
-        P(),
-        P("wide", "narrow"),
-        P("wide", "narrow"),
-        P("wide", "narrow"),
-        P("wide", "narrow"),
-        P("narrow", "wide"),
-        P("narrow", "wide"),
-        P(),
-        P(),
-        P(),
-    )
-    out_specs = (P("wide", "narrow"), P("narrow", "wide"), P("narrow", "wide"))
-    return jax.shard_map(shards, mesh=mesh, in_specs=in_specs, out_specs=out_specs, check_vma=False)
+    devices = mesh.devices
+    wide_devices = devices[:, 0]
+    xs = sorted({d.coords[0] for d in wide_devices})
+    cores = sorted({getattr(d, "core_on_chip", 0) for d in wide_devices})
+    n_x, n_c = len(xs), len(cores)
+    n_z = devices.shape[0] // (n_x * n_c)
+    fine = Mesh(devices.reshape(n_z, n_x, n_c, devices.shape[1]), ("z", "x", "c", "narrow"))
+    rows = P(WIDE, "narrow")
+    cols = P("narrow", WIDE)
+    in_specs = (rows, P(), rows, rows, rows, rows, cols, cols, P(), P(), P())
+    out_specs = (rows, cols, cols)
+    return jax.shard_map(shards, mesh=fine, in_specs=in_specs, out_specs=out_specs, check_vma=False)

time: 401 us -> 499 us (1.24)
  waiting for transfers between devices: 24.6 us -> 305 us
  blocking collectives: 233 us -> 23.7 us
  local copies, waits for them, and re-layouts: 44.6 us -> 67.2 us
  starting transfers between devices: 21.3 us -> 30.7 us
  other arithmetic: 26.6 us -> 20.2 us
    all_gather x2 -> x4, waiting for transfers between devices: 11.2 us -> 280 us  [the longest x2 280 us: gather_rows(): plane = lax.all_gather(block, ('z', 'x'), axis=0, tiled=False)]
    all_gather x2 -> x0, blocking collectives: 209 us -> none  [the longest x1 109 us: shards(): lax.all_gather(value_weight, 'wide', axis=0, tiled=True)]
    all_gather x0 -> x4, local copies, waits for them, and re-layouts: none -> 21.6 us  [the longest x2 13.8 us: gather_rows(): both = lax.all_gather(plane, 'c', axis=0, tiled=False)]
    reshape x0 -> x2, local copies, waits for them, and re-layouts: none -> 15.9 us  [gather_rows(): return both.reshape(-1, block.shape[1])]
    unnamed x40 -> x22, local copies, waits for them, and re-layouts: 18.5 us -> 6.84 us
    ppermute x8, waiting for transfers between devices: 12.7 us -> 24.3 us  [from_partner(): return lax.ppermute(block, axis, route)]
    while x8 -> x40, local copies, waits for them, and re-layouts: 0.02 us -> 9.57 us
    ppermute x8, starting transfers between devices: 21.2 us -> 30.5 us  [from_partner(): return lax.ppermute(block, axis, route)]
  transfers between devices with their start and end apart: 10 -> 12, of which waited for: 4 -> 5; matrix products, arithmetic and copies ran while one was open for 23% -> 13% of each run, Pallas kernels for 0% -> 0%
where the time goes in v1:
time: 499 us; the launch traced here: 494 us
  waiting for transfers between devices  305 us (61%)
  local copies, waits for them, and re-layouts  67.2 us (13%)
  matrix products  31.3 us (6%)
  starting transfers between devices  30.7 us (6%)
  blocking collectives  23.7 us (5%)
  other arithmetic  20.2 us (4%)
  between operations  15.5 us (3%)
    all_gather x2, waiting for transfers between devices, gather_rows(): plane = lax.all_gather(block, ('z', 'x'), axis=0, tiled=False)  280 us
    ppermute x8, starting transfers between devices, from_partner(): return lax.ppermute(block, axis, route)  30.5 us
    ppermute x8, waiting for transfers between devices, from_partner(): return lax.ppermute(block, axis, route)  24.3 us
    reshape x2, local copies, waits for them, and re-layouts, gather_rows(): return both.reshape(-1, block.shape[1])  15.9 us
    all_gather x2, local copies, waits for them, and re-layouts, gather_rows(): both = lax.all_gather(plane, 'c', axis=0, tiled=False)  13.8 us
    dot_general x9, matrix products, step(): jnp.einsum('tgrk,gdk->tgrd', weights.astype(jnp.bfloat16), block_values,...  12.2 us
    dot_general x9, matrix products, step(): jnp.einsum('tgrd,gdk->tgrk', queries, block_keys, preferred_element_type=...  12 us
    all_gather x1, blocking collectives, shards(): whole = lax.all_gather(tokens_in, 'narrow', axis=1, tiled=True)  12 us
  transfers between devices with their start and end apart: 12, of which 5 were waited for; matrix products, arithmetic and copies ran while one was open for 13% of the time, Pallas kernels for 0%

profile of v1, /device:TPU:1, one launch (start us, length us, event | category | flops | bytes accessed | tf_op | source)
XLA Modules:
  0.0 493.9 jit_solution(6493536024206706948)
XLA Ops:
  7.9 1.5 maximum_bitcast_fusion
  9.5 138.6 %all-gather.17.cloned.1.call-done = bf16[64,20,640]{2,1,0:T(8,128)(2,1)} async-done(((bf16[1,20,640]{2,1,0:T(8,128)(2,1)}), bf16[64,20,640]{2,1,0:T(8,128)(2,1)}) %all-gather.17.cloned.1.call-update) | async-done | bytes 1638416 | tf_op jit(solution)/shard_map/all_gather | solution.py:35
  148.1 3.0 copy.36
  151.1 141.2 %all-gather.15.cloned.1.call-done = bf16[64,20,960]{2,1,0:T(8,128)(2,1)} async-done(((bf16[1,20,960]{2,1,0:T(8,128)(2,1)}), bf16[64,20,960]{2,1,0:T(8,128)(2,1)}) %all-gather.15.cloned.1.call-update) | async-done | bytes 2457616 | tf_op jit(solution)/shard_map/all_gather | solution.py:35
  292.3 4.8 copy.33
  298.1 10.7 %collective-permute-start.2 = (bf16[160,1024]{1,0:T(8,128)(2,1)S(1)}, bf16[160,1024]{1,0:T(8,128)(2,1)S(1)}, u32[]{:S(2)}, u32[]{:S(2)}) collective-permute-start(bf16[160,1024]{1,0:T(8,128)(2,1)S(1)} %copy-done.1), channel_id=1, source_target_pairs={{0,4},{4,0},{8,12},{12,8},{16,20},{20,16},{24,28},{28,24},{32,36},... | collective-permute-start | bytes 983048 | tf_op jit(solution)/shard_map/ppermute | solution.py:27
  308.8 1.9 collective-permute-start
  317.3 1.9 broadcast_compare_fusion
  319.9 1.9 add_select_fusion
  321.8 12.0 %all_gather.30 = bf16[128,2560]{1,0:T(8,128)(2,1)S(1)} all-gather(bf16[128,640]{1,0:T(8,128)(2,1)S(1)} %copy-done.3), channel_id=1, replica_groups=mesh['z'=16,'x'=4,'c'=2,'narrow'=4] {'narrow'}, dimensions={1}, use_global_device_ids=true | all-gather | bytes 819200 | tf_op jit(solution)/shard_map/all_gather | solution.py:127
  334.3 1.9 collective-permute-start.1
  336.5 3.5 collective-permute-start.3
  340.0 10.3 %collective-permute-done.1 = bf16[160,2048]{1,0:T(8,128)(2,1)S(1)} collective-permute-done((bf16[160,2048]{1,0:T(8,128)(2,1)S(1)}, bf16[160,2048]{1,0:T(8,128)(2,1)S(1)}, u32[]{:S(2)}, u32[]{:S(2)}) %collective-permute-start.1) | collective-permute-done | bytes 655392 | tf_op jit(solution)/shard_map/ppermute | solution.py:27
  351.8 12.6 %collective-permute-done.3 = bf16[160,2048]{1,0:T(8,128)(2,1)S(1)} collective-permute-done((bf16[160,2048]{1,0:T(8,128)(2,1)S(1)}, bf16[160,2048]{1,0:T(8,128)(2,1)S(1)}, u32[]{:S(2)}, u32[]{:S(2)}) %collective-permute-start.3) | collective-permute-done | bytes 655392 | tf_op jit(solution)/shard_map/ppermute | solution.py:27
  365.8 5.7 %copy.53 = bf16[2,64,20,640]{3,2,0,1:T(8,128)(2,1)} copy(bf16[2,64,20,640]{3,1,0,2:T(8,128)(2,1)} %bitcast.126) | data formatting | bytes 6553600 | tf_op jit(solution)/shard_map/all_gather | solution.py:36
  371.5 6.1 %reshape.253 = bf16[2560,640]{1,0:T(8,128)(2,1)} reshape(bf16[64,2,20,640]{3,2,1,0:T(8,128)(2,1)} %bitcast.123) | data formatting | bytes 6553600 | tf_op jit(solution)/shard_map/reshape | solution.py:38
  377.7 8.1 %copy.52 = bf16[2,64,20,960]{3,2,0,1:T(8,128)(2,1)} copy(bf16[2,64,20,960]{3,1,0,2:T(8,128)(2,1)} %bitcast.124) | data formatting | bytes 9830400 | tf_op jit(solution)/shard_map/all_gather | solution.py:36
  385.7 9.8 %reshape.246 = bf16[2560,960]{1,0:T(8,128)(2,1)} reshape(bf16[64,2,20,960]{3,2,1,0:T(8,128)(2,1)} %bitcast.122) | data formatting | bytes 9830400 | tf_op jit(solution)/shard_map/reshape | solution.py:38
  395.5 4.6 fusion.38
  400.2 5.0 %collective-permute-start.6 = (bf16[128,160]{0,1:T(8,128)(2,1)S(1)}, bf16[128,160]{0,1:T(8,128)(2,1)S(1)}, u32[]{:S(2)}, u32[]{:S(2)}) collective-permute-start(bf16[128,160]{0,1:T(8,128)(2,1)S(1)} %slice.49), channel_id=1, source_target_pairs={{0,4},{4,0},{8,12},{12,8},{16,20},{20,16},{24,28},{28,24},{32,36},... | collective-permute-start | bytes 122888 | tf_op jit(solution)/shard_map/ppermute | solution.py:27
  405.3 1.9 collective-permute-start.4
  407.3 39.9 %while.5 = (s32[]{:T(128)}, f32[128,2,4,80]{0,3,2,1:T(8,128)}, f32[128,2,4]{0,2,1:T(4,128)S(1)}, f32[128,2,4]{0,2,1:T(4,128)S(1)}, pred[4096]{0:T(1024)(128)(4,1...) while((s32[]{:T(128)}, f32[128,2,4,80]{0,3,2,1:T(8,128)}, ...), condition=%wide.region_4.5_spmd.clone, body=%wide.region_1.4_spmd.clone.sunk | while | flops 174118016 | bytes 10396435 | solution.py:111
  447.2 1.9 collective-permute-start.7
  449.2 3.6 collective-permute-start.5
  452.9 1.5 collective-permute-done.5
  456.0 11.7 %all_gather.35 = bf16[128,2560]{0,1:T(8,128)(2,1)} all-gather(bf16[128,640]{0,1:T(8,128)(2,1)S(1)} %bitcast.138), channel_id=1, replica_groups=mesh['z'=16,'x'=4,'c'=2,'narrow'=4] {'narrow'}, dimensions={1}, use_global_device_ids=true | all-gather | bytes 819200 | tf_op jit(solution)/shard_map/all_gather | solution.py:200
  468.0 5.0 %gather_fusion.1 = bf16[1024,160]{1,0:T(8,128)(2,1)} fusion(bf16[160,512]{0,1:T(8,128)(2,1)S(1)} %copy.40, s32[1024]{0:T(1024)S(1)} %fusion.58), kind=kCustom, calls=%fused_computation.1.clone | custom fusion | bytes 659456 | tf_op jit(solution)/shard_map/jit(_take)/gather | solution.py:211
  473.0 5.0 %gather_fusion = bf16[1024,160]{1,0:T(8,128)(2,1)} fusion(bf16[160,512]{0,1:T(8,128)(2,1)S(1)} %copy.38, s32[1024]{0:T(1024)S(1)} %fusion.58), kind=kCustom, calls=%fused_computation.clone | custom fusion | bytes 659456 | tf_op jit(solution)/shard_map/jit(_take)/gather | solution.py:210
  478.0 3.0 bitcast_select_fusion.2
  481.0 1.9 copy.42
  482.9 1.9 copy.43
  484.9 2.5 convolution_convert_fusion
  (192 shorter events, 52.8 us)
Async XLA Ops:
  7.2 140.9 %all-gather.17.cloned.1.call-start = ((), (), s32[]{:S(2)}) async-start(), calls=%async_computation.3 | async-start | bytes 1996800 | tf_op jit(solution)/shard_map/all_gather | solution.py:35
  7.9 284.4 %all-gather.15.cloned.1.call-start = ((), (), s32[]{:S(2)}) async-start(), calls=%async_computation.2 | async-start | bytes 3194880 | tf_op jit(solution)/shard_map/all_gather | solution.py:35
  9.5 356.4 %all-gather.13.cloned.1.call-start = ((), (), s32[]{:S(2)}) async-start(), calls=%async_computation.1 | async-start | bytes 4915200 | tf_op jit(solution)/shard_map/all_gather | solution.py:36
  151.1 226.6 %all-gather.11.cloned.1.call-start = ((), (), s32[]{:S(2)}) async-start(), calls=%async_computation | async-start | bytes 7864320 | tf_op jit(solution)/shard_map/all_gather | solution.py:36
  297.1 1.0 copy-start.1
  297.1 11.7 %copy-start.2 = (bf16[160,1024]{1,0:T(8,128)(2,1)S(1)}, bf16[160,1024]{1,0:T(8,128)(2,1)}, u32[]{:S(2)}) copy-start(bf16[160,1024]{1,0:T(8,128)(2,1)} %param.21) | copy-start | bytes 983044
  297.1 14.7 %copy-start.5 = (s32[32]{0:T(128)S(1)}, s32[32]{0:T(128)}, u32[]{:S(2)}) copy-start(s32[32]{0:T(128)} %param.25) | copy-start | bytes 388
  297.1 16.8 %copy-start.4 = (bf16[2560]{0:T(1024)(128)(2,1)S(1)}, bf16[2560]{0:T(1024)(128)(2,1)}, u32[]{:S(2)}) copy-start(bf16[2560]{0:T(1024)(128)(2,1)} %param.16) | copy-start | bytes 15364
  297.1 16.8 %copy-start.6 = (s32[32]{0:T(128)S(1)}, s32[32]{0:T(128)}, u32[]{:S(2)}) copy-start(s32[32]{0:T(128)} %param.23) | copy-start | bytes 388
  297.1 17.4 %copy-start.7 = (s32[32]{0:T(128)S(1)}, s32[32]{0:T(128)}, u32[]{:S(2)}) copy-start(s32[32]{0:T(128)} %param.24) | copy-start | bytes 388
  297.1 24.7 %copy-start.3 = (bf16[128,640]{1,0:T(8,128)(2,1)S(1)}, bf16[128,640]{1,0:T(8,128)(2,1)}, u32[]{:S(2)}) copy-start(bf16[128,640]{1,0:T(8,128)(2,1)} %param.15) | copy-start | bytes 491524
  298.1 36.1 %collective-permute-start.2 = (bf16[160,1024]{1,0:T(8,128)(2,1)S(1)}, bf16[160,1024]{1,0:T(8,128)(2,1)S(1)}, u32[]{:S(2)}, u32[]{:S(2)}) collective-permute-start(bf16[160,1024]{1,0:T(8,128)(2,1)S(1)} %copy-done.1), channel_id=1, source_target_pairs={{0,4},{4,0},{8,12},{12,8},{16,20},{20,16},{24,28},{28,24},{32,36},... | collective-permute-start | bytes 983048 | tf_op jit(solution)/shard_map/ppermute | solution.py:27
  308.8 25.4 %collective-permute-start = (bf16[160,1024]{1,0:T(8,128)(2,1)S(1)}, bf16[160,1024]{1,0:T(8,128)(2,1)S(1)}, u32[]{:S(2)}, u32[]{:S(2)}) collective-permute-start(bf16[160,1024]{1,0:T(8,128)(2,1)S(1)} %copy-done.2), channel_id=1, source_target_pairs={{0,4},{4,0},{8,12},{12,8},{16,20},{20,16},{24,28},{28,24},{32,36},... | collective-permute-start | bytes 983048 | tf_op jit(solution)/shard_map/ppermute | solution.py:27
  334.3 15.9 %collective-permute-start.1 = (bf16[160,2048]{1,0:T(8,128)(2,1)S(1)}, bf16[160,2048]{1,0:T(8,128)(2,1)S(1)}, u32[]{:S(2)}, u32[]{:S(2)}) collective-permute-start(bf16[160,2048]{1,0:T(8,128)(2,1)S(1)} %pad_maximum_fusion.2), channel_id=1, source_target_pairs={{0,8},{8,0},{4,12},{12,4},{16,24},{24,16},{20,28},{28,20},{32,40},... | collective-permute-start | bytes 1966088 | tf_op jit(solution)/shard_map/ppermute | solution.py:27
  336.5 27.9 %collective-permute-start.3 = (bf16[160,2048]{1,0:T(8,128)(2,1)S(1)}, bf16[160,2048]{1,0:T(8,128)(2,1)S(1)}, u32[]{:S(2)}, u32[]{:S(2)}) collective-permute-start(bf16[160,2048]{1,0:T(8,128)(2,1)S(1)} %pad_maximum_fusion.3), channel_id=1, source_target_pairs={{0,8},{8,0},{4,12},{12,4},{16,24},{24,16},{20,28},{28,20},{32,40},... | collective-permute-start | bytes 1966088 | tf_op jit(solution)/shard_map/ppermute | solution.py:27
  400.2 46.9 %collective-permute-start.6 = (bf16[128,160]{0,1:T(8,128)(2,1)S(1)}, bf16[128,160]{0,1:T(8,128)(2,1)S(1)}, u32[]{:S(2)}, u32[]{:S(2)}) collective-permute-start(bf16[128,160]{0,1:T(8,128)(2,1)S(1)} %slice.49), channel_id=1, source_target_pairs={{0,4},{4,0},{8,12},{12,8},{16,20},{20,16},{24,28},{28,24},{32,36},... | collective-permute-start | bytes 122888 | tf_op jit(solution)/shard_map/ppermute | solution.py:27
  405.3 41.9 %collective-permute-start.4 = (bf16[128,160]{0,1:T(8,128)(2,1)S(1)}, bf16[128,160]{0,1:T(8,128)(2,1)S(1)}, u32[]{:S(2)}, u32[]{:S(2)}) collective-permute-start(bf16[128,160]{0,1:T(8,128)(2,1)S(1)} %bitcast.136), channel_id=1, source_target_pairs={{0,4},{4,0},{8,12},{12,8},{16,20},{20,16},{24,28},{28,24},{32,36},... | collective-permute-start | bytes 122888 | tf_op jit(solution)/shard_map/ppermute | solution.py:27
  409.1 1.0 copy-start.8
  411.6 0.7 copy-start.9
  414.1 1.0 copy-start.8
  416.6 0.7 copy-start.9
  419.1 1.0 copy-start.8
  421.5 0.7 copy-start.9
  424.1 1.0 copy-start.8
  429.1 1.0 copy-start.8
  434.0 1.0 copy-start.8
  439.0 1.0 copy-start.8
  444.0 1.0 copy-start.8
  447.2 5.5 %collective-permute-start.7 = (bf16[256,160]{0,1:T(8,128)(2,1)S(1)}, bf16[256,160]{0,1:T(8,128)(2,1)S(1)}, u32[]{:S(2)}, u32[]{:S(2)}) collective-permute-start(bf16[256,160]{0,1:T(8,128)(2,1)S(1)} %pad_maximum_fusion.8), channel_id=1, source_target_pairs={{0,8},{8,0},{4,12},{12,4},{16,24},{24,16},{20,28},{28,20},{32,40},... | collective-permute-start | bytes 245768 | tf_op jit(solution)/shard_map/ppermute | solution.py:27
  449.2 5.2 %collective-permute-start.5 = (bf16[256,160]{0,1:T(8,128)(2,1)S(1)}, bf16[256,160]{0,1:T(8,128)(2,1)S(1)}, u32[]{:S(2)}, u32[]{:S(2)}) collective-permute-start(bf16[256,160]{0,1:T(8,128)(2,1)S(1)} %pad_maximum_fusion.7), channel_id=1, source_target_pairs={{0,8},{8,0},{4,12},{12,4},{16,24},{24,16},{20,28},{28,20},{32,40},... | collective-permute-start | bytes 245768 | tf_op jit(solution)/shard_map/ppermute | solution.py:27
  454.4 1.0 copy-start.10
  478.0 6.9 %copy-start = (bf16[2560,640]{1,0:T(8,128)(2,1)S(1)}, bf16[2560,640]{1,0:T(8,128)(2,1)}, u32[]{:S(2)}) copy-start(bf16[2560,640]{1,0:T(8,128)(2,1)} %reshape.253) | copy-start | bytes 9830404
  (5 other events, 3.6 us)
Sparse Core Ops, SparseCore 0:
  11.0 137.0 all-gather.16
  151.6 140.6 all-gather.14
  294.4 26.7 all-gather.12
  323.2 27.0 all-gather.10

commit v2 on v1

--- a/solution.py
+++ b/solution.py
@@ -1,10 +1,15 @@
+import functools
 import math
 
 import numpy as np
 import jax
 import jax.numpy as jnp
 from jax import lax
+from jax.experimental import pallas as pl
+from jax.experimental.pallas import tpu as pltpu
 from jax.sharding import Mesh, PartitionSpec as P
+
+MESH_ID = pl.DeviceIdType.MESH
 
 HEAD_DIM = 80
 WIN = 4096
@@ -28,6 +33,104 @@
 
 
 WIDE = ("z", "x", "c")
+
+
+def gather_kernel(nz, nx, nc, blk_ref, out_ref, plane_send, plane_recv, ring_send, ring_recv, die_send, die_recv, local_sem):
+    z = lax.axis_index("z")
+    x = lax.axis_index("x")
+    c = lax.axis_index("c")
+    n = lax.axis_index("narrow")
+    per_plane = nx * nc
+    me_xc = x * nc + c
+    me = z * per_plane + me_xc
+    half = nz // 2
+    step_dir = 1 - 2 * c
+    dst_z = lax.rem(z + step_dir + nz, nz)
+    src_z = lax.rem(z - step_dir + nz, nz)
+    partner = (z, x, 1 - c, n)
+
+    def plane_slot(pz):
+        return out_ref.at[pl.ds(pl.multiple_of(pz * per_plane, per_plane), per_plane)]
+
+    barrier = pltpu.get_barrier_semaphore()
+    for k in range(1, per_plane):
+        peer = lax.rem(me_xc + k, per_plane)
+        pl.semaphore_signal(barrier, inc=1, device_id=(z, peer // nc, lax.rem(peer, nc), n), device_id_type=MESH_ID)
+    for zz in (dst_z, src_z):
+        pl.semaphore_signal(barrier, inc=1, device_id=(zz, x, c, n), device_id_type=MESH_ID)
+    pl.semaphore_wait(barrier, per_plane + 1)
+
+    local = pltpu.make_async_copy(blk_ref, out_ref.at[me], local_sem)
+    local.start()
+    sends = []
+    for k in range(1, per_plane):
+        peer = lax.rem(me_xc + k, per_plane)
+        cp = pltpu.make_async_remote_copy(
+            src_ref=blk_ref, dst_ref=out_ref.at[me],
+            send_sem=plane_send.at[k], recv_sem=plane_recv.at[k],
+            device_id=(z, peer // nc, lax.rem(peer, nc), n), device_id_type=MESH_ID)
+        cp.start()
+        sends.append(cp)
+    for k in range(1, per_plane):
+        sender = lax.rem(me_xc - k + per_plane, per_plane)
+        pltpu.make_async_remote_copy(
+            src_ref=blk_ref, dst_ref=out_ref.at[z * per_plane + sender],
+            send_sem=plane_send.at[k], recv_sem=plane_recv.at[k],
+            device_id=(z, x, c, n), device_id_type=MESH_ID).wait_recv()
+    local.wait()
+
+    for s in range(1, half + 1):
+        send_z = lax.rem(z - step_dir * (s - 1) + 2 * nz, nz)
+        cp = pltpu.make_async_remote_copy(
+            src_ref=plane_slot(send_z), dst_ref=plane_slot(send_z),
+            send_sem=ring_send.at[s - 1], recv_sem=ring_recv.at[s - 1],
+            device_id=(dst_z, x, c, n), device_id_type=MESH_ID)
+        cp.start()
+        sends.append(cp)
+        recv_z = lax.rem(z - step_dir * s + 2 * nz, nz)
+        pltpu.make_async_remote_copy(
+            src_ref=plane_slot(recv_z), dst_ref=plane_slot(recv_z),
+            send_sem=ring_send.at[s - 1], recv_sem=ring_recv.at[s - 1],
+            device_id=(src_z, x, c, n), device_id_type=MESH_ID).wait_recv()
+        if s < half:
+            dp = pltpu.make_async_remote_copy(
+                src_ref=plane_slot(recv_z), dst_ref=plane_slot(recv_z),
+                send_sem=die_send.at[s - 1], recv_sem=die_recv.at[s - 1],
+                device_id=partner, device_id_type=MESH_ID)
+            dp.start()
+            sends.append(dp)
+    for s in range(1, half):
+        other_z = lax.rem(z + step_dir * s + 2 * nz, nz)
+        pltpu.make_async_remote_copy(
+            src_ref=plane_slot(other_z), dst_ref=plane_slot(other_z),
+            send_sem=die_send.at[s - 1], recv_sem=die_recv.at[s - 1],
+            device_id=partner, device_id_type=MESH_ID).wait_recv()
+    for cp in sends:
+        cp.wait_send()
+
+
+def gather_wide(block, nz, nx, nc):
+    count = nz * nx * nc
+    half = nz // 2
+    per_plane = nx * nc
+    nbytes = block.size * block.dtype.itemsize
+    return pl.pallas_call(
+        functools.partial(gather_kernel, nz, nx, nc),
+        out_shape=jax.ShapeDtypeStruct((count,) + block.shape, block.dtype),
+        in_specs=[pl.BlockSpec(memory_space=pl.ANY)],
+        out_specs=pl.BlockSpec(memory_space=pl.ANY),
+        scratch_shapes=[
+            pltpu.SemaphoreType.DMA((per_plane,)),
+            pltpu.SemaphoreType.DMA((per_plane,)),
+            pltpu.SemaphoreType.DMA((half,)),
+            pltpu.SemaphoreType.DMA((half,)),
+            pltpu.SemaphoreType.DMA((half,)),
+            pltpu.SemaphoreType.DMA((half,)),
+            pltpu.SemaphoreType.DMA(()),
+        ],
+        compiler_params=pltpu.CompilerParams(collective_id=0, has_side_effects=True),
+        cost_estimate=pl.CostEstimate(flops=0, transcendentals=0, bytes_accessed=2 * count * nbytes),
+    )(block)
 
 
 def gather_rows(block):
@@ -133,7 +236,14 @@
     local_groups = kv_width // HEAD_DIM
     repeats = local_heads // local_groups
     columns = normed
-    qkv = gather_rows(jnp.concatenate([query_weight, key_weight, value_weight], axis=1))
+    sizes = (query_weight.shape[1], key_weight.shape[1], value_weight.shape[1], out_weight.shape[1])
+    joined = jnp.concatenate([query_weight, key_weight, value_weight, out_weight], axis=1)
+    block_rows, joined_width = joined.shape
+    dims = (lax.psum(1, "z"), lax.psum(1, "x"), lax.psum(1, "c"))
+    gathered = gather_wide(joined.reshape(-1, 128), *dims)
+    all_weights = gathered.reshape(-1, joined_width)
+    qkv = all_weights[:, : sum(sizes[:3])]
+    out_rows = all_weights[:, sum(sizes[:3]) :]
     qkv_sum = jnp.dot(columns, qkv, preferred_element_type=jnp.float32)
     query_sum = qkv_sum[:, :query_width]
     key_sum = qkv_sum[:, query_width : query_width + kv_width]
@@ -201,7 +311,7 @@
     columns = all_heads
     update = jnp.dot(
         columns,
-        gather_rows(out_weight),
+        out_rows,
         preferred_element_type=jnp.float32,
     ).astype(jnp.bfloat16)
     new_index = (cycle_mine - offset) % WIN

time: 499 us -> 252 us (0.51)
  the two profiles are of different devices: /device:TPU:1 before, /device:TPU:2 now
where the time goes in v2:
time: 252 us; the launch traced here: 251 us
  Pallas kernels  87.6 us (35%)
  matrix products  34.5 us (14%)
  local copies, waits for them, and re-layouts  34.2 us (14%)
  blocking collectives  27.9 us (11%)
  other arithmetic  23.3 us (9%)
  starting transfers between devices  20.3 us (8%)
  waiting for transfers between devices  20.1 us (8%)
  between operations  2.56 us (1%)
    pallas_call x1, Pallas kernels, gather_wide(): pl.pallas_call(functools.partial(gather_kernel, nz, nx, nc), out_shape=ja...  87.6 us
    ppermute x8, starting transfers between devices, from_partner(): return lax.ppermute(block, axis, route)  20.3 us
    ppermute x8, waiting for transfers between devices, from_partner(): return lax.ppermute(block, axis, route)  20.1 us
    reshape x1, local copies, waits for them, and re-layouts, shards(): all_weights = gathered.reshape(-1, joined_width)  15.3 us
    all_gather x1, blocking collectives, shards(): whole = lax.all_gather(tokens_in, 'narrow', axis=1, tiled=True)  14.4 us
    all_gather x1, blocking collectives, shards(): all_heads = lax.all_gather(attended, 'narrow', axis=1, tiled=True)  13.5 us
    dot_general x9, matrix products, step(): jnp.einsum('tgrd,gdk->tgrk', queries, block_keys, preferred_element_type=...  13.4 us
    dot_general x9, matrix products, step(): jnp.einsum('tgrk,gdk->tgrd', weights.astype(jnp.bfloat16), block_values,...  12.2 us
  transfers between devices with their start and end apart: 8, of which 4 were waited for; matrix products, arithmetic and copies ran while one was open for 12% of the time, Pallas kernels for 0%

profile of v2, /device:TPU:2, one launch (start us, length us, event | category | flops | bytes accessed | tf_op | source)
XLA Modules:
  0.0 251.1 jit_solution(7924319593308186156)
XLA Ops:
  2.3 87.6 %shard_map.130 = bf16[128,250,128]{2,1,0:T(8,128)(2,1)} custom-call(bf16[250,128]{1,0:T(8,128)(2,1)} %reshape.246.blk_ref), custom_call_target="tpu_custom_call" | custom-call | bytes 16384000 | tf_op jit(solution)/shard_map/pallas_call | solution.py:117
  90.0 15.3 %reshape.247 = bf16[2560,1600]{1,0:T(8,128)(2,1)} reshape(bf16[128,250,128]{2,1,0:T(8,128)(2,1)} %shard_map.130) | data formatting | bytes 16384000 | tf_op jit(solution)/shard_map/reshape | solution.py:244
  105.3 14.4 %all_gather.6 = bf16[128,2560]{1,0:T(8,128)(2,1)S(1)} all-gather(bf16[128,640]{1,0:T(8,128)(2,1)S(1)} %copy-done.7), channel_id=1, replica_groups=mesh['z'=16,'x'=4,'c'=2,'narrow'=4] {'narrow'}, dimensions={1}, use_global_device_ids=true | all-gather | bytes 819200 | tf_op jit(solution)/shard_map/all_gather | solution.py:230
  119.9 4.7 %fusion.23 = f32[128,960]{0,1:T(8,128)S(1)} fusion(bf16[2560,1600]{1,0:T(8,128)(2,1)} %reshape.247, bf16[128,2560]{1,0:T(8,128)(2,1)S(1)} %all_gather.6, f32[2560]{0:T(1024)S(1)} %convert_element_type.43, f32[128]{0:T(128)S(1)} %add_rsqrt_fusion), kind=kOutput, calls=%fused_computation.32 | convolution fusion | flops 630456320 | bytes 6400512 | tf_op jit(solution)/shard_map/dot_general | solution.py:247
  124.7 1.9 collective-permute-start.6
  128.1 2.4 collective-permute-start.4
  130.5 1.9 collective-permute-start.2
  132.5 2.4 collective-permute-start
  136.8 2.0 broadcast_compare_fusion
  138.8 2.0 add_select_fusion
  144.1 3.8 %collective-permute-start.7 = (bf16[256,160]{0,1:T(8,128)(2,1)S(1)}, bf16[256,160]{0,1:T(8,128)(2,1)S(1)}, u32[]{:S(2)}, u32[]{:S(2)}) collective-permute-start(bf16[256,160]{0,1:T(8,128)(2,1)S(1)} %pad_maximum_fusion.8), channel_id=1, source_target_pairs={{0,8},{8,0},{4,12},{12,4},{16,24},{24,16},{20,28},{28,20},{32,40},... | collective-permute-start | bytes 245768 | tf_op jit(solution)/shard_map/ppermute | solution.py:32
  148.0 2.0 collective-permute-start.5
  151.5 2.9 %collective-permute-done.5 = bf16[256,160]{0,1:T(8,128)(2,1)S(1)} collective-permute-done((bf16[256,160]{0,1:T(8,128)(2,1)S(1)}, bf16[256,160]{0,1:T(8,128)(2,1)S(1)}, u32[]{:S(2)}, u32[]{:S(2)}) %collective-permute-start.5) | collective-permute-done | bytes 81952 | tf_op jit(solution)/shard_map/ppermute | solution.py:32
  154.6 4.9 %gather_fusion.1 = bf16[1024,160]{1,0:T(8,128)(2,1)} fusion(bf16[160,512]{0,1:T(8,128)(2,1)S(1)} %copy.26, s32[1024]{0:T(1024)S(1)} %fusion.64), kind=kCustom, calls=%fused_computation.1.clone | custom fusion | bytes 659456 | tf_op jit(solution)/shard_map/jit(_take)/gather | solution.py:321
  159.5 4.9 %gather_fusion = bf16[1024,160]{1,0:T(8,128)(2,1)} fusion(bf16[160,512]{0,1:T(8,128)(2,1)S(1)} %copy.24, s32[1024]{0:T(1024)S(1)} %fusion.64), kind=kCustom, calls=%fused_computation.clone | custom fusion | bytes 659456 | tf_op jit(solution)/shard_map/jit(_take)/gather | solution.py:320
  167.2 2.0 collective-permute-start.1
  169.3 1.5 bitcast_select_fusion.2
  170.8 1.9 copy.28
  173.7 1.9 fusion.27
  175.6 3.8 %collective-permute-start.3 = (bf16[160,2048]{1,0:T(8,128)(2,1)S(1)}, bf16[160,2048]{1,0:T(8,128)(2,1)S(1)}, u32[]{:S(2)}, u32[]{:S(2)}) collective-permute-start(bf16[160,2048]{1,0:T(8,128)(2,1)S(1)} %pad_maximum_fusion.3), channel_id=1, source_target_pairs={{0,8},{8,0},{4,12},{12,4},{16,24},{24,16},{20,28},{28,20},{32,40},... | collective-permute-start | bytes 1966088 | tf_op jit(solution)/shard_map/ppermute | solution.py:32
  179.4 7.7 %collective-permute-done.1 = bf16[160,2048]{1,0:T(8,128)(2,1)} collective-permute-done((bf16[160,2048]{1,0:T(8,128)(2,1)}, bf16[160,2048]{1,0:T(8,128)(2,1)}, u32[]{:S(2)}, u32[]{:S(2)}) %collective-permute-start.1) | collective-permute-done | bytes 655392 | tf_op jit(solution)/shard_map/ppermute | solution.py:32
  189.7 8.9 %collective-permute-done.3 = bf16[160,2048]{1,0:T(8,128)(2,1)S(1)} collective-permute-done((bf16[160,2048]{1,0:T(8,128)(2,1)S(1)}, bf16[160,2048]{1,0:T(8,128)(2,1)S(1)}, u32[]{:S(2)}, u32[]{:S(2)}) %collective-permute-start.3) | collective-permute-done | bytes 655392 | tf_op jit(solution)/shard_map/ppermute | solution.py:32
  200.1 30.5 %while.5 = (s32[]{:T(128)}, f32[128,2,4,80]{0,3,2,1:T(8,128)S(1)}, f32[128,2,4]{0,2,1:T(4,128)S(1)}, f32[128,2,4]{0,2,1:T(4,128)S(1)}, pred[4096]{0:T(1024)(128)...) while((s32[]{:T(128)}, f32[128,2,4,80]{0,3,2,1:T(8,128)S(1)}, ...), condition=%wide.region_4.5_spmd.clone, body=%wide.region_1.4_spmd.clone.sunk | while | flops 174118016 | bytes 7774939 | solution.py:214
  202.5 1.5 fusion.90
  206.3 1.5 fusion.90
  210.1 1.5 fusion.90
  213.9 1.5 fusion.90
  217.7 1.5 fusion.90
  221.5 1.5 fusion.90
  230.7 2.2 fusion.30
  233.4 13.5 %all_gather.7 = bf16[128,2560]{0,1:T(8,128)(2,1)S(1)} all-gather(bf16[128,640]{0,1:T(8,128)(2,1)S(1)} %bitcast.121), channel_id=1, replica_groups=mesh['z'=16,'x'=4,'c'=2,'narrow'=4] {'narrow'}, dimensions={1}, use_global_device_ids=true | all-gather | bytes 819200 | tf_op jit(solution)/shard_map/all_gather | solution.py:310
  246.9 4.2 %fusion.38 = bf16[128,640]{1,0:T(8,128)(2,1)} fusion(bf16[128,2560]{0,1:T(8,128)(2,1)S(1)} %all_gather.7, bf16[2560,1600]{1,0:T(8,128)(2,1)} %reshape.247), kind=kOutput, calls=%fused_computation.54 | convolution fusion | flops 419512320 | bytes 4096000 | tf_op jit(solution)/shard_map/dot_general | solution.py:312
  (155 shorter events, 38.3 us)
Async XLA Ops:
  90.0 15.3 %copy-start.7 = (bf16[128,640]{1,0:T(8,128)(2,1)S(1)}, bf16[128,640]{1,0:T(8,128)(2,1)}, u32[]{:S(2)}) copy-start(bf16[128,640]{1,0:T(8,128)(2,1)} %param.15) | copy-start | bytes 491524
  90.0 29.7 %copy-start.9 = (bf16[2560]{0:T(1024)(128)(2,1)S(1)}, bf16[2560]{0:T(1024)(128)(2,1)}, u32[]{:S(2)}) copy-start(bf16[2560]{0:T(1024)(128)(2,1)} %param.16) | copy-start | bytes 15364
  119.9 6.8 %copy-start.10 = (s32[32]{0:T(128)S(1)}, s32[32]{0:T(128)}, u32[]{:S(2)}) copy-start(s32[32]{0:T(128)} %param.23) | copy-start | bytes 388
  119.9 10.6 %copy-start.3 = (bf16[160,1024]{1,0:T(8,128)(2,1)S(1)}, bf16[160,1024]{1,0:T(8,128)(2,1)}, u32[]{:S(2)}) copy-start(bf16[160,1024]{1,0:T(8,128)(2,1)} %param.22) | copy-start | bytes 983044
  119.9 12.6 %copy-start.4 = (bf16[160,1024]{1,0:T(8,128)(2,1)S(1)}, bf16[160,1024]{1,0:T(8,128)(2,1)}, u32[]{:S(2)}) copy-start(bf16[160,1024]{1,0:T(8,128)(2,1)} %param.21) | copy-start | bytes 983044
  119.9 15.7 %copy-start.11 = (s32[32]{0:T(128)S(1)}, s32[32]{0:T(128)}, u32[]{:S(2)}) copy-start(s32[32]{0:T(128)} %param.24) | copy-start | bytes 388
  119.9 16.3 %copy-start.12 = (s32[32]{0:T(128)S(1)}, s32[32]{0:T(128)}, u32[]{:S(2)}) copy-start(s32[32]{0:T(128)} %param.25) | copy-start | bytes 388
  124.7 19.4 %collective-permute-start.6 = (bf16[128,160]{0,1:T(8,128)(2,1)S(1)}, bf16[128,160]{0,1:T(8,128)(2,1)S(1)}, u32[]{:S(2)}, u32[]{:S(2)}) collective-permute-start(bf16[128,160]{0,1:T(8,128)(2,1)S(1)} %slice.65), channel_id=1, source_target_pairs={{0,4},{4,0},{8,12},{12,8},{16,20},{20,16},{24,28},{28,24},{32,36},... | collective-permute-start | bytes 122888 | tf_op jit(solution)/shard_map/ppermute | solution.py:32
  128.1 16.0 %collective-permute-start.4 = (bf16[128,160]{0,1:T(8,128)(2,1)S(1)}, bf16[128,160]{0,1:T(8,128)(2,1)S(1)}, u32[]{:S(2)}, u32[]{:S(2)}) collective-permute-start(bf16[128,160]{0,1:T(8,128)(2,1)S(1)} %bitcast.119), channel_id=1, source_target_pairs={{0,4},{4,0},{8,12},{12,8},{16,20},{20,16},{24,28},{28,24},{32,36},... | collective-permute-start | bytes 122888 | tf_op jit(solution)/shard_map/ppermute | solution.py:32
  130.5 33.9 %collective-permute-start.2 = (bf16[160,1024]{1,0:T(8,128)(2,1)S(1)}, bf16[160,1024]{1,0:T(8,128)(2,1)S(1)}, u32[]{:S(2)}, u32[]{:S(2)}) collective-permute-start(bf16[160,1024]{1,0:T(8,128)(2,1)S(1)} %copy-done.3), channel_id=1, source_target_pairs={{0,4},{4,0},{8,12},{12,8},{16,20},{20,16},{24,28},{28,24},{32,36},... | collective-permute-start | bytes 983048 | tf_op jit(solution)/shard_map/ppermute | solution.py:32
  132.5 32.7 %collective-permute-start = (bf16[160,1024]{1,0:T(8,128)(2,1)S(1)}, bf16[160,1024]{1,0:T(8,128)(2,1)}, u32[]{:S(2)}, u32[]{:S(2)}) collective-permute-start(bf16[160,1024]{1,0:T(8,128)(2,1)S(1)} %copy-done.4), channel_id=1, source_target_pairs={{0,4},{4,0},{8,12},{12,8},{16,20},{20,16},{24,28},{28,24},{32,36},... | collective-permute-start | bytes 983048 | tf_op jit(solution)/shard_map/ppermute | solution.py:32
  144.1 6.4 %collective-permute-start.7 = (bf16[256,160]{0,1:T(8,128)(2,1)S(1)}, bf16[256,160]{0,1:T(8,128)(2,1)S(1)}, u32[]{:S(2)}, u32[]{:S(2)}) collective-permute-start(bf16[256,160]{0,1:T(8,128)(2,1)S(1)} %pad_maximum_fusion.8), channel_id=1, source_target_pairs={{0,8},{8,0},{4,12},{12,4},{16,24},{24,16},{20,28},{28,20},{32,40},... | collective-permute-start | bytes 245768 | tf_op jit(solution)/shard_map/ppermute | solution.py:32
  148.0 6.3 %collective-permute-start.5 = (bf16[256,160]{0,1:T(8,128)(2,1)S(1)}, bf16[256,160]{0,1:T(8,128)(2,1)S(1)}, u32[]{:S(2)}, u32[]{:S(2)}) collective-permute-start(bf16[256,160]{0,1:T(8,128)(2,1)S(1)} %pad_maximum_fusion.7), channel_id=1, source_target_pairs={{0,8},{8,0},{4,12},{12,4},{16,24},{24,16},{20,28},{28,20},{32,40},... | collective-permute-start | bytes 245768 | tf_op jit(solution)/shard_map/ppermute | solution.py:32
  164.4 4.8 %copy-start.1 = (bf16[1024,160]{1,0:T(8,128)(2,1)S(1)}, bf16[1024,160]{1,0:T(8,128)(2,1)}, u32[]{:S(2)}) copy-start(bf16[1024,160]{1,0:T(8,128)(2,1)} %gather_fusion.1) | copy-start | bytes 983044
  164.4 4.8 %copy-start.2 = (bf16[1024,160]{1,0:T(8,128)(2,1)S(1)}, bf16[1024,160]{1,0:T(8,128)(2,1)}, u32[]{:S(2)}) copy-start(bf16[1024,160]{1,0:T(8,128)(2,1)} %gather_fusion) | copy-start | bytes 983044
  164.4 0.7 copy-start.6
  167.2 19.9 %collective-permute-start.1 = (bf16[160,2048]{1,0:T(8,128)(2,1)}, bf16[160,2048]{1,0:T(8,128)(2,1)}, u32[]{:S(2)}, u32[]{:S(2)}) collective-permute-start(bf16[160,2048]{1,0:T(8,128)(2,1)} %pad_maximum_fusion.2), channel_id=1, source_target_pairs={{0,8},{8,0},{4,12},{12,4},{16,24},{24,16},{20,28},{28,20},{32,40},... | collective-permute-start | bytes 1966088 | tf_op jit(solution)/shard_map/ppermute | solution.py:32
  169.3 4.4 %copy-start.5 = (pred[128,512]{0,1:T(8,128)(4,1)S(1)}, pred[128,512]{0,1:T(8,128)(4,1)}, u32[]{:S(2)}) copy-start(pred[128,512]{0,1:T(8,128)(4,1)} %fusion.48) | copy-start | bytes 196612
  175.6 23.0 %collective-permute-start.3 = (bf16[160,2048]{1,0:T(8,128)(2,1)S(1)}, bf16[160,2048]{1,0:T(8,128)(2,1)S(1)}, u32[]{:S(2)}, u32[]{:S(2)}) collective-permute-start(bf16[160,2048]{1,0:T(8,128)(2,1)S(1)} %pad_maximum_fusion.3), channel_id=1, source_target_pairs={{0,8},{8,0},{4,12},{12,4},{16,24},{24,16},{20,28},{28,20},{32,40},... | collective-permute-start | bytes 1966088 | tf_op jit(solution)/shard_map/ppermute | solution.py:32
  189.7 10.5 %copy-start.13 = (f32[128,2,4,80]{0,3,2,1:T(8,128)S(1)}, f32[128,2,4,80]{0,3,2,1:T(8,128)}, u32[]{:S(2)}) copy-start(f32[128,2,4,80]{0,3,2,1:T(8,128)} %custom-call) | copy-start | bytes 983044
  200.1 32.7 %copy-start.8 = (bf16[512,160]{0,1:T(8,128)(2,1)S(1)}, bf16[512,160]{0,1:T(8,128)(2,1)}, u32[]{:S(2)}) copy-start(bf16[512,160]{0,1:T(8,128)(2,1)} %get-tuple-element.287) | copy-start | bytes 491524
  230.6 2.2 copy-start

commit v3 on v2

--- a/solution.py
+++ b/solution.py
@@ -35,7 +35,9 @@
 WIDE = ("z", "x", "c")
 
 
-def gather_kernel(nz, nx, nc, blk_ref, out_ref, plane_send, plane_recv, ring_send, ring_recv, die_send, die_recv, local_sem):
+def gather_kernel(nz, nx, nc, nn, blk_ref, cache_ref, tok_ref, out_ref, cache_out, tok_out,
+                  plane_send, plane_recv, ring_send, ring_recv, die_send, die_recv, local_sem,
+                  cache_send, cache_recv, tok_send, tok_recv):
     z = lax.axis_index("z")
     x = lax.axis_index("x")
     c = lax.axis_index("c")
@@ -43,6 +45,8 @@
     per_plane = nx * nc
     me_xc = x * nc + c
     me = z * per_plane + me_xc
+    place = lax.rem(x, 2) * nc + c
+    x_base = x - lax.rem(x, 2)
     half = nz // 2
     step_dir = 1 - 2 * c
     dst_z = lax.rem(z + step_dir + nz, nz)
@@ -51,6 +55,9 @@
 
     def plane_slot(pz):
         return out_ref.at[pl.ds(pl.multiple_of(pz * per_plane, per_plane), per_plane)]
+
+    def group_dev(p):
+        return (z, x_base + p // nc, lax.rem(p, nc), n)
 
     barrier = pltpu.get_barrier_semaphore()
     for k in range(1, per_plane):
@@ -58,11 +65,16 @@
         pl.semaphore_signal(barrier, inc=1, device_id=(z, peer // nc, lax.rem(peer, nc), n), device_id_type=MESH_ID)
     for zz in (dst_z, src_z):
         pl.semaphore_signal(barrier, inc=1, device_id=(zz, x, c, n), device_id_type=MESH_ID)
-    pl.semaphore_wait(barrier, per_plane + 1)
-
-    local = pltpu.make_async_copy(blk_ref, out_ref.at[me], local_sem)
-    local.start()
+    for k in range(1, nn):
+        pl.semaphore_signal(barrier, inc=1, device_id=(z, x, c, lax.rem(n + k, nn)), device_id_type=MESH_ID)
+    pl.semaphore_wait(barrier, per_plane + 1 + nn - 1)
+
     sends = []
+    locals_ = []
+    for src, dst in ((blk_ref, out_ref.at[me]), (cache_ref, cache_out.at[place]), (tok_ref, tok_out.at[n])):
+        cp = pltpu.make_async_copy(src, dst, local_sem.at[len(locals_)])
+        cp.start()
+        locals_.append(cp)
     for k in range(1, per_plane):
         peer = lax.rem(me_xc + k, per_plane)
         cp = pltpu.make_async_remote_copy(
@@ -71,13 +83,27 @@
             device_id=(z, peer // nc, lax.rem(peer, nc), n), device_id_type=MESH_ID)
         cp.start()
         sends.append(cp)
+    for k in range(1, 2 * nc):
+        cp = pltpu.make_async_remote_copy(
+            src_ref=cache_ref, dst_ref=cache_out.at[place],
+            send_sem=cache_send.at[k], recv_sem=cache_recv.at[k],
+            device_id=group_dev(place ^ k), device_id_type=MESH_ID)
+        cp.start()
+        sends.append(cp)
+    for k in range(1, nn):
+        cp = pltpu.make_async_remote_copy(
+            src_ref=tok_ref, dst_ref=tok_out.at[n],
+            send_sem=tok_send.at[k], recv_sem=tok_recv.at[k],
+            device_id=(z, x, c, lax.rem(n + k, nn)), device_id_type=MESH_ID)
+        cp.start()
+        sends.append(cp)
     for k in range(1, per_plane):
         sender = lax.rem(me_xc - k + per_plane, per_plane)
         pltpu.make_async_remote_copy(
             src_ref=blk_ref, dst_ref=out_ref.at[z * per_plane + sender],
             send_sem=plane_send.at[k], recv_sem=plane_recv.at[k],
             device_id=(z, x, c, n), device_id_type=MESH_ID).wait_recv()
-    local.wait()
+    locals_[0].wait()
 
     for s in range(1, half + 1):
         send_z = lax.rem(z - step_dir * (s - 1) + 2 * nz, nz)
@@ -105,20 +131,37 @@
             src_ref=plane_slot(other_z), dst_ref=plane_slot(other_z),
             send_sem=die_send.at[s - 1], recv_sem=die_recv.at[s - 1],
             device_id=partner, device_id_type=MESH_ID).wait_recv()
+    for k in range(1, 2 * nc):
+        pltpu.make_async_remote_copy(
+            src_ref=cache_ref, dst_ref=cache_out.at[place ^ k],
+            send_sem=cache_send.at[k], recv_sem=cache_recv.at[k],
+            device_id=(z, x, c, n), device_id_type=MESH_ID).wait_recv()
+    for k in range(1, nn):
+        pltpu.make_async_remote_copy(
+            src_ref=tok_ref, dst_ref=tok_out.at[lax.rem(n - k + nn, nn)],
+            send_sem=tok_send.at[k], recv_sem=tok_recv.at[k],
+            device_id=(z, x, c, n), device_id_type=MESH_ID).wait_recv()
+    for cp in locals_[1:]:
+        cp.wait()
     for cp in sends:
         cp.wait_send()
 
 
-def gather_wide(block, nz, nx, nc):
+def gather_wide(block, cache, tokens, nz, nx, nc, nn):
     count = nz * nx * nc
     half = nz // 2
     per_plane = nx * nc
+    group = 2 * nc
     nbytes = block.size * block.dtype.itemsize
     return pl.pallas_call(
-        functools.partial(gather_kernel, nz, nx, nc),
-        out_shape=jax.ShapeDtypeStruct((count,) + block.shape, block.dtype),
-        in_specs=[pl.BlockSpec(memory_space=pl.ANY)],
-        out_specs=pl.BlockSpec(memory_space=pl.ANY),
+        functools.partial(gather_kernel, nz, nx, nc, nn),
+        out_shape=(
+            jax.ShapeDtypeStruct((count,) + block.shape, block.dtype),
+            jax.ShapeDtypeStruct((group,) + cache.shape, cache.dtype),
+            jax.ShapeDtypeStruct((nn,) + tokens.shape, tokens.dtype),
+        ),
+        in_specs=[pl.BlockSpec(memory_space=pl.ANY)] * 3,
+        out_specs=[pl.BlockSpec(memory_space=pl.ANY)] * 3,
         scratch_shapes=[
             pltpu.SemaphoreType.DMA((per_plane,)),
             pltpu.SemaphoreType.DMA((per_plane,)),
@@ -126,11 +169,15 @@
             pltpu.SemaphoreType.DMA((half,)),
             pltpu.SemaphoreType.DMA((half,)),
             pltpu.SemaphoreType.DMA((half,)),
-            pltpu.SemaphoreType.DMA(()),
+            pltpu.SemaphoreType.DMA((3,)),
+            pltpu.SemaphoreType.DMA((group,)),
+            pltpu.SemaphoreType.DMA((group,)),
+            pltpu.SemaphoreType.DMA((nn,)),
+            pltpu.SemaphoreType.DMA((nn,)),
         ],
         compiler_params=pltpu.CompilerParams(collective_id=0, has_side_effects=True),
         cost_estimate=pl.CostEstimate(flops=0, transcendentals=0, bytes_accessed=2 * count * nbytes),
-    )(block)
+    )(block, cache, tokens)
 
 
 def gather_rows(block):
@@ -214,6 +261,29 @@
     return lax.fori_loop(0, key_count // block, step, state)
 
 
+def exchange(block, axis, count, pairing):
+    pieces = [block]
+    for k in range(1, count):
+        route = [(src, pairing(src, k)) for src in range(count)]
+        route = [(dst, src) for src, dst in route]
+        pieces.append(lax.ppermute(block, axis, [(pairing(d, k), d) for d in range(count)]))
+    return jnp.stack(pieces)
+
+
+def in_member_order(stacked, me, pairing, along):
+    count = stacked.shape[0]
+    parts = [stacked[pairing(me, q)] for q in range(count)]
+    return jnp.concatenate(parts, axis=along)
+
+
+def shift_pair(me, k):
+    return (me - k) % 4
+
+
+def xor_pair(me, k):
+    return me ^ k
+
+
 def shards(
     tokens_in,
     norm_gain,
@@ -227,7 +297,42 @@
     append_slot,
     shard_owner,
 ):
-    whole = lax.all_gather(tokens_in, "narrow", axis=1, tiled=True)
+    n_narrow = lax.psum(1, "narrow")
+    me_narrow = lax.axis_index("narrow")
+    position = lax.axis_index(WIDE)
+    request = position // GROUP
+    place = position % GROUP
+
+    def narrow_pair(me, k):
+        return (me - k) % n_narrow
+
+    def narrow_src(me, q):
+        return (me - q) % n_narrow
+
+
+    def group_pair(d, k):
+        return d ^ k
+
+    def group_route_pieces(block):
+        pieces = [block]
+        for k in range(1, GROUP):
+            route = [(src, src ^ k) for src in range(lax.psum(1, WIDE))]
+            pieces.append(lax.ppermute(block, WIDE, route))
+        return jnp.stack(pieces)
+
+
+    sizes = (query_weight.shape[1], key_weight.shape[1], value_weight.shape[1], out_weight.shape[1])
+    joined = jnp.concatenate([query_weight, key_weight, value_weight, out_weight], axis=1)
+    block_rows, joined_width = joined.shape
+    dims = (lax.psum(1, "z"), lax.psum(1, "x"), lax.psum(1, "c"))
+    gathered, cache_blocks, tok_pieces = gather_wide(
+        joined.reshape(-1, 128), jnp.concatenate([cache_keys, cache_values], axis=0), tokens_in,
+        *dims, n_narrow)
+    whole = jnp.concatenate([tok_pieces[q] for q in range(n_narrow)], axis=1)
+    all_weights = gathered.reshape(-1, joined_width)
+    qkv = all_weights[:, : sum(sizes[:3])]
+    out_rows = all_weights[:, sum(sizes[:3]) :]
+
     normed = rms_normed(whole, norm_gain)
     tok_rows = whole.shape[0]
     query_width = query_weight.shape[1]
@@ -235,22 +340,10 @@
     local_heads = query_width // HEAD_DIM
     local_groups = kv_width // HEAD_DIM
     repeats = local_heads // local_groups
-    columns = normed
-    sizes = (query_weight.shape[1], key_weight.shape[1], value_weight.shape[1], out_weight.shape[1])
-    joined = jnp.concatenate([query_weight, key_weight, value_weight, out_weight], axis=1)
-    block_rows, joined_width = joined.shape
-    dims = (lax.psum(1, "z"), lax.psum(1, "x"), lax.psum(1, "c"))
-    gathered = gather_wide(joined.reshape(-1, 128), *dims)
-    all_weights = gathered.reshape(-1, joined_width)
-    qkv = all_weights[:, : sum(sizes[:3])]
-    out_rows = all_weights[:, sum(sizes[:3]) :]
-    qkv_sum = jnp.dot(columns, qkv, preferred_element_type=jnp.float32)
+    qkv_sum = jnp.dot(normed, qkv, preferred_element_type=jnp.float32)
     query_sum = qkv_sum[:, :query_width]
     key_sum = qkv_sum[:, query_width : query_width + kv_width]
     value_sum = qkv_sum[:, query_width + kv_width :]
-    position = lax.axis_index(WIDE)
-    request = position // GROUP
-    place = position % GROUP
     length = cached_len[request]
     offset = append_slot[request]
     owner = shard_owner[request]
@@ -266,18 +359,15 @@
     )
     new_values = value_sum.astype(jnp.bfloat16)
     shard_rows = cache_keys.shape[1]
-    within = jnp.arange(shard_rows, dtype=jnp.int32)
-    cycle_mine = (place - owner) % GROUP * shard_rows + within
-    old_keys, old_values = (cache_keys, cache_values)
-    for bit in range(GROUP_BITS):
-        upper = place // 2**bit % 2 == 1
-        other_keys, other_values, other_old_keys, other_old_values = from_partner(
-            (new_keys, new_values, old_keys, old_values), WIDE, bit
-        )
-        new_keys = ordered(new_keys, other_keys, upper, 0)
-        new_values = ordered(new_values, other_values, upper, 0)
-        old_keys = ordered(old_keys, other_old_keys, upper, 1)
-        old_values = ordered(old_values, other_old_values, upper, 1)
+
+    old_both = jnp.concatenate([cache_blocks[q] for q in range(GROUP)], axis=1)
+    old_keys = old_both[:kv_width]
+    old_values = old_both[kv_width:]
+    new_both = jnp.concatenate([new_keys, new_values], axis=1)
+    new_both = in_member_order(group_route_pieces(new_both), place, lambda me, q: me ^ q, 0)
+    new_keys = new_both[:, :kv_width]
+    new_values = new_both[:, kv_width:]
+
     slot_index = jnp.arange(old_keys.shape[1], dtype=jnp.int32)
     cycle = (slot_index // shard_rows - owner) % GROUP * shard_rows + slot_index % shard_rows
     cached_pos = (cycle - offset + length) % WIN
@@ -307,18 +397,21 @@
     )
     accum, top_score, total = state
     attended = (accum / total[..., None]).astype(jnp.bfloat16).reshape(tok_rows, query_width)
-    all_heads = lax.all_gather(attended, "narrow", axis=1, tiled=True)
-    columns = all_heads
-    update = jnp.dot(
-        columns,
-        out_rows,
-        preferred_element_type=jnp.float32,
-    ).astype(jnp.bfloat16)
-    new_index = (cycle_mine - offset) % WIN
-    written = new_index < new_count
-    take_rows = jnp.minimum(new_index, new_count - 1)
-    put_keys = jnp.where(written[None, :], jnp.take(key_cols, take_rows, axis=1), cache_keys)
-    put_values = jnp.where(written[None, :], jnp.take(value_cols, take_rows, axis=1), cache_values)
+    head_pieces = exchange(attended, "narrow", n_narrow, lambda d, k: (d - k) % n_narrow)
+    all_heads = in_member_order(head_pieces, me_narrow, lambda me, q: (me - q) % n_narrow, 1)
+    update = jnp.dot(all_heads, out_rows, preferred_element_type=jnp.float32).astype(jnp.bfloat16)
+
+    first = ((place - owner) % GROUP * shard_rows - offset) % WIN
+    keys_ext = jnp.concatenate(
+        [key_cols, jnp.zeros((kv_width, WIN - new_count), key_cols.dtype), key_cols,
+         jnp.zeros((kv_width, shard_rows - new_count), key_cols.dtype)], axis=1)
+    values_ext = jnp.concatenate(
+        [value_cols, jnp.zeros((kv_width, WIN - new_count), value_cols.dtype), value_cols,
+         jnp.zeros((kv_width, shard_rows - new_count), value_cols.dtype)], axis=1)
+    spot = (first + jnp.arange(shard_rows, dtype=jnp.int32)) % WIN
+    written = spot < new_count
+    put_keys = jnp.where(written[None, :], lax.dynamic_slice_in_dim(keys_ext, first, shard_rows, 1), cache_keys)
+    put_values = jnp.where(written[None, :], lax.dynamic_slice_in_dim(values_ext, first, shard_rows, 1), cache_values)
     return (update, put_keys, put_values)
 
 

time: 252 us -> 193 us (0.77)
  the two profiles are of different devices: /device:TPU:2 before, /device:TPU:1 now
where the time goes in v3:
time: 193 us; the launch traced here: 191 us
  Pallas kernels  88.4 us (46%)
  matrix products  33.3 us (17%)
  local copies, waits for them, and re-layouts  23.7 us (12%)
  starting transfers between devices  19.5 us (10%)
  other arithmetic  17.3 us (9%)
  waiting for transfers between devices  5.2 us (3%)
  between operations  3.25 us (2%)
    pallas_call x1, Pallas kernels, gather_wide(): pl.pallas_call(functools.partial(gather_kernel, nz, nx, nc, nn), out_shap...  88.4 us
    reshape x1, local copies, waits for them, and re-layouts, shards(): all_weights = gathered.reshape(-1, joined_width)  15.3 us
    dot_general x9, matrix products, step(): jnp.einsum('tgrk,gdk->tgrd', weights.astype(jnp.bfloat16), block_values,...  12.2 us
    dot_general x9, matrix products, step(): jnp.einsum('tgrd,gdk->tgrk', queries, block_keys, preferred_element_type=...  12 us
    ppermute x3, starting transfers between devices, group_route_pieces(): pieces.append(lax.ppermute(block, WIDE, route))  11.6 us
    ppermute x3, starting transfers between devices, exchange(): lax.ppermute(block, axis, [(pairing(d, k), d) for d in range(count)])  7.92 us
    ppermute x3, waiting for transfers between devices, exchange(): lax.ppermute(block, axis, [(pairing(d, k), d) for d in range(count)])  5.19 us
    dot_general x1, matrix products, shards(): qkv_sum = jnp.dot(normed, qkv, preferred_element_type=jnp.float32)  4.81 us
  transfers between devices with their start and end apart: 6, of which 2 were waited for; matrix products, arithmetic and copies ran while one was open for 22% of the time, Pallas kernels for 0%

profile of v3, /device:TPU:1, one launch (start us, length us, event | category | flops | bytes accessed | tf_op | source)
XLA Modules:
  0.0 191.2 jit_solution(10903562049325282689)
XLA Ops:
  2.3 2.0 %pad_maximum_fusion.1.cache_ref = bf16[320,1024]{1,0:T(8,128)(2,1)} fusion(bf16[160,1024]{1,0:T(8,128)(2,1)} %param.20, bf16[160,1024]{1,0:T(8,128)(2,1)} %param.19), kind=kLoop, calls=%fused_computation.59 | loop fusion | flops 1310720 | bytes 1310720 | tf_op jit(solution)/shard_map/concatenate | solution.py:329
  4.3 88.4 %shard_map.130 = (bf16[128,250,128]{2,1,0:T(8,128)(2,1)}, bf16[4,320,1024]{2,1,0:T(8,128)(2,1)}, bf16[4,128,640]{2,1,0:T(8,128)(2,1)}) custom-call(bf16[250,128]{1,0:T(8,128)(2,1)} %reshape.239.blk_ref, bf16[320,1024]{1,0:T(8,128)(2,1)} %pad_maximum_fusion.1.cache_ref, bf16[128,640]{1,0:T(8,128)(2,1)} %tok_ref.1), custom_call_target="tpu_custom_call" | custom-call | bytes 16384000 | tf_op jit(solution)/shard_map/pallas_call | solution.py:156
  92.7 15.3 %reshape.241 = bf16[2560,1600]{1,0:T(8,128)(2,1)} reshape(bf16[128,250,128]{2,1,0:T(8,128)(2,1)} %get-tuple-element.209) | data formatting | bytes 16384000 | tf_op jit(solution)/shard_map/reshape | solution.py:332
  108.3 4.8 %fusion.23 = f32[128,960]{0,1:T(8,128)S(1)} fusion(bf16[2560,1600]{1,0:T(8,128)(2,1)} %reshape.241, f32[2560]{0:T(1024)S(1)} %convert_element_type.43, f32[128]{0:T(128)S(1)} %add_rsqrt_fusion, bf16[128,640]{1,0:T(8,128)(2,1)S(1)} %get-tuple-element.286, bf16[128,640]{1,0:T(8,128)(2,1)S(1)} %get-tuple-element.287, ...), kind=kOutput, calls=%fused_computation.30 | convolution fusion | flops 632750080 | bytes 6400512 | tf_op jit(solution)/shard_map/dot_general | solution.py:343
  116.0 5.6 %collective-permute-start.2 = (bf16[128,320]{0,1:T(8,128)(2,1)}, bf16[128,320]{0,1:T(8,128)(2,1)}, u32[]{:S(2)}, u32[]{:S(2)}) collective-permute-start(bf16[128,320]{0,1:T(8,128)(2,1)} %get-tuple-element.302), channel_id=1, source_target_pairs={{0,12},{4,8},{8,4},{12,0},{16,28},{20,24},{24,20},{28,16},{32,44},... | collective-permute-start | bytes 245768 | tf_op jit(solution)/shard_map/ppermute | solution.py:320
  121.6 4.0 %collective-permute-start.1 = (bf16[128,320]{0,1:T(8,128)(2,1)}, bf16[128,320]{0,1:T(8,128)(2,1)}, u32[]{:S(2)}, u32[]{:S(2)}) collective-permute-start(bf16[128,320]{0,1:T(8,128)(2,1)} %get-tuple-element.302), channel_id=1, source_target_pairs={{0,8},{4,12},{8,0},{12,4},{16,24},{20,28},{24,16},{28,20},{32,40},... | collective-permute-start | bytes 245768 | tf_op jit(solution)/shard_map/ppermute | solution.py:320
  125.6 1.9 %collective-permute-start = (bf16[128,320]{0,1:T(8,128)(2,1)}, bf16[128,320]{0,1:T(8,128)(2,1)}, u32[]{:S(2)}, u32[]{:S(2)}) collective-permute-start(bf16[128,320]{0,1:T(8,128)(2,1)} %get-tuple-element.302), channel_id=1, source_target_pairs={{0,4},{4,0},{8,12},{12,8},{16,20},{20,16},{24,28},{28,24},{32,36},... | collective-permute-start | bytes 245768 | tf_op jit(solution)/shard_map/ppermute | solution.py:320
  130.2 2.0 %broadcast_compare_fusion = pred[4096]{0:T(1024)(128)(4,1)S(1)} fusion(s32[]{:T(128)} %bitcast.2, s32[]{:T(128)} %bitcast.1, s32[]{:T(128)} %bitcast), kind=kLoop, calls=%fused_computation.135 | loop fusion | flops 163840 | bytes 4108 | tf_op jit(solution)/shard_map/lt | solution.py:381
  132.2 2.0 %add_select_fusion = s32[4096]{0:T(1024)S(1)} fusion(s32[]{:T(128)} %bitcast.2, s32[]{:T(128)} %bitcast.1, s32[]{:T(128)} %bitcast), kind=kLoop, calls=%fused_computation.116 | loop fusion | flops 159744 | bytes 16396 | tf_op jit(solution)/shard_map/jit(remainder)/select_n | solution.py:373
  136.9 1.7 fusion.90
  138.7 30.5 %while.5 = (s32[]{:T(128)}, f32[128,2,4,80]{0,3,2,1:T(8,128)S(1)}, f32[128,2,4]{0,2,1:T(4,128)S(1)}, f32[128,2,4]{0,2,1:T(4,128)S(1)}, pred[4096]{0:T(1024)(128)...) while((s32[]{:T(128)}, f32[128,2,4,80]{0,3,2,1:T(8,128)S(1)}, ...), condition=%wide.region_4.5_spmd.clone, body=%wide.region_1.4_spmd.clone.sunk | while | flops 174118016 | bytes 7774939 | solution.py:261
  139.1 1.4 fusion.106
  141.0 1.5 fusion.109
  142.9 1.4 fusion.106
  144.8 1.5 fusion.109
  146.7 1.4 fusion.106
  148.6 1.5 fusion.109
  150.5 1.4 fusion.106
  152.5 1.5 fusion.109
  154.3 1.4 fusion.106
  156.3 1.5 fusion.109
  158.2 1.4 fusion.106
  160.1 1.5 fusion.109
  163.9 1.5 fusion.109
  165.8 1.4 fusion.106
  167.7 1.5 fusion.109
  172.3 2.6 %collective-permute-start.5 = (bf16[128,640]{0,1:T(8,128)(2,1)S(1)}, bf16[128,640]{0,1:T(8,128)(2,1)S(1)}, u32[]{:S(2)}, u32[]{:S(2)}) collective-permute-start(bf16[128,640]{0,1:T(8,128)(2,1)S(1)} %bitcast.153), channel_id=1, source_target_pairs={{1,0},{2,1},{3,2},{0,3},{5,4},{6,5},{7,6},{4,7},{9,8},{10,9},{11,1... | collective-permute-start | bytes 491528 | tf_op jit(solution)/shard_map/ppermute | solution.py:269
  174.9 3.4 %collective-permute-start.4 = (bf16[128,640]{0,1:T(8,128)(2,1)S(1)}, bf16[128,640]{0,1:T(8,128)(2,1)S(1)}, u32[]{:S(2)}, u32[]{:S(2)}) collective-permute-start(bf16[128,640]{0,1:T(8,128)(2,1)S(1)} %bitcast.154), channel_id=1, source_target_pairs={{2,0},{3,1},{0,2},{1,3},{6,4},{7,5},{4,6},{5,7},{10,8},{11,9},{8,1... | collective-permute-start | bytes 491528 | tf_op jit(solution)/shard_map/ppermute | solution.py:269
  178.3 1.9 %collective-permute-start.3 = (bf16[128,640]{0,1:T(8,128)(2,1)S(1)}, bf16[128,640]{0,1:T(8,128)(2,1)S(1)}, u32[]{:S(2)}, u32[]{:S(2)}) collective-permute-start(bf16[128,640]{0,1:T(8,128)(2,1)S(1)} %bitcast.155), channel_id=1, source_target_pairs={{3,0},{0,1},{1,2},{2,3},{7,4},{4,5},{5,6},{6,7},{11,8},{8,9},{9,10... | collective-permute-start | bytes 491528 | tf_op jit(solution)/shard_map/ppermute | solution.py:269
  181.7 1.6 collective-permute-done.4
  183.3 3.6 %collective-permute-done.3 = bf16[128,640]{0,1:T(8,128)(2,1)S(1)} collective-permute-done((bf16[128,640]{0,1:T(8,128)(2,1)S(1)}, bf16[128,640]{0,1:T(8,128)(2,1)S(1)}, u32[]{:S(2)}, u32[]{:S(2)}) %collective-permute-start.3) | collective-permute-done | bytes 163872 | tf_op jit(solution)/shard_map/ppermute | solution.py:269
  187.0 4.2 %fusion.38 = bf16[128,640]{1,0:T(8,128)(2,1)} fusion(bf16[2560,1600]{1,0:T(8,128)(2,1)} %reshape.241, bf16[128,640]{0,1:T(8,128)(2,1)S(1)} %get-tuple-element.282, bf16[128,640]{0,1:T(8,128)(2,1)S(1)} %get-tuple-element.283, bf16[128,640]{0,1:T(8,128)(2,1)S(1)} %get-tuple-element.284, bf16[128,640]{0,1:T(8,128)(2,1)S(1)} %get-tuple-element.281), kind=kOutput, calls=%fused_computation.55 | convolution fusion | flops 422133760 | bytes 4096000 | tf_op jit(solution)/shard_map/dot_general | solution.py:402
  (130 shorter events, 20.5 us)
Async XLA Ops:
  92.7 15.3 %copy-start.5 = (bf16[2560]{0:T(1024)(128)(2,1)S(1)}, bf16[2560]{0:T(1024)(128)(2,1)}, u32[]{:S(2)}) copy-start(bf16[2560]{0:T(1024)(128)(2,1)} %param.14) | copy-start | bytes 15364
  92.7 15.3 %copy-start.3 = (bf16[4,128,640]{2,1,0:T(8,128)(2,1)S(1)}, bf16[4,128,640]{2,1,0:T(8,128)(2,1)}, u32[]{:S(2)}) copy-start(bf16[4,128,640]{2,1,0:T(8,128)(2,1)} %get-tuple-element.208) | copy-start | bytes 1966084
  108.3 4.9 %copy-start.6 = (s32[32]{0:T(128)S(1)}, s32[32]{0:T(128)}, u32[]{:S(2)}) copy-start(s32[32]{0:T(128)} %param.21) | copy-start | bytes 388
  108.3 19.9 %copy-start.7 = (s32[32]{0:T(128)S(1)}, s32[32]{0:T(128)}, u32[]{:S(2)}) copy-start(s32[32]{0:T(128)} %param.22) | copy-start | bytes 388
  108.3 28.1 %copy-start = (bf16[4,320,1024]{2,1,0:T(8,128)(2,1)S(1)}, bf16[4,320,1024]{2,1,0:T(8,128)(2,1)}, u32[]{:S(2)}) copy-start(bf16[4,320,1024]{2,1,0:T(8,128)(2,1)} %get-tuple-element.207) | copy-start | bytes 7864324
  114.7 0.6 copy-start.4
  116.0 53.6 %collective-permute-start.2 = (bf16[128,320]{0,1:T(8,128)(2,1)}, bf16[128,320]{0,1:T(8,128)(2,1)}, u32[]{:S(2)}, u32[]{:S(2)}) collective-permute-start(bf16[128,320]{0,1:T(8,128)(2,1)} %get-tuple-element.302), channel_id=1, source_target_pairs={{0,12},{4,8},{8,4},{12,0},{16,28},{20,24},{24,20},{28,16},{32,44},... | collective-permute-start | bytes 245768 | tf_op jit(solution)/shard_map/ppermute | solution.py:320
  121.6 48.0 %collective-permute-start.1 = (bf16[128,320]{0,1:T(8,128)(2,1)}, bf16[128,320]{0,1:T(8,128)(2,1)}, u32[]{:S(2)}, u32[]{:S(2)}) collective-permute-start(bf16[128,320]{0,1:T(8,128)(2,1)} %get-tuple-element.302), channel_id=1, source_target_pairs={{0,8},{4,12},{8,0},{12,4},{16,24},{20,28},{24,16},{28,20},{32,40},... | collective-permute-start | bytes 245768 | tf_op jit(solution)/shard_map/ppermute | solution.py:320
  125.6 44.0 %collective-permute-start = (bf16[128,320]{0,1:T(8,128)(2,1)}, bf16[128,320]{0,1:T(8,128)(2,1)}, u32[]{:S(2)}, u32[]{:S(2)}) collective-permute-start(bf16[128,320]{0,1:T(8,128)(2,1)} %get-tuple-element.302), channel_id=1, source_target_pairs={{0,4},{4,0},{8,12},{12,8},{16,20},{20,16},{24,28},{28,24},{32,36},... | collective-permute-start | bytes 245768 | tf_op jit(solution)/shard_map/ppermute | solution.py:320
  136.9 1.8 copy-start.8
  171.7 8.5 %copy-start.1 = (bf16[160,1024]{1,0:T(8,128)(2,1)S(1)}, bf16[160,1024]{1,0:T(8,128)(2,1)}, u32[]{:S(2)}) copy-start(bf16[160,1024]{1,0:T(8,128)(2,1)} %param.20) | copy-start | bytes 983044
  171.8 8.5 %copy-start.2 = (bf16[160,1024]{1,0:T(8,128)(2,1)S(1)}, bf16[160,1024]{1,0:T(8,128)(2,1)}, u32[]{:S(2)}) copy-start(bf16[160,1024]{1,0:T(8,128)(2,1)} %param.19) | copy-start | bytes 983044
  172.3 9.4 %collective-permute-start.5 = (bf16[128,640]{0,1:T(8,128)(2,1)S(1)}, bf16[128,640]{0,1:T(8,128)(2,1)S(1)}, u32[]{:S(2)}, u32[]{:S(2)}) collective-permute-start(bf16[128,640]{0,1:T(8,128)(2,1)S(1)} %bitcast.153), channel_id=1, source_target_pairs={{1,0},{2,1},{3,2},{0,3},{5,4},{6,5},{7,6},{4,7},{9,8},{10,9},{11,1... | collective-permute-start | bytes 491528 | tf_op jit(solution)/shard_map/ppermute | solution.py:269
  174.9 8.3 %collective-permute-start.4 = (bf16[128,640]{0,1:T(8,128)(2,1)S(1)}, bf16[128,640]{0,1:T(8,128)(2,1)S(1)}, u32[]{:S(2)}, u32[]{:S(2)}) collective-permute-start(bf16[128,640]{0,1:T(8,128)(2,1)S(1)} %bitcast.154), channel_id=1, source_target_pairs={{2,0},{3,1},{0,2},{1,3},{6,4},{7,5},{4,6},{5,7},{10,8},{11,9},{8,1... | collective-permute-start | bytes 491528 | tf_op jit(solution)/shard_map/ppermute | solution.py:269
  178.3 8.5 %collective-permute-start.3 = (bf16[128,640]{0,1:T(8,128)(2,1)S(1)}, bf16[128,640]{0,1:T(8,128)(2,1)S(1)}, u32[]{:S(2)}, u32[]{:S(2)}) collective-permute-start(bf16[128,640]{0,1:T(8,128)(2,1)S(1)} %bitcast.155), channel_id=1, source_target_pairs={{3,0},{0,1},{1,2},{2,3},{7,4},{4,5},{5,6},{6,7},{11,8},{8,9},{9,10... | collective-permute-start | bytes 491528 | tf_op jit(solution)/shard_map/ppermute | solution.py:269

commit v4 on v3

--- a/solution.py
+++ b/solution.py
@@ -83,6 +83,13 @@
             device_id=(z, peer // nc, lax.rem(peer, nc), n), device_id_type=MESH_ID)
         cp.start()
         sends.append(cp)
+    for k in range(1, per_plane):
+        sender = lax.rem(me_xc - k + per_plane, per_plane)
+        pltpu.make_async_remote_copy(
+            src_ref=blk_ref, dst_ref=out_ref.at[z * per_plane + sender],
+            send_sem=plane_send.at[k], recv_sem=plane_recv.at[k],
+            device_id=(z, x, c, n), device_id_type=MESH_ID).wait_recv()
+    locals_[0].wait()
     for k in range(1, 2 * nc):
         cp = pltpu.make_async_remote_copy(
             src_ref=cache_ref, dst_ref=cache_out.at[place],
@@ -97,13 +104,6 @@
             device_id=(z, x, c, lax.rem(n + k, nn)), device_id_type=MESH_ID)
         cp.start()
         sends.append(cp)
-    for k in range(1, per_plane):
-        sender = lax.rem(me_xc - k + per_plane, per_plane)
-        pltpu.make_async_remote_copy(
-            src_ref=blk_ref, dst_ref=out_ref.at[z * per_plane + sender],
-            send_sem=plane_send.at[k], recv_sem=plane_recv.at[k],
-            device_id=(z, x, c, n), device_id_type=MESH_ID).wait_recv()
-    locals_[0].wait()
 
     for s in range(1, half + 1):
         send_z = lax.rem(z - step_dir * (s - 1) + 2 * nz, nz)
@@ -145,6 +145,69 @@
         cp.wait()
     for cp in sends:
         cp.wait_send()
+
+
+def swap_kernel(kind, count, src_ref, out_ref, send_sem, recv_sem, local_sem):
+    z = lax.axis_index("z")
+    x = lax.axis_index("x")
+    c = lax.axis_index("c")
+    n = lax.axis_index("narrow")
+    if kind == "narrow":
+        me = n
+
+        def device(k):
+            return (z, x, c, lax.rem(n + k, count))
+
+        def sender(k):
+            return lax.rem(n - k + count, count)
+    else:
+        me = lax.rem(x, 2) * 2 + c
+        x_base = x - lax.rem(x, 2)
+
+        def device(k):
+            p = me ^ k
+            return (z, x_base + p // 2, lax.rem(p, 2), n)
+
+        def sender(k):
+            return me ^ k
+
+    barrier = pltpu.get_barrier_semaphore()
+    for k in range(1, count):
+        pl.semaphore_signal(barrier, inc=1, device_id=device(k), device_id_type=MESH_ID)
+    pl.semaphore_wait(barrier, count - 1)
+    local = pltpu.make_async_copy(src_ref, out_ref.at[me], local_sem)
+    local.start()
+    sends = []
+    for k in range(1, count):
+        cp = pltpu.make_async_remote_copy(
+            src_ref=src_ref, dst_ref=out_ref.at[me],
+            send_sem=send_sem.at[k], recv_sem=recv_sem.at[k],
+            device_id=device(k), device_id_type=MESH_ID)
+        cp.start()
+        sends.append(cp)
+    for k in range(1, count):
+        pltpu.make_async_remote_copy(
+            src_ref=src_ref, dst_ref=out_ref.at[sender(k)],
+            send_sem=send_sem.at[k], recv_sem=recv_sem.at[k],
+            device_id=(z, x, c, n), device_id_type=MESH_ID).wait_recv()
+    local.wait()
+    for cp in sends:
+        cp.wait_send()
+
+
+def swap(block, kind, count, ident):
+    return pl.pallas_call(
+        functools.partial(swap_kernel, kind, count),
+        out_shape=jax.ShapeDtypeStruct((count,) + block.shape, block.dtype),
+        in_specs=[pl.BlockSpec(memory_space=pltpu.VMEM)],
+        out_specs=pl.BlockSpec(memory_space=pltpu.VMEM),
+        scratch_shapes=[
+            pltpu.SemaphoreType.DMA((count,)),
+            pltpu.SemaphoreType.DMA((count,)),
+            pltpu.SemaphoreType.DMA(()),
+        ],
+        compiler_params=pltpu.CompilerParams(collective_id=ident, has_side_effects=True),
+    )(block)
 
 
 def gather_wide(block, cache, tokens, nz, nx, nc, nn):
@@ -364,7 +427,8 @@
     old_keys = old_both[:kv_width]
     old_values = old_both[kv_width:]
     new_both = jnp.concatenate([new_keys, new_values], axis=1)
-    new_both = in_member_order(group_route_pieces(new_both), place, lambda me, q: me ^ q, 0)
+    new_pieces = swap(new_both, "group", GROUP, 2)
+    new_both = jnp.concatenate([new_pieces[q] for q in range(GROUP)], axis=0)
     new_keys = new_both[:, :kv_width]
     new_values = new_both[:, kv_width:]
 
@@ -397,8 +461,8 @@
     )
     accum, top_score, total = state
     attended = (accum / total[..., None]).astype(jnp.bfloat16).reshape(tok_rows, query_width)
-    head_pieces = exchange(attended, "narrow", n_narrow, lambda d, k: (d - k) % n_narrow)
-    all_heads = in_member_order(head_pieces, me_narrow, lambda me, q: (me - q) % n_narrow, 1)
+    head_pieces = swap(attended, "narrow", n_narrow, 1)
+    all_heads = jnp.concatenate([head_pieces[q] for q in range(n_narrow)], axis=1)
     update = jnp.dot(all_heads, out_rows, preferred_element_type=jnp.float32).astype(jnp.bfloat16)
 
     first = ((place - owner) % GROUP * shard_rows - offset) % WIN

time: 193 us -> 205 us (1.062)
  Pallas kernels: 88.4 us -> 115 us
  starting transfers between devices: 19.5 us -> 0 us
  matrix products: 33.3 us -> 42 us
  waiting for transfers between devices: 5.2 us -> 0 us
  local copies, waits for them, and re-layouts: 23.7 us -> 27 us
    pallas_call x0 -> x2, Pallas kernels: none -> 27.6 us  [swap(): pl.pallas_call(functools.partial(swap_kernel, kind, count), out_shape=jax...]
    ppermute x6 -> x0, starting transfers between devices: 19.5 us -> none  [the longest x3 11.6 us: group_route_pieces(): pieces.append(lax.ppermute(block, WIDE, route))]
    dot_general x9, matrix products: 12.2 us -> 19.9 us  [step(): jnp.einsum('tgrk,gdk->tgrd', weights.astype(jnp.bfloat16), block_values,...]
    ppermute x6 -> x0, waiting for transfers between devices: 5.2 us -> none  [the longest x3 5.19 us: exchange(): lax.ppermute(block, axis, [(pairing(d, k), d) for d in range(count)])]
    another operation x5 -> x2, other arithmetic: 2.54 us -> 0.07 us  [the longest x2 1.66 us: group_route_pieces(): return jnp.stack(pieces)]
    squeeze x2, local copies, waits for them, and re-layouts: 0.09 us -> 2.29 us  [the longest x1 1.21 us: shards(): head_pieces[q]]
  transfers between devices with their start and end apart: 6 -> 0, of which waited for: 2 -> 0; matrix products, arithmetic and copies ran while one was open for 22% -> 0% of each run, Pallas kernels for 0% -> 0%
where the time goes in v4:
time: 205 us; the launch traced here: 204 us
  Pallas kernels  115 us (56%)
  matrix products  42 us (20%)
  local copies, waits for them, and re-layouts  27 us (13%)
  other arithmetic  17 us (8%)
  between operations  2.87 us (1%)
    pallas_call x1, Pallas kernels, gather_wide(): pl.pallas_call(functools.partial(gather_kernel, nz, nx, nc, nn), out_shap...  87.3 us
    pallas_call x2, Pallas kernels, swap(): pl.pallas_call(functools.partial(swap_kernel, kind, count), out_shape=jax...  27.6 us
    dot_general x9, matrix products, step(): jnp.einsum('tgrk,gdk->tgrd', weights.astype(jnp.bfloat16), block_values,...  19.9 us
    reshape x1, local copies, waits for them, and re-layouts, shards(): all_weights = gathered.reshape(-1, joined_width)  15.3 us
    dot_general x9, matrix products, step(): jnp.einsum('tgrd,gdk->tgrk', queries, block_keys, preferred_element_type=...  13.4 us
    reduce_sum x9, other arithmetic, step(): sum_new = sum_old * rescale + jnp.sum(weights, axis=-1)  5.74 us
    dot_general x1, matrix products, shards(): qkv_sum = jnp.dot(normed, qkv, preferred_element_type=jnp.float32)  4.67 us

profile of v4, /device:TPU:1, one launch (start us, length us, event | category | flops | bytes accessed | tf_op | source)
XLA Modules:
  0.0 204.1 jit_solution(8569340803408600366)
XLA Ops:
  2.3 2.0 pad_maximum_fusion.1.cache_ref
  4.3 87.3 %shard_map.130 = (bf16[128,250,128]{2,1,0:T(8,128)(2,1)}, bf16[4,320,1024]{2,1,0:T(8,128)(2,1)}, bf16[4,128,640]{2,1,0:T(8,128)(2,1)}) custom-call(bf16[250,128]{1,0:T(8,128)(2,1)} %reshape.239.blk_ref, bf16[320,1024]{1,0:T(8,128)(2,1)} %pad_maximum_fusion.1.cache_ref, bf16[128,640]{1,0:T(8,128)(2,1)} %tok_ref.1), custom_call_target="tpu_custom_call" | custom-call | bytes 16384000 | tf_op jit(solution)/shard_map/pallas_call | solution.py:219
  91.6 15.3 %reshape.241 = bf16[2560,1600]{1,0:T(8,128)(2,1)} reshape(bf16[128,250,128]{2,1,0:T(8,128)(2,1)} %get-tuple-element.209) | data formatting | bytes 16384000 | tf_op jit(solution)/shard_map/reshape | solution.py:395
  107.2 4.7 %fusion.23 = f32[128,960]{0,1:T(8,128)S(1)} fusion(bf16[2560,1600]{1,0:T(8,128)(2,1)} %reshape.241, f32[2560]{0:T(1024)S(1)} %convert_element_type.43, f32[128]{0:T(128)S(1)} %add_rsqrt_fusion, bf16[128,640]{1,0:T(8,128)(2,1)S(1)} %get-tuple-element.286, bf16[128,640]{1,0:T(8,128)(2,1)S(1)} %get-tuple-element.287, ...), kind=kOutput, calls=%fused_computation.30 | convolution fusion | flops 632750080 | bytes 6400512 | tf_op jit(solution)/shard_map/dot_general | solution.py:406
  114.3 14.2 %shard_map.131 = bf16[4,128,320]{2,1,0:T(8,128)(2,1)} custom-call(bf16[128,320]{1,0:T(8,128)(2,1)} %pad_maximum_fusion.6.src_ref), custom_call_target="tpu_custom_call" | custom-call | tf_op jit(solution)/shard_map/pallas_call | solution.py:199
  132.2 1.9 fusion.27
  135.2 1.8 broadcast_compare_fusion
  137.1 1.8 add_select_fusion
  139.5 1.8 fusion.89
  141.3 36.8 %while.5 = (s32[]{:T(128)}, f32[128,2,4,80]{0,3,2,1:T(8,128)}, f32[128,2,4]{0,2,1:T(4,128)S(1)}, f32[128,2,4]{0,2,1:T(4,128)S(1)}, pred[4096]{0:T(1024)(128)(4,1...) while((s32[]{:T(128)}, f32[128,2,4,80]{0,3,2,1:T(8,128)}, ...), condition=%wide.region_4.5_spmd.clone, body=%wide.region_1.4_spmd.clone.sunk | while | flops 174118016 | bytes 7774939 | solution.py:324
  141.7 1.4 fusion.105
  143.6 2.2 %fusion.108 = f32[128,2,4,80]{0,3,2,1:T(8,128)} fusion(f32[2,512,128,4]{2,1,3,0:T(8,128)S(1)} %get-tuple-element.376, f32[128,2,4]{0,2,1:T(4,128)S(1)} %select_maximum_fusion.2, pred[128,512]{0,1:T(8,128)(4,1)S(1)} %fusion.104, f32[128,2,4,80]{0,3,2,1:T(8,128)} %get-tuple-element.395, bf16[2,80,4096]{2,1,0:T(8,128)(2,1)} %get-tuple-element.416, ...), kind=kOutput, calls=%fused_computation.9.clone.1 | convolution fusion | flops 86228992 | bytes 2990085 | tf_op jit(solution)/shard_map/while/body/eval_jaxpr/tgrk,gdk->tgrd/dot_general | solution.py:316
  146.1 1.4 fusion.105
  148.1 2.3 %fusion.108 = f32[128,2,4,80]{0,3,2,1:T(8,128)} fusion(f32[2,512,128,4]{2,1,3,0:T(8,128)S(1)} %get-tuple-element.376, f32[128,2,4]{0,2,1:T(4,128)S(1)} %select_maximum_fusion.2, pred[128,512]{0,1:T(8,128)(4,1)S(1)} %fusion.104, f32[128,2,4,80]{0,3,2,1:T(8,128)} %get-tuple-element.395, bf16[2,80,4096]{2,1,0:T(8,128)(2,1)} %get-tuple-element.416, ...), kind=kOutput, calls=%fused_computation.9.clone.1 | convolution fusion | flops 86228992 | bytes 2990085 | tf_op jit(solution)/shard_map/while/body/eval_jaxpr/tgrk,gdk->tgrd/dot_general | solution.py:316
  150.8 1.4 fusion.105
  152.7 2.3 %fusion.108 = f32[128,2,4,80]{0,3,2,1:T(8,128)} fusion(f32[2,512,128,4]{2,1,3,0:T(8,128)S(1)} %get-tuple-element.376, f32[128,2,4]{0,2,1:T(4,128)S(1)} %select_maximum_fusion.2, pred[128,512]{0,1:T(8,128)(4,1)S(1)} %fusion.104, f32[128,2,4,80]{0,3,2,1:T(8,128)} %get-tuple-element.395, bf16[2,80,4096]{2,1,0:T(8,128)(2,1)} %get-tuple-element.416, ...), kind=kOutput, calls=%fused_computation.9.clone.1 | convolution fusion | flops 86228992 | bytes 2990085 | tf_op jit(solution)/shard_map/while/body/eval_jaxpr/tgrk,gdk->tgrd/dot_general | solution.py:316
  155.4 1.4 fusion.105
  157.3 2.3 %fusion.108 = f32[128,2,4,80]{0,3,2,1:T(8,128)} fusion(f32[2,512,128,4]{2,1,3,0:T(8,128)S(1)} %get-tuple-element.376, f32[128,2,4]{0,2,1:T(4,128)S(1)} %select_maximum_fusion.2, pred[128,512]{0,1:T(8,128)(4,1)S(1)} %fusion.104, f32[128,2,4,80]{0,3,2,1:T(8,128)} %get-tuple-element.395, bf16[2,80,4096]{2,1,0:T(8,128)(2,1)} %get-tuple-element.416, ...), kind=kOutput, calls=%fused_computation.9.clone.1 | convolution fusion | flops 86228992 | bytes 2990085 | tf_op jit(solution)/shard_map/while/body/eval_jaxpr/tgrk,gdk->tgrd/dot_general | solution.py:316
  160.0 1.4 fusion.105
  161.9 2.3 %fusion.108 = f32[128,2,4,80]{0,3,2,1:T(8,128)} fusion(f32[2,512,128,4]{2,1,3,0:T(8,128)S(1)} %get-tuple-element.376, f32[128,2,4]{0,2,1:T(4,128)S(1)} %select_maximum_fusion.2, pred[128,512]{0,1:T(8,128)(4,1)S(1)} %fusion.104, f32[128,2,4,80]{0,3,2,1:T(8,128)} %get-tuple-element.395, bf16[2,80,4096]{2,1,0:T(8,128)(2,1)} %get-tuple-element.416, ...), kind=kOutput, calls=%fused_computation.9.clone.1 | convolution fusion | flops 86228992 | bytes 2990085 | tf_op jit(solution)/shard_map/while/body/eval_jaxpr/tgrk,gdk->tgrd/dot_general | solution.py:316
  164.6 1.4 fusion.105
  166.5 2.3 %fusion.108 = f32[128,2,4,80]{0,3,2,1:T(8,128)} fusion(f32[2,512,128,4]{2,1,3,0:T(8,128)S(1)} %get-tuple-element.376, f32[128,2,4]{0,2,1:T(4,128)S(1)} %select_maximum_fusion.2, pred[128,512]{0,1:T(8,128)(4,1)S(1)} %fusion.104, f32[128,2,4,80]{0,3,2,1:T(8,128)} %get-tuple-element.395, bf16[2,80,4096]{2,1,0:T(8,128)(2,1)} %get-tuple-element.416, ...), kind=kOutput, calls=%fused_computation.9.clone.1 | convolution fusion | flops 86228992 | bytes 2990085 | tf_op jit(solution)/shard_map/while/body/eval_jaxpr/tgrk,gdk->tgrd/dot_general | solution.py:316
  169.2 1.4 fusion.105
  171.2 2.3 %fusion.108 = f32[128,2,4,80]{0,3,2,1:T(8,128)} fusion(f32[2,512,128,4]{2,1,3,0:T(8,128)S(1)} %get-tuple-element.376, f32[128,2,4]{0,2,1:T(4,128)S(1)} %select_maximum_fusion.2, pred[128,512]{0,1:T(8,128)(4,1)S(1)} %fusion.104, f32[128,2,4,80]{0,3,2,1:T(8,128)} %get-tuple-element.395, bf16[2,80,4096]{2,1,0:T(8,128)(2,1)} %get-tuple-element.416, ...), kind=kOutput, calls=%fused_computation.9.clone.1 | convolution fusion | flops 86228992 | bytes 2990085 | tf_op jit(solution)/shard_map/while/body/eval_jaxpr/tgrk,gdk->tgrd/dot_general | solution.py:316
  173.9 1.4 fusion.105
  175.8 2.3 %fusion.108 = f32[128,2,4,80]{0,3,2,1:T(8,128)} fusion(f32[2,512,128,4]{2,1,3,0:T(8,128)S(1)} %get-tuple-element.376, f32[128,2,4]{0,2,1:T(4,128)S(1)} %select_maximum_fusion.2, pred[128,512]{0,1:T(8,128)(4,1)S(1)} %fusion.104, f32[128,2,4,80]{0,3,2,1:T(8,128)} %get-tuple-element.395, bf16[2,80,4096]{2,1,0:T(8,128)(2,1)} %get-tuple-element.416, ...), kind=kOutput, calls=%fused_computation.9.clone.1 | convolution fusion | flops 86228992 | bytes 2990085 | tf_op jit(solution)/shard_map/while/body/eval_jaxpr/tgrk,gdk->tgrd/dot_general | solution.py:316
  178.1 2.2 %fusion.30 = f32[128,2,4]{0,2,1:T(4,128)S(1)} fusion(f32[2,512,128,4]{2,1,3,0:T(8,128)} %get-tuple-element.304, f32[128,2,4]{0,2,1:T(4,128)S(1)} %max.11, pred[128,512]{0,1:T(8,128)(4,1)S(1)} %fusion.63), kind=kLoop, calls=%fused_computation.46 | loop fusion | flops 2096128 | bytes 2170880 | tf_op jit(solution)/shard_map/while/body/eval_jaxpr/reduce_sum | solution.py:315
  180.3 1.5 fusion.37
  182.6 13.4 %shard_map.132 = bf16[4,128,640]{2,1,0:T(8,128)(2,1)} custom-call(bf16[128,640]{1,0:T(8,128)(2,1)} %copy.45.src_ref), custom_call_target="tpu_custom_call" | custom-call | tf_op jit(solution)/shard_map/pallas_call | solution.py:199
  196.0 1.2 slice_bitcast_fusion.9
  197.3 4.0 %fusion.38 = bf16[128,640]{1,0:T(8,128)(2,1)} fusion(bf16[2560,1600]{1,0:T(8,128)(2,1)} %reshape.241, bf16[128,640]{1,0:T(8,128)(2,1)S(1)} %get-tuple-element.282, bf16[128,640]{1,0:T(8,128)(2,1)S(1)} %get-tuple-element.283, bf16[128,640]{1,0:T(8,128)(2,1)S(1)} %get-tuple-element.284, bf16[128,640]{1,0:T(8,128)(2,1)S(1)} %get-tuple-element.281), kind=kOutput, calls=%fused_computation.55 | convolution fusion | flops 422133760 | bytes 4096000 | tf_op jit(solution)/shard_map/dot_general | solution.py:466
  202.7 1.4 fusion.58
  (125 shorter events, 16.5 us)
Async XLA Ops:
  91.6 15.3 %copy-start.6 = (bf16[2560]{0:T(1024)(128)(2,1)S(1)}, bf16[2560]{0:T(1024)(128)(2,1)}, u32[]{:S(2)}) copy-start(bf16[2560]{0:T(1024)(128)(2,1)} %param.14) | copy-start | bytes 15364
  91.6 15.3 %copy-start.4 = (bf16[4,128,640]{2,1,0:T(8,128)(2,1)S(1)}, bf16[4,128,640]{2,1,0:T(8,128)(2,1)}, u32[]{:S(2)}) copy-start(bf16[4,128,640]{2,1,0:T(8,128)(2,1)} %get-tuple-element.208) | copy-start | bytes 1966084
  107.1 4.9 %copy-start.7 = (s32[32]{0:T(128)S(1)}, s32[32]{0:T(128)}, u32[]{:S(2)}) copy-start(s32[32]{0:T(128)} %param.21) | copy-start | bytes 388
  111.8 17.8 %copy-start.5 = (f32[128,960]{0,1:T(8,128)}, f32[128,960]{0,1:T(8,128)S(1)}, u32[]{:S(2)}) copy-start(f32[128,960]{0,1:T(8,128)S(1)} %fusion.23) | copy-start | bytes 1474564
  130.6 3.4 %copy-start.8 = (s32[32]{0:T(128)S(1)}, s32[32]{0:T(128)}, u32[]{:S(2)}) copy-start(s32[32]{0:T(128)} %param.22) | copy-start | bytes 388
  130.7 4.0 %copy-start.9 = (s32[32]{0:T(128)S(1)}, s32[32]{0:T(128)}, u32[]{:S(2)}) copy-start(s32[32]{0:T(128)} %param.23) | copy-start | bytes 388
  130.8 8.1 %copy-start.1 = (bf16[4,320,1024]{2,1,0:T(8,128)(2,1)S(1)}, bf16[4,320,1024]{2,1,0:T(8,128)(2,1)}, u32[]{:S(2)}) copy-start(bf16[4,320,1024]{2,1,0:T(8,128)(2,1)} %get-tuple-element.207) | copy-start | bytes 7864324
  178.1 2.2 %copy-start = (f32[2,512,128,4]{2,1,3,0:T(8,128)S(1)}, f32[2,512,128,4]{2,1,3,0:T(8,128)}, u32[]{:S(2)}) copy-start(f32[2,512,128,4]{2,1,3,0:T(8,128)} %get-tuple-element.304) | copy-start | bytes 6291460
  197.3 5.4 %copy-start.2 = (bf16[160,1024]{1,0:T(8,128)(2,1)S(1)}, bf16[160,1024]{1,0:T(8,128)(2,1)}, u32[]{:S(2)}) copy-start(bf16[160,1024]{1,0:T(8,128)(2,1)} %param.20) | copy-start | bytes 983044
  197.3 5.4 %copy-start.3 = (bf16[160,1024]{1,0:T(8,128)(2,1)S(1)}, bf16[160,1024]{1,0:T(8,128)(2,1)}, u32[]{:S(2)}) copy-start(bf16[160,1024]{1,0:T(8,128)(2,1)} %param.19) | copy-start | bytes 983044

commit v5 on v3

--- a/solution.py
+++ b/solution.py
@@ -33,6 +33,7 @@
 
 
 WIDE = ("z", "x", "c")
+RING_SUBS = 4
 
 
 def gather_kernel(nz, nx, nc, nn, blk_ref, cache_ref, tok_ref, out_ref, cache_out, tok_out,
@@ -83,6 +84,13 @@
             device_id=(z, peer // nc, lax.rem(peer, nc), n), device_id_type=MESH_ID)
         cp.start()
         sends.append(cp)
+    for k in range(1, per_plane):
+        sender = lax.rem(me_xc - k + per_plane, per_plane)
+        pltpu.make_async_remote_copy(
+            src_ref=blk_ref, dst_ref=out_ref.at[z * per_plane + sender],
+            send_sem=plane_send.at[k], recv_sem=plane_recv.at[k],
+            device_id=(z, x, c, n), device_id_type=MESH_ID).wait_recv()
+    locals_[0].wait()
     for k in range(1, 2 * nc):
         cp = pltpu.make_async_remote_copy(
             src_ref=cache_ref, dst_ref=cache_out.at[place],
@@ -97,40 +105,44 @@
             device_id=(z, x, c, lax.rem(n + k, nn)), device_id_type=MESH_ID)
         cp.start()
         sends.append(cp)
-    for k in range(1, per_plane):
-        sender = lax.rem(me_xc - k + per_plane, per_plane)
-        pltpu.make_async_remote_copy(
-            src_ref=blk_ref, dst_ref=out_ref.at[z * per_plane + sender],
-            send_sem=plane_send.at[k], recv_sem=plane_recv.at[k],
-            device_id=(z, x, c, n), device_id_type=MESH_ID).wait_recv()
-    locals_[0].wait()
+
+    subs = RING_SUBS
+    sub_len = per_plane // subs
+
+    def sub_slot(pz, j):
+        return out_ref.at[pl.ds(pl.multiple_of(pz * per_plane + j * sub_len, sub_len), sub_len)]
+
+    def ring_copy(s, j, pz, device):
+        return pltpu.make_async_remote_copy(
+            src_ref=sub_slot(pz, j), dst_ref=sub_slot(pz, j),
+            send_sem=ring_send.at[s - 1, j], recv_sem=ring_recv.at[s - 1, j],
+            device_id=device, device_id_type=MESH_ID)
+
+    def die_copy(s, j, pz):
+        return pltpu.make_async_remote_copy(
+            src_ref=sub_slot(pz, j), dst_ref=sub_slot(pz, j),
+            send_sem=die_send.at[s - 1, j], recv_sem=die_recv.at[s - 1, j],
+            device_id=partner, device_id_type=MESH_ID)
 
     for s in range(1, half + 1):
         send_z = lax.rem(z - step_dir * (s - 1) + 2 * nz, nz)
-        cp = pltpu.make_async_remote_copy(
-            src_ref=plane_slot(send_z), dst_ref=plane_slot(send_z),
-            send_sem=ring_send.at[s - 1], recv_sem=ring_recv.at[s - 1],
-            device_id=(dst_z, x, c, n), device_id_type=MESH_ID)
-        cp.start()
-        sends.append(cp)
-        recv_z = lax.rem(z - step_dir * s + 2 * nz, nz)
-        pltpu.make_async_remote_copy(
-            src_ref=plane_slot(recv_z), dst_ref=plane_slot(recv_z),
-            send_sem=ring_send.at[s - 1], recv_sem=ring_recv.at[s - 1],
-            device_id=(src_z, x, c, n), device_id_type=MESH_ID).wait_recv()
-        if s < half:
-            dp = pltpu.make_async_remote_copy(
-                src_ref=plane_slot(recv_z), dst_ref=plane_slot(recv_z),
-                send_sem=die_send.at[s - 1], recv_sem=die_recv.at[s - 1],
-                device_id=partner, device_id_type=MESH_ID)
-            dp.start()
-            sends.append(dp)
+        for j in range(subs):
+            if s > 1:
+                ring_copy(s - 1, j, send_z, (src_z, x, c, n)).wait_recv()
+                if s - 1 < half:
+                    dp = die_copy(s - 1, j, send_z)
+                    dp.start()
+                    sends.append(dp)
+            cp = ring_copy(s, j, send_z, (dst_z, x, c, n))
+            cp.start()
+            sends.append(cp)
+    last_z = lax.rem(z - step_dir * half + 2 * nz, nz)
+    for j in range(subs):
+        ring_copy(half, j, last_z, (src_z, x, c, n)).wait_recv()
     for s in range(1, half):
         other_z = lax.rem(z + step_dir * s + 2 * nz, nz)
-        pltpu.make_async_remote_copy(
-            src_ref=plane_slot(other_z), dst_ref=plane_slot(other_z),
-            send_sem=die_send.at[s - 1], recv_sem=die_recv.at[s - 1],
-            device_id=partner, device_id_type=MESH_ID).wait_recv()
+        for j in range(subs):
+            die_copy(s, j, other_z).wait_recv()
     for k in range(1, 2 * nc):
         pltpu.make_async_remote_copy(
             src_ref=cache_ref, dst_ref=cache_out.at[place ^ k],
@@ -165,10 +177,10 @@
         scratch_shapes=[
             pltpu.SemaphoreType.DMA((per_plane,)),
             pltpu.SemaphoreType.DMA((per_plane,)),
-            pltpu.SemaphoreType.DMA((half,)),
-            pltpu.SemaphoreType.DMA((half,)),
-            pltpu.SemaphoreType.DMA((half,)),
-            pltpu.SemaphoreType.DMA((half,)),
+            pltpu.SemaphoreType.DMA((half, RING_SUBS)),
+            pltpu.SemaphoreType.DMA((half, RING_SUBS)),
+            pltpu.SemaphoreType.DMA((half, RING_SUBS)),
+            pltpu.SemaphoreType.DMA((half, RING_SUBS)),
             pltpu.SemaphoreType.DMA((3,)),
             pltpu.SemaphoreType.DMA((group,)),
             pltpu.SemaphoreType.DMA((group,)),

time: 193 us -> 173 us (0.90)
  Pallas kernels: 88.4 us -> 67.7 us
    pallas_call x1, Pallas kernels: 88.4 us -> 67.7 us  [gather_wide(): pl.pallas_call(functools.partial(gather_kernel, nz, nx, nc, nn), out_shap...]
  transfers between devices with their start and end apart: 6 -> 6, of which waited for: 2 -> 2; matrix products, arithmetic and copies ran while one was open for 22% -> 24% of each run, Pallas kernels for 0% -> 0%
where the time goes in v5:
time: 173 us; the launch traced here: 171 us
  Pallas kernels  67.7 us (39%)
  matrix products  33.3 us (19%)
  local copies, waits for them, and re-layouts  23.7 us (14%)
  starting transfers between devices  19.5 us (11%)
  other arithmetic  17.3 us (10%)
  waiting for transfers between devices  6.03 us (3%)
  between operations  3.25 us (2%)
    pallas_call x1, Pallas kernels, gather_wide(): pl.pallas_call(functools.partial(gather_kernel, nz, nx, nc, nn), out_shap...  67.7 us
    reshape x1, local copies, waits for them, and re-layouts, shards(): all_weights = gathered.reshape(-1, joined_width)  15.3 us
    dot_general x9, matrix products, step(): jnp.einsum('tgrk,gdk->tgrd', weights.astype(jnp.bfloat16), block_values,...  12.2 us
    dot_general x9, matrix products, step(): jnp.einsum('tgrd,gdk->tgrk', queries, block_keys, preferred_element_type=...  12 us
    ppermute x3, starting transfers between devices, group_route_pieces(): pieces.append(lax.ppermute(block, WIDE, route))  11.5 us
    ppermute x3, starting transfers between devices, exchange(): lax.ppermute(block, axis, [(pairing(d, k), d) for d in range(count)])  7.99 us
    ppermute x3, waiting for transfers between devices, exchange(): lax.ppermute(block, axis, [(pairing(d, k), d) for d in range(count)])  6.03 us
    dot_general x1, matrix products, shards(): qkv_sum = jnp.dot(normed, qkv, preferred_element_type=jnp.float32)  4.81 us
  transfers between devices with their start and end apart: 6, of which 2 were waited for; matrix products, arithmetic and copies ran while one was open for 24% of the time, Pallas kernels for 0%

profile of v5, /device:TPU:1, one launch (start us, length us, event | category | flops | bytes accessed | tf_op | source)
XLA Modules:
  0.0 171.4 jit_solution(1509533516473897868)
XLA Ops:
  2.3 2.0 %pad_maximum_fusion.1.cache_ref = bf16[320,1024]{1,0:T(8,128)(2,1)} fusion(bf16[160,1024]{1,0:T(8,128)(2,1)} %param.20, bf16[160,1024]{1,0:T(8,128)(2,1)} %param.19), kind=kLoop, calls=%fused_computation.59 | loop fusion | flops 1310720 | bytes 1310720 | tf_op jit(solution)/shard_map/concatenate | solution.py:341
  4.3 67.7 %shard_map.130 = (bf16[128,250,128]{2,1,0:T(8,128)(2,1)}, bf16[4,320,1024]{2,1,0:T(8,128)(2,1)}, bf16[4,128,640]{2,1,0:T(8,128)(2,1)}) custom-call(bf16[250,128]{1,0:T(8,128)(2,1)} %reshape.239.blk_ref, bf16[320,1024]{1,0:T(8,128)(2,1)} %pad_maximum_fusion.1.cache_ref, bf16[128,640]{1,0:T(8,128)(2,1)} %tok_ref.1), custom_call_target="tpu_custom_call" | custom-call | bytes 16384000 | tf_op jit(solution)/shard_map/pallas_call | solution.py:168
  72.0 15.3 %reshape.241 = bf16[2560,1600]{1,0:T(8,128)(2,1)} reshape(bf16[128,250,128]{2,1,0:T(8,128)(2,1)} %get-tuple-element.209) | data formatting | bytes 16384000 | tf_op jit(solution)/shard_map/reshape | solution.py:344
  87.7 4.8 %fusion.23 = f32[128,960]{0,1:T(8,128)S(1)} fusion(bf16[2560,1600]{1,0:T(8,128)(2,1)} %reshape.241, f32[2560]{0:T(1024)S(1)} %convert_element_type.43, f32[128]{0:T(128)S(1)} %add_rsqrt_fusion, bf16[128,640]{1,0:T(8,128)(2,1)S(1)} %get-tuple-element.286, bf16[128,640]{1,0:T(8,128)(2,1)S(1)} %get-tuple-element.287, ...), kind=kOutput, calls=%fused_computation.30 | convolution fusion | flops 632750080 | bytes 6400512 | tf_op jit(solution)/shard_map/dot_general | solution.py:355
  95.3 6.0 %collective-permute-start.2 = (bf16[128,320]{0,1:T(8,128)(2,1)}, bf16[128,320]{0,1:T(8,128)(2,1)}, u32[]{:S(2)}, u32[]{:S(2)}) collective-permute-start(bf16[128,320]{0,1:T(8,128)(2,1)} %get-tuple-element.302), channel_id=1, source_target_pairs={{0,12},{4,8},{8,4},{12,0},{16,28},{20,24},{24,20},{28,16},{32,44},... | collective-permute-start | bytes 245768 | tf_op jit(solution)/shard_map/ppermute | solution.py:332
  101.3 3.6 %collective-permute-start.1 = (bf16[128,320]{0,1:T(8,128)(2,1)}, bf16[128,320]{0,1:T(8,128)(2,1)}, u32[]{:S(2)}, u32[]{:S(2)}) collective-permute-start(bf16[128,320]{0,1:T(8,128)(2,1)} %get-tuple-element.302), channel_id=1, source_target_pairs={{0,8},{4,12},{8,0},{12,4},{16,24},{20,28},{24,16},{28,20},{32,40},... | collective-permute-start | bytes 245768 | tf_op jit(solution)/shard_map/ppermute | solution.py:332
  104.9 1.9 %collective-permute-start = (bf16[128,320]{0,1:T(8,128)(2,1)}, bf16[128,320]{0,1:T(8,128)(2,1)}, u32[]{:S(2)}, u32[]{:S(2)}) collective-permute-start(bf16[128,320]{0,1:T(8,128)(2,1)} %get-tuple-element.302), channel_id=1, source_target_pairs={{0,4},{4,0},{8,12},{12,8},{16,20},{20,16},{24,28},{28,24},{32,36},... | collective-permute-start | bytes 245768 | tf_op jit(solution)/shard_map/ppermute | solution.py:332
  109.5 2.0 %broadcast_compare_fusion = pred[4096]{0:T(1024)(128)(4,1)S(1)} fusion(s32[]{:T(128)} %bitcast.2, s32[]{:T(128)} %bitcast.1, s32[]{:T(128)} %bitcast), kind=kLoop, calls=%fused_computation.135 | loop fusion | flops 163840 | bytes 4108 | tf_op jit(solution)/shard_map/lt | solution.py:393
  111.5 2.0 %add_select_fusion = s32[4096]{0:T(1024)S(1)} fusion(s32[]{:T(128)} %bitcast.2, s32[]{:T(128)} %bitcast.1, s32[]{:T(128)} %bitcast), kind=kLoop, calls=%fused_computation.116 | loop fusion | flops 159744 | bytes 16396 | tf_op jit(solution)/shard_map/jit(remainder)/select_n | solution.py:385
  116.2 1.7 %fusion.90 = (bf16[160,4096]{1,0:T(8,128)(2,1)}, bf16[160,4096]{1,0:T(8,128)(2,1)}) fusion(bf16[320,4096]{1,0:T(8,128)(2,1)S(1)} %pad_maximum_fusion), kind=kLoop, calls=%fused_computation.159 | loop fusion | bytes 5242880 | tf_op jit(solution)/shard_map/slice | solution.py:377
  118.0 30.5 %while.5 = (s32[]{:T(128)}, f32[128,2,4,80]{0,3,2,1:T(8,128)S(1)}, f32[128,2,4]{0,2,1:T(4,128)S(1)}, f32[128,2,4]{0,2,1:T(4,128)S(1)}, pred[4096]{0:T(1024)(128)...) while((s32[]{:T(128)}, f32[128,2,4,80]{0,3,2,1:T(8,128)S(1)}, ...), condition=%wide.region_4.5_spmd.clone, body=%wide.region_1.4_spmd.clone.sunk | while | flops 174118016 | bytes 7774939 | solution.py:273
  118.4 1.4 fusion.106
  120.3 1.5 fusion.109
  122.2 1.4 fusion.106
  124.1 1.5 fusion.109
  126.0 1.4 fusion.106
  127.9 1.5 fusion.109
  129.8 1.4 fusion.106
  131.7 1.5 fusion.109
  135.6 1.5 fusion.109
  137.4 1.4 fusion.106
  139.4 1.5 fusion.109
  141.3 1.4 fusion.106
  143.2 1.5 fusion.109
  145.1 1.4 fusion.106
  147.0 1.5 fusion.109
  151.6 3.1 %collective-permute-start.5 = (bf16[128,640]{0,1:T(8,128)(2,1)S(1)}, bf16[128,640]{0,1:T(8,128)(2,1)S(1)}, u32[]{:S(2)}, u32[]{:S(2)}) collective-permute-start(bf16[128,640]{0,1:T(8,128)(2,1)S(1)} %bitcast.153), channel_id=1, source_target_pairs={{1,0},{2,1},{3,2},{0,3},{5,4},{6,5},{7,6},{4,7},{9,8},{10,9},{11,1... | collective-permute-start | bytes 491528 | tf_op jit(solution)/shard_map/ppermute | solution.py:281
  154.6 2.9 %collective-permute-start.4 = (bf16[128,640]{0,1:T(8,128)(2,1)S(1)}, bf16[128,640]{0,1:T(8,128)(2,1)S(1)}, u32[]{:S(2)}, u32[]{:S(2)}) collective-permute-start(bf16[128,640]{0,1:T(8,128)(2,1)S(1)} %bitcast.154), channel_id=1, source_target_pairs={{2,0},{3,1},{0,2},{1,3},{6,4},{7,5},{4,6},{5,7},{10,8},{11,9},{8,1... | collective-permute-start | bytes 491528 | tf_op jit(solution)/shard_map/ppermute | solution.py:281
  157.6 2.0 %collective-permute-start.3 = (bf16[128,640]{0,1:T(8,128)(2,1)S(1)}, bf16[128,640]{0,1:T(8,128)(2,1)S(1)}, u32[]{:S(2)}, u32[]{:S(2)}) collective-permute-start(bf16[128,640]{0,1:T(8,128)(2,1)S(1)} %bitcast.155), channel_id=1, source_target_pairs={{3,0},{0,1},{1,2},{2,3},{7,4},{4,5},{5,6},{6,7},{11,8},{8,9},{9,10... | collective-permute-start | bytes 491528 | tf_op jit(solution)/shard_map/ppermute | solution.py:281
  161.0 2.0 %collective-permute-done.4 = bf16[128,640]{0,1:T(8,128)(2,1)S(1)} collective-permute-done((bf16[128,640]{0,1:T(8,128)(2,1)S(1)}, bf16[128,640]{0,1:T(8,128)(2,1)S(1)}, u32[]{:S(2)}, u32[]{:S(2)}) %collective-permute-start.4) | collective-permute-done | bytes 163872 | tf_op jit(solution)/shard_map/ppermute | solution.py:281
  163.0 4.0 %collective-permute-done.3 = bf16[128,640]{0,1:T(8,128)(2,1)S(1)} collective-permute-done((bf16[128,640]{0,1:T(8,128)(2,1)S(1)}, bf16[128,640]{0,1:T(8,128)(2,1)S(1)}, u32[]{:S(2)}, u32[]{:S(2)}) %collective-permute-start.3) | collective-permute-done | bytes 163872 | tf_op jit(solution)/shard_map/ppermute | solution.py:281
  167.2 4.2 %fusion.38 = bf16[128,640]{1,0:T(8,128)(2,1)} fusion(bf16[2560,1600]{1,0:T(8,128)(2,1)} %reshape.241, bf16[128,640]{0,1:T(8,128)(2,1)S(1)} %get-tuple-element.282, bf16[128,640]{0,1:T(8,128)(2,1)S(1)} %get-tuple-element.283, bf16[128,640]{0,1:T(8,128)(2,1)S(1)} %get-tuple-element.284, bf16[128,640]{0,1:T(8,128)(2,1)S(1)} %get-tuple-element.281), kind=kOutput, calls=%fused_computation.55 | convolution fusion | flops 422133760 | bytes 4096000 | tf_op jit(solution)/shard_map/dot_general | solution.py:414
  (130 shorter events, 20.5 us)
Async XLA Ops:
  72.0 15.3 %copy-start.5 = (bf16[2560]{0:T(1024)(128)(2,1)S(1)}, bf16[2560]{0:T(1024)(128)(2,1)}, u32[]{:S(2)}) copy-start(bf16[2560]{0:T(1024)(128)(2,1)} %param.14) | copy-start | bytes 15364
  72.0 15.3 %copy-start.3 = (bf16[4,128,640]{2,1,0:T(8,128)(2,1)S(1)}, bf16[4,128,640]{2,1,0:T(8,128)(2,1)}, u32[]{:S(2)}) copy-start(bf16[4,128,640]{2,1,0:T(8,128)(2,1)} %get-tuple-element.208) | copy-start | bytes 1966084
  87.6 4.9 %copy-start.6 = (s32[32]{0:T(128)S(1)}, s32[32]{0:T(128)}, u32[]{:S(2)}) copy-start(s32[32]{0:T(128)} %param.21) | copy-start | bytes 388
  87.7 19.9 %copy-start.7 = (s32[32]{0:T(128)S(1)}, s32[32]{0:T(128)}, u32[]{:S(2)}) copy-start(s32[32]{0:T(128)} %param.22) | copy-start | bytes 388
  87.7 28.0 %copy-start = (bf16[4,320,1024]{2,1,0:T(8,128)(2,1)S(1)}, bf16[4,320,1024]{2,1,0:T(8,128)(2,1)}, u32[]{:S(2)}) copy-start(bf16[4,320,1024]{2,1,0:T(8,128)(2,1)} %get-tuple-element.207) | copy-start | bytes 7864324
  94.0 0.6 copy-start.4
  95.3 53.5 %collective-permute-start.2 = (bf16[128,320]{0,1:T(8,128)(2,1)}, bf16[128,320]{0,1:T(8,128)(2,1)}, u32[]{:S(2)}, u32[]{:S(2)}) collective-permute-start(bf16[128,320]{0,1:T(8,128)(2,1)} %get-tuple-element.302), channel_id=1, source_target_pairs={{0,12},{4,8},{8,4},{12,0},{16,28},{20,24},{24,20},{28,16},{32,44},... | collective-permute-start | bytes 245768 | tf_op jit(solution)/shard_map/ppermute | solution.py:332
  101.3 47.6 %collective-permute-start.1 = (bf16[128,320]{0,1:T(8,128)(2,1)}, bf16[128,320]{0,1:T(8,128)(2,1)}, u32[]{:S(2)}, u32[]{:S(2)}) collective-permute-start(bf16[128,320]{0,1:T(8,128)(2,1)} %get-tuple-element.302), channel_id=1, source_target_pairs={{0,8},{4,12},{8,0},{12,4},{16,24},{20,28},{24,16},{28,20},{32,40},... | collective-permute-start | bytes 245768 | tf_op jit(solution)/shard_map/ppermute | solution.py:332
  104.9 44.0 %collective-permute-start = (bf16[128,320]{0,1:T(8,128)(2,1)}, bf16[128,320]{0,1:T(8,128)(2,1)}, u32[]{:S(2)}, u32[]{:S(2)}) collective-permute-start(bf16[128,320]{0,1:T(8,128)(2,1)} %get-tuple-element.302), channel_id=1, source_target_pairs={{0,4},{4,0},{8,12},{12,8},{16,20},{20,16},{24,28},{28,24},{32,36},... | collective-permute-start | bytes 245768 | tf_op jit(solution)/shard_map/ppermute | solution.py:332
  116.2 1.8 %copy-start.8 = (f32[128,2,4,80]{0,3,2,1:T(8,128)S(1)}, f32[128,2,4,80]{0,3,2,1:T(8,128)}, u32[]{:S(2)}) copy-start(f32[128,2,4,80]{0,3,2,1:T(8,128)} %custom-call) | copy-start | bytes 983044
  151.0 8.6 %copy-start.1 = (bf16[160,1024]{1,0:T(8,128)(2,1)S(1)}, bf16[160,1024]{1,0:T(8,128)(2,1)}, u32[]{:S(2)}) copy-start(bf16[160,1024]{1,0:T(8,128)(2,1)} %param.20) | copy-start | bytes 983044
  151.0 8.6 %copy-start.2 = (bf16[160,1024]{1,0:T(8,128)(2,1)S(1)}, bf16[160,1024]{1,0:T(8,128)(2,1)}, u32[]{:S(2)}) copy-start(bf16[160,1024]{1,0:T(8,128)(2,1)} %param.19) | copy-start | bytes 983044
  151.6 9.4 %collective-permute-start.5 = (bf16[128,640]{0,1:T(8,128)(2,1)S(1)}, bf16[128,640]{0,1:T(8,128)(2,1)S(1)}, u32[]{:S(2)}, u32[]{:S(2)}) collective-permute-start(bf16[128,640]{0,1:T(8,128)(2,1)S(1)} %bitcast.153), channel_id=1, source_target_pairs={{1,0},{2,1},{3,2},{0,3},{5,4},{6,5},{7,6},{4,7},{9,8},{10,9},{11,1... | collective-permute-start | bytes 491528 | tf_op jit(solution)/shard_map/ppermute | solution.py:281
  154.6 8.3 %collective-permute-start.4 = (bf16[128,640]{0,1:T(8,128)(2,1)S(1)}, bf16[128,640]{0,1:T(8,128)(2,1)S(1)}, u32[]{:S(2)}, u32[]{:S(2)}) collective-permute-start(bf16[128,640]{0,1:T(8,128)(2,1)S(1)} %bitcast.154), channel_id=1, source_target_pairs={{2,0},{3,1},{0,2},{1,3},{6,4},{7,5},{4,6},{5,7},{10,8},{11,9},{8,1... | collective-permute-start | bytes 491528 | tf_op jit(solution)/shard_map/ppermute | solution.py:281
  157.6 9.4 %collective-permute-start.3 = (bf16[128,640]{0,1:T(8,128)(2,1)S(1)}, bf16[128,640]{0,1:T(8,128)(2,1)S(1)}, u32[]{:S(2)}, u32[]{:S(2)}) collective-permute-start(bf16[128,640]{0,1:T(8,128)(2,1)S(1)} %bitcast.155), channel_id=1, source_target_pairs={{3,0},{0,1},{1,2},{2,3},{7,4},{4,5},{5,6},{6,7},{11,8},{8,9},{9,10... | collective-permute-start | bytes 491528 | tf_op jit(solution)/shard_map/ppermute | solution.py:281

commit v6 on v5

--- a/solution.py
+++ b/solution.py
@@ -33,7 +33,7 @@
 
 
 WIDE = ("z", "x", "c")
-RING_SUBS = 4
+RING_SUBS = 8
 
 
 def gather_kernel(nz, nx, nc, nn, blk_ref, cache_ref, tok_ref, out_ref, cache_out, tok_out,
@@ -391,7 +391,7 @@
         old_values,
         cached_pos,
         cached_pos < length,
-        512,
+        1024,
     )
     key_cols = new_keys.T
     value_cols = new_values.T
@@ -405,7 +405,7 @@
         value_cols,
         new_pos,
         jnp.ones((new_count,), dtype=bool),
-        512,
+        1024,
     )
     accum, top_score, total = state
     attended = (accum / total[..., None]).astype(jnp.bfloat16).reshape(tok_rows, query_width)

time: 173 us -> 178 us (1.029)
  other arithmetic: 17.3 us -> 26 us
  matrix products: 33.3 us -> 30.7 us
  local copies, waits for them, and re-layouts: 23.7 us -> 21.9 us
    reduce_sum x9 -> x5, other arithmetic: 4 us -> 13.3 us  [step(): sum_new = sum_old * rescale + jnp.sum(weights, axis=-1)]
    dot_general x9 -> x5, matrix products: 12.2 us -> 9.91 us  [step(): jnp.einsum('tgrk,gdk->tgrd', weights.astype(jnp.bfloat16), block_values,...]
    dot_general x9 -> x5, matrix products: 12 us -> 11.7 us  [step(): jnp.einsum('tgrd,gdk->tgrk', queries, block_keys, preferred_element_type=...]
  transfers between devices with their start and end apart: 6 -> 6, of which waited for: 2 -> 2; matrix products, arithmetic and copies ran while one was open for 24% -> 25% of each run, Pallas kernels for 0% -> 0%
where the time goes in v6:
time: 178 us; the launch traced here: 176 us
  Pallas kernels  68.9 us (39%)
  matrix products  30.7 us (17%)
  other arithmetic  26 us (15%)
  local copies, waits for them, and re-layouts  21.9 us (12%)
  starting transfers between devices  19.6 us (11%)
  waiting for transfers between devices  6.03 us (3%)
  between operations  3.19 us (2%)
    pallas_call x1, Pallas kernels, gather_wide(): pl.pallas_call(functools.partial(gather_kernel, nz, nx, nc, nn), out_shap...  68.9 us
    reshape x1, local copies, waits for them, and re-layouts, shards(): all_weights = gathered.reshape(-1, joined_width)  15.3 us
    reduce_sum x5, other arithmetic, step(): sum_new = sum_old * rescale + jnp.sum(weights, axis=-1)  13.3 us
    dot_general x5, matrix products, step(): jnp.einsum('tgrd,gdk->tgrk', queries, block_keys, preferred_element_type=...  11.7 us
    ppermute x3, starting transfers between devices, group_route_pieces(): pieces.append(lax.ppermute(block, WIDE, route))  11.6 us
    dot_general x5, matrix products, step(): jnp.einsum('tgrk,gdk->tgrd', weights.astype(jnp.bfloat16), block_values,...  9.91 us
    ppermute x3, starting transfers between devices, exchange(): lax.ppermute(block, axis, [(pairing(d, k), d) for d in range(count)])  7.99 us
    ppermute x3, waiting for transfers between devices, exchange(): lax.ppermute(block, axis, [(pairing(d, k), d) for d in range(count)])  6.02 us
  transfers between devices with their start and end apart: 6, of which 2 were waited for; matrix products, arithmetic and copies ran while one was open for 25% of the time, Pallas kernels for 0%

profile of v6, /device:TPU:1, one launch (start us, length us, event | category | flops | bytes accessed | tf_op | source)
XLA Modules:
  0.0 176.5 jit_solution(4686558427921404985)
XLA Ops:
  0.6 0.9 concatenate.40
  2.3 2.0 %pad_maximum_fusion.1.cache_ref = bf16[320,1024]{1,0:T(8,128)(2,1)} fusion(bf16[160,1024]{1,0:T(8,128)(2,1)} %param.20, bf16[160,1024]{1,0:T(8,128)(2,1)} %param.19), kind=kLoop, calls=%fused_computation.58 | loop fusion | flops 1310720 | bytes 1310720 | tf_op jit(solution)/shard_map/concatenate | solution.py:341
  4.3 68.9 %shard_map.130 = (bf16[128,250,128]{2,1,0:T(8,128)(2,1)}, bf16[4,320,1024]{2,1,0:T(8,128)(2,1)}, bf16[4,128,640]{2,1,0:T(8,128)(2,1)}) custom-call(bf16[250,128]{1,0:T(8,128)(2,1)} %reshape.239.blk_ref, bf16[320,1024]{1,0:T(8,128)(2,1)} %pad_maximum_fusion.1.cache_ref, bf16[128,640]{1,0:T(8,128)(2,1)} %tok_ref.1), custom_call_target="tpu_custom_call" | custom-call | bytes 16384000 | tf_op jit(solution)/shard_map/pallas_call | solution.py:168
  73.2 15.3 %reshape.241 = bf16[2560,1600]{1,0:T(8,128)(2,1)} reshape(bf16[128,250,128]{2,1,0:T(8,128)(2,1)} %get-tuple-element.209) | data formatting | bytes 16384000 | tf_op jit(solution)/shard_map/reshape | solution.py:344
  88.8 4.8 %fusion.27 = f32[128,960]{0,1:T(8,128)S(1)} fusion(bf16[2560,1600]{1,0:T(8,128)(2,1)} %reshape.241, f32[2560]{0:T(1024)S(1)} %convert_element_type.43, f32[128]{0:T(128)S(1)} %add_rsqrt_fusion, bf16[128,640]{1,0:T(8,128)(2,1)S(1)} %get-tuple-element.286, bf16[128,640]{1,0:T(8,128)(2,1)S(1)} %get-tuple-element.287, ...), kind=kOutput, calls=%fused_computation.29 | convolution fusion | flops 632750080 | bytes 6400512 | tf_op jit(solution)/shard_map/dot_general | solution.py:355
  96.3 6.1 %collective-permute-start.2 = (bf16[128,320]{0,1:T(8,128)(2,1)}, bf16[128,320]{0,1:T(8,128)(2,1)}, u32[]{:S(2)}, u32[]{:S(2)}) collective-permute-start(bf16[128,320]{0,1:T(8,128)(2,1)} %get-tuple-element.302), channel_id=1, source_target_pairs={{0,12},{4,8},{8,4},{12,0},{16,28},{20,24},{24,20},{28,16},{32,44},... | collective-permute-start | bytes 245768 | tf_op jit(solution)/shard_map/ppermute | solution.py:332
  102.4 3.6 %collective-permute-start.1 = (bf16[128,320]{0,1:T(8,128)(2,1)}, bf16[128,320]{0,1:T(8,128)(2,1)}, u32[]{:S(2)}, u32[]{:S(2)}) collective-permute-start(bf16[128,320]{0,1:T(8,128)(2,1)} %get-tuple-element.302), channel_id=1, source_target_pairs={{0,8},{4,12},{8,0},{12,4},{16,24},{20,28},{24,16},{28,20},{32,40},... | collective-permute-start | bytes 245768 | tf_op jit(solution)/shard_map/ppermute | solution.py:332
  106.0 1.9 %collective-permute-start = (bf16[128,320]{0,1:T(8,128)(2,1)}, bf16[128,320]{0,1:T(8,128)(2,1)}, u32[]{:S(2)}, u32[]{:S(2)}) collective-permute-start(bf16[128,320]{0,1:T(8,128)(2,1)} %get-tuple-element.302), channel_id=1, source_target_pairs={{0,4},{4,0},{8,12},{12,8},{16,20},{20,16},{24,28},{28,24},{32,36},... | collective-permute-start | bytes 245768 | tf_op jit(solution)/shard_map/ppermute | solution.py:332
  109.3 1.3 dynamic_slice.73
  110.6 2.0 %broadcast_compare_fusion = pred[4096]{0:T(1024)(128)(4,1)S(1)} fusion(s32[]{:T(128)} %bitcast.2, s32[]{:T(128)} %bitcast.1, s32[]{:T(128)} %bitcast), kind=kLoop, calls=%fused_computation.134 | loop fusion | flops 163840 | bytes 4108 | tf_op jit(solution)/shard_map/lt | solution.py:393
  112.6 2.0 %add_select_fusion = s32[4096]{0:T(1024)S(1)} fusion(s32[]{:T(128)} %bitcast.2, s32[]{:T(128)} %bitcast.1, s32[]{:T(128)} %bitcast), kind=kLoop, calls=%fused_computation.115 | loop fusion | flops 159744 | bytes 16396 | tf_op jit(solution)/shard_map/jit(remainder)/select_n | solution.py:385
  117.6 35.9 %while.5 = (s32[]{:T(128)}, f32[128,2,4,80]{0,3,2,1:T(8,128)}, f32[128,2,4]{0,2,1:T(4,128)S(1)}, f32[128,2,4]{0,2,1:T(4,128)S(1)}, pred[4096]{0:T(1024)(128)(4,1...) while((s32[]{:T(128)}, f32[128,2,4,80]{0,3,2,1:T(8,128)}, ...), condition=%wide.region_4.5_spmd.clone, body=%wide.region_1.4_spmd.clone.sunk | while | flops 347985024 | bytes 31441140 | solution.py:273
  118.0 2.8 %fusion.110 = (f32[128,2,4]{0,2,1:T(4,128)S(1)}, f32[2,1024,128,4]{2,1,3,0:T(8,128)}) fusion(pred[128,1024]{0,1:T(8,128)(4,1)S(1)} %fusion.109, bf16[128,2,4,80]{0,3,2,1:T(8,128)(2,1)S(1)} %get-tuple-element.419, bf16[2,80,4096]{2,1,0:T(8,128)(2,1)S(1)} %get-tuple-element.418, s32[]{:T(128)S(6)} %select_n.240), kind=kOutput, calls=%fused_computation.3.clone.1 | convolution fusion | flops 170916864 | bytes 4820996 | tf_op jit(solution)/shard_map/while/body/eval_jaxpr/tgrd,gdk->tgrk/dot_general | solution.py:252
  120.9 3.2 %fusion.111 = f32[128,2,4]{0,2,1:T(4,128)S(1)} fusion(f32[2,1024,128,4]{2,1,3,0:T(8,128)} %get-tuple-element.380, f32[128,2,4]{0,2,1:T(4,128)S(1)} %select_maximum_fusion.2, pred[128,1024]{0,1:T(8,128)(4,1)S(1)} %fusion.109), kind=kLoop, calls=%fused_computation.6.clone.1 | loop fusion | flops 4193280 | bytes 4333568 | tf_op jit(solution)/shard_map/while/body/eval_jaxpr/reduce_sum | solution.py:264
  124.3 1.6 fusion.113
  126.3 2.8 %fusion.110 = (f32[128,2,4]{0,2,1:T(4,128)S(1)}, f32[2,1024,128,4]{2,1,3,0:T(8,128)}) fusion(pred[128,1024]{0,1:T(8,128)(4,1)S(1)} %fusion.109, bf16[128,2,4,80]{0,3,2,1:T(8,128)(2,1)S(1)} %get-tuple-element.419, bf16[2,80,4096]{2,1,0:T(8,128)(2,1)S(1)} %get-tuple-element.418, s32[]{:T(128)S(6)} %select_n.240), kind=kOutput, calls=%fused_computation.3.clone.1 | convolution fusion | flops 170916864 | bytes 4820996 | tf_op jit(solution)/shard_map/while/body/eval_jaxpr/tgrd,gdk->tgrk/dot_general | solution.py:252
  129.1 3.2 %fusion.111 = f32[128,2,4]{0,2,1:T(4,128)S(1)} fusion(f32[2,1024,128,4]{2,1,3,0:T(8,128)} %get-tuple-element.380, f32[128,2,4]{0,2,1:T(4,128)S(1)} %select_maximum_fusion.2, pred[128,1024]{0,1:T(8,128)(4,1)S(1)} %fusion.109), kind=kLoop, calls=%fused_computation.6.clone.1 | loop fusion | flops 4193280 | bytes 4333568 | tf_op jit(solution)/shard_map/while/body/eval_jaxpr/reduce_sum | solution.py:264
  132.5 2.6 %fusion.113 = f32[128,2,4,80]{0,3,2,1:T(8,128)} fusion(f32[2,1024,128,4]{2,1,3,0:T(8,128)S(1)} %copy-done, f32[128,2,4]{0,2,1:T(4,128)S(1)} %select_maximum_fusion.2, pred[128,1024]{0,1:T(8,128)(4,1)S(1)} %fusion.109, f32[128,2,4,80]{0,3,2,1:T(8,128)} %get-tuple-element.399, bf16[2,80,4096]{2,1,0:T(8,128)(2,1)S(1)} %get-tuple-element.420, ...), kind=kOutput, calls=%fused_computation.11.clone.1 | convolution fusion | flops 172212224 | bytes 5316613 | tf_op jit(solution)/shard_map/while/body/eval_jaxpr/tgrk,gdk->tgrd/dot_general | solution.py:265
  135.5 2.8 %fusion.110 = (f32[128,2,4]{0,2,1:T(4,128)S(1)}, f32[2,1024,128,4]{2,1,3,0:T(8,128)}) fusion(pred[128,1024]{0,1:T(8,128)(4,1)S(1)} %fusion.109, bf16[128,2,4,80]{0,3,2,1:T(8,128)(2,1)S(1)} %get-tuple-element.419, bf16[2,80,4096]{2,1,0:T(8,128)(2,1)S(1)} %get-tuple-element.418, s32[]{:T(128)S(6)} %select_n.240), kind=kOutput, calls=%fused_computation.3.clone.1 | convolution fusion | flops 170916864 | bytes 4820996 | tf_op jit(solution)/shard_map/while/body/eval_jaxpr/tgrd,gdk->tgrk/dot_general | solution.py:252
  138.3 3.2 %fusion.111 = f32[128,2,4]{0,2,1:T(4,128)S(1)} fusion(f32[2,1024,128,4]{2,1,3,0:T(8,128)} %get-tuple-element.380, f32[128,2,4]{0,2,1:T(4,128)S(1)} %select_maximum_fusion.2, pred[128,1024]{0,1:T(8,128)(4,1)S(1)} %fusion.109), kind=kLoop, calls=%fused_computation.6.clone.1 | loop fusion | flops 4193280 | bytes 4333568 | tf_op jit(solution)/shard_map/while/body/eval_jaxpr/reduce_sum | solution.py:264
  141.8 2.6 %fusion.113 = f32[128,2,4,80]{0,3,2,1:T(8,128)} fusion(f32[2,1024,128,4]{2,1,3,0:T(8,128)S(1)} %copy-done, f32[128,2,4]{0,2,1:T(4,128)S(1)} %select_maximum_fusion.2, pred[128,1024]{0,1:T(8,128)(4,1)S(1)} %fusion.109, f32[128,2,4,80]{0,3,2,1:T(8,128)} %get-tuple-element.399, bf16[2,80,4096]{2,1,0:T(8,128)(2,1)S(1)} %get-tuple-element.420, ...), kind=kOutput, calls=%fused_computation.11.clone.1 | convolution fusion | flops 172212224 | bytes 5316613 | tf_op jit(solution)/shard_map/while/body/eval_jaxpr/tgrk,gdk->tgrd/dot_general | solution.py:265
  144.7 2.8 %fusion.110 = (f32[128,2,4]{0,2,1:T(4,128)S(1)}, f32[2,1024,128,4]{2,1,3,0:T(8,128)}) fusion(pred[128,1024]{0,1:T(8,128)(4,1)S(1)} %fusion.109, bf16[128,2,4,80]{0,3,2,1:T(8,128)(2,1)S(1)} %get-tuple-element.419, bf16[2,80,4096]{2,1,0:T(8,128)(2,1)S(1)} %get-tuple-element.418, s32[]{:T(128)S(6)} %select_n.240), kind=kOutput, calls=%fused_computation.3.clone.1 | convolution fusion | flops 170916864 | bytes 4820996 | tf_op jit(solution)/shard_map/while/body/eval_jaxpr/tgrd,gdk->tgrk/dot_general | solution.py:252
  147.5 3.2 %fusion.111 = f32[128,2,4]{0,2,1:T(4,128)S(1)} fusion(f32[2,1024,128,4]{2,1,3,0:T(8,128)} %get-tuple-element.380, f32[128,2,4]{0,2,1:T(4,128)S(1)} %select_maximum_fusion.2, pred[128,1024]{0,1:T(8,128)(4,1)S(1)} %fusion.109), kind=kLoop, calls=%fused_computation.6.clone.1 | loop fusion | flops 4193280 | bytes 4333568 | tf_op jit(solution)/shard_map/while/body/eval_jaxpr/reduce_sum | solution.py:264
  151.0 2.6 %fusion.113 = f32[128,2,4,80]{0,3,2,1:T(8,128)} fusion(f32[2,1024,128,4]{2,1,3,0:T(8,128)S(1)} %copy-done, f32[128,2,4]{0,2,1:T(4,128)S(1)} %select_maximum_fusion.2, pred[128,1024]{0,1:T(8,128)(4,1)S(1)} %fusion.109, f32[128,2,4,80]{0,3,2,1:T(8,128)} %get-tuple-element.399, bf16[2,80,4096]{2,1,0:T(8,128)(2,1)S(1)} %get-tuple-element.420, ...), kind=kOutput, calls=%fused_computation.11.clone.1 | convolution fusion | flops 172212224 | bytes 5316613 | tf_op jit(solution)/shard_map/while/body/eval_jaxpr/tgrk,gdk->tgrd/dot_general | solution.py:265
  153.9 1.0 pad_maximum_fusion.4
  156.6 3.1 %collective-permute-start.5 = (bf16[128,640]{0,1:T(8,128)(2,1)S(1)}, bf16[128,640]{0,1:T(8,128)(2,1)S(1)}, u32[]{:S(2)}, u32[]{:S(2)}) collective-permute-start(bf16[128,640]{0,1:T(8,128)(2,1)S(1)} %bitcast.157), channel_id=1, source_target_pairs={{1,0},{2,1},{3,2},{0,3},{5,4},{6,5},{7,6},{4,7},{9,8},{10,9},{11,1... | collective-permute-start | bytes 491528 | tf_op jit(solution)/shard_map/ppermute | solution.py:281
  159.7 2.9 %collective-permute-start.4 = (bf16[128,640]{0,1:T(8,128)(2,1)S(1)}, bf16[128,640]{0,1:T(8,128)(2,1)S(1)}, u32[]{:S(2)}, u32[]{:S(2)}) collective-permute-start(bf16[128,640]{0,1:T(8,128)(2,1)S(1)} %bitcast.158), channel_id=1, source_target_pairs={{2,0},{3,1},{0,2},{1,3},{6,4},{7,5},{4,6},{5,7},{10,8},{11,9},{8,1... | collective-permute-start | bytes 491528 | tf_op jit(solution)/shard_map/ppermute | solution.py:281
  162.7 2.0 %collective-permute-start.3 = (bf16[128,640]{0,1:T(8,128)(2,1)S(1)}, bf16[128,640]{0,1:T(8,128)(2,1)S(1)}, u32[]{:S(2)}, u32[]{:S(2)}) collective-permute-start(bf16[128,640]{0,1:T(8,128)(2,1)S(1)} %bitcast.159), channel_id=1, source_target_pairs={{3,0},{0,1},{1,2},{2,3},{7,4},{4,5},{5,6},{6,7},{11,8},{8,9},{9,10... | collective-permute-start | bytes 491528 | tf_op jit(solution)/shard_map/ppermute | solution.py:281
  164.7 1.4 fusion.62
  166.1 2.0 %collective-permute-done.4 = bf16[128,640]{0,1:T(8,128)(2,1)S(1)} collective-permute-done((bf16[128,640]{0,1:T(8,128)(2,1)S(1)}, bf16[128,640]{0,1:T(8,128)(2,1)S(1)}, u32[]{:S(2)}, u32[]{:S(2)}) %collective-permute-start.4) | collective-permute-done | bytes 163872 | tf_op jit(solution)/shard_map/ppermute | solution.py:281
  168.0 4.1 %collective-permute-done.3 = bf16[128,640]{0,1:T(8,128)(2,1)S(1)} collective-permute-done((bf16[128,640]{0,1:T(8,128)(2,1)S(1)}, bf16[128,640]{0,1:T(8,128)(2,1)S(1)}, u32[]{:S(2)}, u32[]{:S(2)}) %collective-permute-start.3) | collective-permute-done | bytes 163872 | tf_op jit(solution)/shard_map/ppermute | solution.py:281
  172.2 4.2 %fusion.42 = bf16[128,640]{1,0:T(8,128)(2,1)} fusion(bf16[2560,1600]{1,0:T(8,128)(2,1)} %reshape.241, bf16[128,640]{0,1:T(8,128)(2,1)S(1)} %get-tuple-element.282, bf16[128,640]{0,1:T(8,128)(2,1)S(1)} %get-tuple-element.283, bf16[128,640]{0,1:T(8,128)(2,1)S(1)} %get-tuple-element.284, bf16[128,640]{0,1:T(8,128)(2,1)S(1)} %get-tuple-element.281), kind=kOutput, calls=%fused_computation.54 | convolution fusion | flops 422133760 | bytes 4096000 | tf_op jit(solution)/shard_map/dot_general | solution.py:414
  (98 shorter events, 10.4 us)
Async XLA Ops:
  73.2 15.3 %copy-start.6 = (bf16[2560]{0:T(1024)(128)(2,1)S(1)}, bf16[2560]{0:T(1024)(128)(2,1)}, u32[]{:S(2)}) copy-start(bf16[2560]{0:T(1024)(128)(2,1)} %param.14) | copy-start | bytes 15364
  73.2 15.3 %copy-start.4 = (bf16[4,128,640]{2,1,0:T(8,128)(2,1)S(1)}, bf16[4,128,640]{2,1,0:T(8,128)(2,1)}, u32[]{:S(2)}) copy-start(bf16[4,128,640]{2,1,0:T(8,128)(2,1)} %get-tuple-element.208) | copy-start | bytes 1966084
  88.8 4.9 %copy-start.7 = (s32[32]{0:T(128)S(1)}, s32[32]{0:T(128)}, u32[]{:S(2)}) copy-start(s32[32]{0:T(128)} %param.21) | copy-start | bytes 388
  88.8 19.8 %copy-start.8 = (s32[32]{0:T(128)S(1)}, s32[32]{0:T(128)}, u32[]{:S(2)}) copy-start(s32[32]{0:T(128)} %param.22) | copy-start | bytes 388
  88.8 28.0 %copy-start.1 = (bf16[4,320,1024]{2,1,0:T(8,128)(2,1)S(1)}, bf16[4,320,1024]{2,1,0:T(8,128)(2,1)}, u32[]{:S(2)}) copy-start(bf16[4,320,1024]{2,1,0:T(8,128)(2,1)} %get-tuple-element.207) | copy-start | bytes 7864324
  95.1 0.6 copy-start.5
  96.3 57.5 %collective-permute-start.2 = (bf16[128,320]{0,1:T(8,128)(2,1)}, bf16[128,320]{0,1:T(8,128)(2,1)}, u32[]{:S(2)}, u32[]{:S(2)}) collective-permute-start(bf16[128,320]{0,1:T(8,128)(2,1)} %get-tuple-element.302), channel_id=1, source_target_pairs={{0,12},{4,8},{8,4},{12,0},{16,28},{20,24},{24,20},{28,16},{32,44},... | collective-permute-start | bytes 245768 | tf_op jit(solution)/shard_map/ppermute | solution.py:332
  102.4 51.4 %collective-permute-start.1 = (bf16[128,320]{0,1:T(8,128)(2,1)}, bf16[128,320]{0,1:T(8,128)(2,1)}, u32[]{:S(2)}, u32[]{:S(2)}) collective-permute-start(bf16[128,320]{0,1:T(8,128)(2,1)} %get-tuple-element.302), channel_id=1, source_target_pairs={{0,8},{4,12},{8,0},{12,4},{16,24},{20,28},{24,16},{28,20},{32,40},... | collective-permute-start | bytes 245768 | tf_op jit(solution)/shard_map/ppermute | solution.py:332
  106.0 47.9 %collective-permute-start = (bf16[128,320]{0,1:T(8,128)(2,1)}, bf16[128,320]{0,1:T(8,128)(2,1)}, u32[]{:S(2)}, u32[]{:S(2)}) collective-permute-start(bf16[128,320]{0,1:T(8,128)(2,1)} %get-tuple-element.302), channel_id=1, source_target_pairs={{0,4},{4,0},{8,12},{12,8},{16,20},{20,16},{24,28},{28,24},{32,36},... | collective-permute-start | bytes 245768 | tf_op jit(solution)/shard_map/ppermute | solution.py:332
  120.9 3.4 %copy-start = (f32[2,1024,128,4]{2,1,3,0:T(8,128)S(1)}, f32[2,1024,128,4]{2,1,3,0:T(8,128)}, u32[]{:S(2)}) copy-start(f32[2,1024,128,4]{2,1,3,0:T(8,128)} %get-tuple-element.380) | copy-start | bytes 12582916 | tf_op jit(solution)/shard_map/while
  129.1 3.4 %copy-start = (f32[2,1024,128,4]{2,1,3,0:T(8,128)S(1)}, f32[2,1024,128,4]{2,1,3,0:T(8,128)}, u32[]{:S(2)}) copy-start(f32[2,1024,128,4]{2,1,3,0:T(8,128)} %get-tuple-element.380) | copy-start | bytes 12582916 | tf_op jit(solution)/shard_map/while
  138.3 3.4 %copy-start = (f32[2,1024,128,4]{2,1,3,0:T(8,128)S(1)}, f32[2,1024,128,4]{2,1,3,0:T(8,128)}, u32[]{:S(2)}) copy-start(f32[2,1024,128,4]{2,1,3,0:T(8,128)} %get-tuple-element.380) | copy-start | bytes 12582916 | tf_op jit(solution)/shard_map/while
  147.5 3.4 %copy-start = (f32[2,1024,128,4]{2,1,3,0:T(8,128)S(1)}, f32[2,1024,128,4]{2,1,3,0:T(8,128)}, u32[]{:S(2)}) copy-start(f32[2,1024,128,4]{2,1,3,0:T(8,128)} %get-tuple-element.380) | copy-start | bytes 12582916 | tf_op jit(solution)/shard_map/while
  155.1 1.0 copy-start.9
  156.1 8.6 %copy-start.2 = (bf16[160,1024]{1,0:T(8,128)(2,1)S(1)}, bf16[160,1024]{1,0:T(8,128)(2,1)}, u32[]{:S(2)}) copy-start(bf16[160,1024]{1,0:T(8,128)(2,1)} %param.20) | copy-start | bytes 983044
  156.1 8.6 %copy-start.3 = (bf16[160,1024]{1,0:T(8,128)(2,1)S(1)}, bf16[160,1024]{1,0:T(8,128)(2,1)}, u32[]{:S(2)}) copy-start(bf16[160,1024]{1,0:T(8,128)(2,1)} %param.19) | copy-start | bytes 983044
  156.6 9.4 %collective-permute-start.5 = (bf16[128,640]{0,1:T(8,128)(2,1)S(1)}, bf16[128,640]{0,1:T(8,128)(2,1)S(1)}, u32[]{:S(2)}, u32[]{:S(2)}) collective-permute-start(bf16[128,640]{0,1:T(8,128)(2,1)S(1)} %bitcast.157), channel_id=1, source_target_pairs={{1,0},{2,1},{3,2},{0,3},{5,4},{6,5},{7,6},{4,7},{9,8},{10,9},{11,1... | collective-permute-start | bytes 491528 | tf_op jit(solution)/shard_map/ppermute | solution.py:281
  159.7 8.3 %collective-permute-start.4 = (bf16[128,640]{0,1:T(8,128)(2,1)S(1)}, bf16[128,640]{0,1:T(8,128)(2,1)S(1)}, u32[]{:S(2)}, u32[]{:S(2)}) collective-permute-start(bf16[128,640]{0,1:T(8,128)(2,1)S(1)} %bitcast.158), channel_id=1, source_target_pairs={{2,0},{3,1},{0,2},{1,3},{6,4},{7,5},{4,6},{5,7},{10,8},{11,9},{8,1... | collective-permute-start | bytes 491528 | tf_op jit(solution)/shard_map/ppermute | solution.py:281
  162.7 9.4 %collective-permute-start.3 = (bf16[128,640]{0,1:T(8,128)(2,1)S(1)}, bf16[128,640]{0,1:T(8,128)(2,1)S(1)}, u32[]{:S(2)}, u32[]{:S(2)}) collective-permute-start(bf16[128,640]{0,1:T(8,128)(2,1)S(1)} %bitcast.159), channel_id=1, source_target_pairs={{3,0},{0,1},{1,2},{2,3},{7,4},{4,5},{5,6},{6,7},{11,8},{8,9},{9,10... | collective-permute-start | bytes 491528 | tf_op jit(solution)/shard_map/ppermute | solution.py:281

commit v7 on v5

--- a/solution.py
+++ b/solution.py
@@ -36,7 +36,7 @@
 RING_SUBS = 4
 
 
-def gather_kernel(nz, nx, nc, nn, blk_ref, cache_ref, tok_ref, out_ref, cache_out, tok_out,
+def gather_kernel(nz, nx, nc, nn, blk_a, blk_b, cache_ref, tok_ref, out_a, out_b, cache_out, tok_out,
                   plane_send, plane_recv, ring_send, ring_recv, die_send, die_recv, local_sem,
                   cache_send, cache_recv, tok_send, tok_recv):
     z = lax.axis_index("z")
@@ -53,9 +53,7 @@
     dst_z = lax.rem(z + step_dir + nz, nz)
     src_z = lax.rem(z - step_dir + nz, nz)
     partner = (z, x, 1 - c, n)
-
-    def plane_slot(pz):
-        return out_ref.at[pl.ds(pl.multiple_of(pz * per_plane, per_plane), per_plane)]
+    weights = ((blk_a, out_a), (blk_b, out_b))
 
     def group_dev(p):
         return (z, x_base + p // nc, lax.rem(p, nc), n)
@@ -72,25 +70,29 @@
 
     sends = []
     locals_ = []
-    for src, dst in ((blk_ref, out_ref.at[me]), (cache_ref, cache_out.at[place]), (tok_ref, tok_out.at[n])):
+    pairs = ((blk_a, out_a.at[me]), (blk_b, out_b.at[me]), (cache_ref, cache_out.at[place]), (tok_ref, tok_out.at[n]))
+    for src, dst in pairs:
         cp = pltpu.make_async_copy(src, dst, local_sem.at[len(locals_)])
         cp.start()
         locals_.append(cp)
     for k in range(1, per_plane):
         peer = lax.rem(me_xc + k, per_plane)
-        cp = pltpu.make_async_remote_copy(
-            src_ref=blk_ref, dst_ref=out_ref.at[me],
-            send_sem=plane_send.at[k], recv_sem=plane_recv.at[k],
-            device_id=(z, peer // nc, lax.rem(peer, nc), n), device_id_type=MESH_ID)
-        cp.start()
-        sends.append(cp)
+        for a, (blk, out) in enumerate(weights):
+            cp = pltpu.make_async_remote_copy(
+                src_ref=blk, dst_ref=out.at[me],
+                send_sem=plane_send.at[a, k], recv_sem=plane_recv.at[a, k],
+                device_id=(z, peer // nc, lax.rem(peer, nc), n), device_id_type=MESH_ID)
+            cp.start()
+            sends.append(cp)
     for k in range(1, per_plane):
         sender = lax.rem(me_xc - k + per_plane, per_plane)
-        pltpu.make_async_remote_copy(
-            src_ref=blk_ref, dst_ref=out_ref.at[z * per_plane + sender],
-            send_sem=plane_send.at[k], recv_sem=plane_recv.at[k],
-            device_id=(z, x, c, n), device_id_type=MESH_ID).wait_recv()
+        for a, (blk, out) in enumerate(weights):
+            pltpu.make_async_remote_copy(
+                src_ref=blk, dst_ref=out.at[z * per_plane + sender],
+                send_sem=plane_send.at[a, k], recv_sem=plane_recv.at[a, k],
+                device_id=(z, x, c, n), device_id_type=MESH_ID).wait_recv()
     locals_[0].wait()
+    locals_[1].wait()
     for k in range(1, 2 * nc):
         cp = pltpu.make_async_remote_copy(
             src_ref=cache_ref, dst_ref=cache_out.at[place],
@@ -109,40 +111,44 @@
     subs = RING_SUBS
     sub_len = per_plane // subs
 
-    def sub_slot(pz, j):
-        return out_ref.at[pl.ds(pl.multiple_of(pz * per_plane + j * sub_len, sub_len), sub_len)]
-
-    def ring_copy(s, j, pz, device):
+    def sub_slot(out, pz, j):
+        return out.at[pl.ds(pl.multiple_of(pz * per_plane + j * sub_len, sub_len), sub_len)]
+
+    def ring_copy(a, s, j, pz, device):
+        out = weights[a][1]
         return pltpu.make_async_remote_copy(
-            src_ref=sub_slot(pz, j), dst_ref=sub_slot(pz, j),
-            send_sem=ring_send.at[s - 1, j], recv_sem=ring_recv.at[s - 1, j],
+            src_ref=sub_slot(out, pz, j), dst_ref=sub_slot(out, pz, j),
+            send_sem=ring_send.at[a, s - 1, j], recv_sem=ring_recv.at[a, s - 1, j],
             device_id=device, device_id_type=MESH_ID)
 
-    def die_copy(s, j, pz):
+    def die_copy(a, s, j, pz):
+        out = weights[a][1]
         return pltpu.make_async_remote_copy(
-            src_ref=sub_slot(pz, j), dst_ref=sub_slot(pz, j),
-            send_sem=die_send.at[s - 1, j], recv_sem=die_recv.at[s - 1, j],
+            src_ref=sub_slot(out, pz, j), dst_ref=sub_slot(out, pz, j),
+            send_sem=die_send.at[a, s - 1, j], recv_sem=die_recv.at[a, s - 1, j],
             device_id=partner, device_id_type=MESH_ID)
 
     for s in range(1, half + 1):
         send_z = lax.rem(z - step_dir * (s - 1) + 2 * nz, nz)
         for j in range(subs):
-            if s > 1:
-                ring_copy(s - 1, j, send_z, (src_z, x, c, n)).wait_recv()
-                if s - 1 < half:
-                    dp = die_copy(s - 1, j, send_z)
+            for a in range(len(weights)):
+                if s > 1:
+                    ring_copy(a, s - 1, j, send_z, (src_z, x, c, n)).wait_recv()
+                    dp = die_copy(a, s - 1, j, send_z)
                     dp.start()
                     sends.append(dp)
-            cp = ring_copy(s, j, send_z, (dst_z, x, c, n))
-            cp.start()
-            sends.append(cp)
+                cp = ring_copy(a, s, j, send_z, (dst_z, x, c, n))
+                cp.start()
+                sends.append(cp)
     last_z = lax.rem(z - step_dir * half + 2 * nz, nz)
     for j in range(subs):
-        ring_copy(half, j, last_z, (src_z, x, c, n)).wait_recv()
+        for a in range(len(weights)):
+            ring_copy(a, half, j, last_z, (src_z, x, c, n)).wait_recv()
     for s in range(1, half):
         other_z = lax.rem(z + step_dir * s + 2 * nz, nz)
         for j in range(subs):
-            die_copy(s, j, other_z).wait_recv()
+            for a in range(len(weights)):
+                die_copy(a, s, j, other_z).wait_recv()
     for k in range(1, 2 * nc):
         pltpu.make_async_remote_copy(
             src_ref=cache_ref, dst_ref=cache_out.at[place ^ k],
@@ -153,35 +159,36 @@
             src_ref=tok_ref, dst_ref=tok_out.at[lax.rem(n - k + nn, nn)],
             send_sem=tok_send.at[k], recv_sem=tok_recv.at[k],
             device_id=(z, x, c, n), device_id_type=MESH_ID).wait_recv()
-    for cp in locals_[1:]:
+    for cp in locals_[2:]:
         cp.wait()
     for cp in sends:
         cp.wait_send()
 
 
-def gather_wide(block, cache, tokens, nz, nx, nc, nn):
+def gather_wide(block_a, block_b, cache, tokens, nz, nx, nc, nn):
     count = nz * nx * nc
     half = nz // 2
     per_plane = nx * nc
     group = 2 * nc
-    nbytes = block.size * block.dtype.itemsize
+    nbytes = block_a.size * 2 + block_b.size * 2
     return pl.pallas_call(
         functools.partial(gather_kernel, nz, nx, nc, nn),
         out_shape=(
-            jax.ShapeDtypeStruct((count,) + block.shape, block.dtype),
+            jax.ShapeDtypeStruct((count,) + block_a.shape, block_a.dtype),
+            jax.ShapeDtypeStruct((count,) + block_b.shape, block_b.dtype),
             jax.ShapeDtypeStruct((group,) + cache.shape, cache.dtype),
             jax.ShapeDtypeStruct((nn,) + tokens.shape, tokens.dtype),
         ),
-        in_specs=[pl.BlockSpec(memory_space=pl.ANY)] * 3,
-        out_specs=[pl.BlockSpec(memory_space=pl.ANY)] * 3,
+        in_specs=[pl.BlockSpec(memory_space=pl.ANY)] * 4,
+        out_specs=[pl.BlockSpec(memory_space=pl.ANY)] * 4,
         scratch_shapes=[
-            pltpu.SemaphoreType.DMA((per_plane,)),
-            pltpu.SemaphoreType.DMA((per_plane,)),
-            pltpu.SemaphoreType.DMA((half, RING_SUBS)),
-            pltpu.SemaphoreType.DMA((half, RING_SUBS)),
-            pltpu.SemaphoreType.DMA((half, RING_SUBS)),
-            pltpu.SemaphoreType.DMA((half, RING_SUBS)),
-            pltpu.SemaphoreType.DMA((3,)),
+            pltpu.SemaphoreType.DMA((2, per_plane)),
+            pltpu.SemaphoreType.DMA((2, per_plane)),
+            pltpu.SemaphoreType.DMA((2, half, RING_SUBS)),
+            pltpu.SemaphoreType.DMA((2, half, RING_SUBS)),
+            pltpu.SemaphoreType.DMA((2, half, RING_SUBS)),
+            pltpu.SemaphoreType.DMA((2, half, RING_SUBS)),
+            pltpu.SemaphoreType.DMA((4,)),
             pltpu.SemaphoreType.DMA((group,)),
             pltpu.SemaphoreType.DMA((group,)),
             pltpu.SemaphoreType.DMA((nn,)),
@@ -189,7 +196,7 @@
         ],
         compiler_params=pltpu.CompilerParams(collective_id=0, has_side_effects=True),
         cost_estimate=pl.CostEstimate(flops=0, transcendentals=0, bytes_accessed=2 * count * nbytes),
-    )(block, cache, tokens)
+    )(block_a, block_b, cache, tokens)
 
 
 def gather_rows(block):
@@ -333,17 +340,27 @@
         return jnp.stack(pieces)
 
 
-    sizes = (query_weight.shape[1], key_weight.shape[1], value_weight.shape[1], out_weight.shape[1])
-    joined = jnp.concatenate([query_weight, key_weight, value_weight, out_weight], axis=1)
+    q_cols, kv_cols = query_weight.shape[1], key_weight.shape[1]
+    joined = jnp.concatenate([query_weight, out_weight, key_weight, value_weight], axis=1)
     block_rows, joined_width = joined.shape
+    tiled_rows = block_rows // 16 * 16
     dims = (lax.psum(1, "z"), lax.psum(1, "x"), lax.psum(1, "c"))
-    gathered, cache_blocks, tok_pieces = gather_wide(
-        joined.reshape(-1, 128), jnp.concatenate([cache_keys, cache_values], axis=0), tokens_in,
-        *dims, n_narrow)
+    part_a, part_b, cache_blocks, tok_pieces = gather_wide(
+        joined[:tiled_rows], joined[tiled_rows:].reshape(-1, 128),
+        jnp.concatenate([cache_keys, cache_values], axis=0), tokens_in, *dims, n_narrow)
     whole = jnp.concatenate([tok_pieces[q] for q in range(n_narrow)], axis=1)
-    all_weights = gathered.reshape(-1, joined_width)
-    qkv = all_weights[:, : sum(sizes[:3])]
-    out_rows = all_weights[:, sum(sizes[:3]) :]
+    weights_a = part_a.reshape(-1, joined_width)
+    weights_b = part_b.reshape(-1, block_rows - tiled_rows, joined_width).reshape(-1, joined_width)
+
+    def split_rows(act):
+        grouped = act.reshape(act.shape[0], -1, block_rows)
+        return (grouped[:, :, :tiled_rows].reshape(act.shape[0], -1),
+                grouped[:, :, tiled_rows:].reshape(act.shape[0], -1))
+
+    def project(act, lo, hi):
+        act_a, act_b = split_rows(act)
+        return (jnp.dot(act_a, weights_a[:, lo:hi], preferred_element_type=jnp.float32)
+                + jnp.dot(act_b, weights_b[:, lo:hi], preferred_element_type=jnp.float32))
 
     normed = rms_normed(whole, norm_gain)
     tok_rows = whole.shape[0]
@@ -352,10 +369,10 @@
     local_heads = query_width // HEAD_DIM
     local_groups = kv_width // HEAD_DIM
     repeats = local_heads // local_groups
-    qkv_sum = jnp.dot(normed, qkv, preferred_element_type=jnp.float32)
-    query_sum = qkv_sum[:, :query_width]
-    key_sum = qkv_sum[:, query_width : query_width + kv_width]
-    value_sum = qkv_sum[:, query_width + kv_width :]
+    query_sum = project(normed, 0, q_cols)
+    kv_sum = project(normed, 2 * q_cols, 2 * q_cols + 2 * kv_cols)
+    key_sum = kv_sum[:, :kv_width]
+    value_sum = kv_sum[:, kv_width:]
     length = cached_len[request]
     offset = append_slot[request]
     owner = shard_owner[request]
@@ -411,7 +428,7 @@
     attended = (accum / total[..., None]).astype(jnp.bfloat16).reshape(tok_rows, query_width)
     head_pieces = exchange(attended, "narrow", n_narrow, lambda d, k: (d - k) % n_narrow)
     all_heads = in_member_order(head_pieces, me_narrow, lambda me, q: (me - q) % n_narrow, 1)
-    update = jnp.dot(all_heads, out_rows, preferred_element_type=jnp.float32).astype(jnp.bfloat16)
+    update = project(all_heads, q_cols, 2 * q_cols).astype(jnp.bfloat16)
 
     first = ((place - owner) % GROUP * shard_rows - offset) % WIN
     keys_ext = jnp.concatenate(

time: 173 us -> 182 us (1.052)
  local copies, waits for them, and re-layouts: 23.7 us -> 33 us
  matrix products: 33.3 us -> 26.1 us
  other arithmetic: 17.3 us -> 21.1 us
  Pallas kernels: 67.7 us -> 70.5 us
    reshape x2 -> x1, local copies, waits for them, and re-layouts: 16.1 us -> 0.69 us  [shards(): joined[tiled_rows:].reshape(-1, 128)]
    dot_general x9, matrix products: 12 us -> 4.76 us  [step(): jnp.einsum('tgrd,gdk->tgrk', queries, block_keys, preferred_element_type=...]
    while x8 -> x40, local copies, waits for them, and re-layouts: 0.02 us -> 5.74 us
    dynamic_slice x8, local copies, waits for them, and re-layouts: 0.62 us -> 6.01 us  [step(): block_pos = lax.dynamic_slice_in_dim(key_pos, start, block, 0)]
    dynamic_slice x8, local copies, waits for them, and re-layouts: 0.62 us -> 5.82 us  [step(): block_ok = lax.dynamic_slice_in_dim(key_ok, start, block, 0)]
    another operation x2 -> x3, local copies, waits for them, and re-layouts: 0.01 us -> 3.5 us  [the longest x1 3.49 us: shards(): part_b.reshape(-1, block_rows - tiled_rows, joined_width)]
    pallas_call x1, Pallas kernels: 67.7 us -> 70.5 us  [gather_wide(): pl.pallas_call(functools.partial(gather_kernel, nz, nx, nc, nn), out_shap...]
    convert_element_type x1, other arithmetic: 0.01 us -> 2.24 us  [rms_normed(): return (values * scaling * gain.astype(jnp.float32)).astype(jnp.bfloat16)]
  transfers between devices with their start and end apart: 6 -> 6, of which waited for: 2 -> 2; matrix products, arithmetic and copies ran while one was open for 24% -> 28% of each run, Pallas kernels for 0% -> 0%
where the time goes in v7:
time: 182 us; the launch traced here: 181 us
  Pallas kernels  70.5 us (39%)
  local copies, waits for them, and re-layouts  33 us (18%)
  matrix products  26.1 us (14%)
  other arithmetic  21.1 us (12%)
  starting transfers between devices  20.2 us (11%)
  waiting for transfers between devices  6.03 us (3%)
  between operations  3.31 us (2%)
    pallas_call x1, Pallas kernels, gather_wide(): pl.pallas_call(functools.partial(gather_kernel, nz, nx, nc, nn), out_shap...  70.5 us
    dot_general x9, matrix products, step(): jnp.einsum('tgrk,gdk->tgrd', weights.astype(jnp.bfloat16), block_values,...  12.2 us
    ppermute x3, starting transfers between devices, group_route_pieces(): pieces.append(lax.ppermute(block, WIDE, route))  12.2 us
    ppermute x3, starting transfers between devices, exchange(): lax.ppermute(block, axis, [(pairing(d, k), d) for d in range(count)])  7.96 us
    dot_general x3, matrix products, project(): jnp.dot(act_a, weights_a[:, lo:hi], preferred_element_type=jnp.float32)  6.8 us
    ppermute x3, waiting for transfers between devices, exchange(): lax.ppermute(block, axis, [(pairing(d, k), d) for d in range(count)])  6.02 us
    dynamic_slice x8, local copies, waits for them, and re-layouts, step(): block_pos = lax.dynamic_slice_in_dim(key_pos, start, block, 0)  6.01 us
    dynamic_slice x8, local copies, waits for them, and re-layouts, step(): block_ok = lax.dynamic_slice_in_dim(key_ok, start, block, 0)  5.82 us
  transfers between devices with their start and end apart: 6, of which 2 were waited for; matrix products, arithmetic and copies ran while one was open for 28% of the time, Pallas kernels for 0%

profile of v7, /device:TPU:1, one launch (start us, length us, event | category | flops | bytes accessed | tf_op | source)
XLA Modules:
  0.0 180.8 jit_solution(15487524251326197544)
XLA Ops:
  3.7 2.0 %pad_maximum_fusion.1.cache_ref = bf16[320,1024]{1,0:T(8,128)(2,1)} fusion(bf16[160,1024]{1,0:T(8,128)(2,1)} %param.20, bf16[160,1024]{1,0:T(8,128)(2,1)} %param.19), kind=kLoop, calls=%fused_computation.63 | loop fusion | flops 1310720 | bytes 1310720 | tf_op jit(solution)/shard_map/concatenate | solution.py:350
  5.6 70.5 %shard_map.130 = (bf16[128,16,1600]{2,1,0:T(8,128)(2,1)}, bf16[128,50,128]{2,1,0:T(8,128)(2,1)}, bf16[4,320,1024]{2,1,0:T(8,128)(2,1)}, bf16[4,128,640]{2,1,0:T(8,128)(2,1)}) custom-call(bf16[16,1600]{1,0:T(8,128)(2,1)} %slice.123.blk_a, bf16[50,128]{1,0:T(8,128)(2,1)} %reshape.283.blk_b, bf16[320,1024]{1,0:T(8,128)(2,1)} %pad_maximum_fusion.1.cache_ref, ...), custom_call_target="tpu_custom_call" | custom-call | bytes 16384000 | tf_op jit(solution)/shard_map/pallas_call | solution.py:174
  76.2 1.3 slice_bitcast_fusion.9
  78.5 2.2 %multiply_convert_fusion = bf16[128,128,20]{0,2,1:T(8,128)(2,1)S(1)} fusion(bf16[128,32,20]{0,2,1:T(8,128)(2,1)S(1)} %concatenate.66, bf16[128,32,20]{0,2,1:T(8,128)(2,1)S(1)} %concatenate.65, bf16[128,32,20]{0,2,1:T(8,128)(2,1)S(1)} %concatenate.64, bf16[128,32,20]{0,2,1:T(8,128)(2,1)S(1)} %concatenate.63, f32[128,20]{1,0:T(8,128)S(1)} %reshape.296, ...), kind=kLoop, calls=%fused_computation.48 | loop fusion | flops 2293760 | bytes 1321472 | tf_op jit(solution)/shard_map/convert_element_type | solution.py:213
  80.8 3.5 %reshape_reshape.3 = bf16[512,1600]{1,0:T(8,128)(2,1)S(1)} reshape(bf16[128,50,128]{2,1,0:T(8,128)(2,1)} %get-tuple-element.211) | data formatting | bytes 3276800 | tf_op jit(solution)/shard_map/reshape;reshape | solution.py:353
  84.4 2.1 %fusion.32 = f32[128,320]{0,1:T(8,128)S(1)} fusion(bf16[128,2048]{0,1:T(8,128)(2,1)S(1)} %bitcast.166, bf16[2048,1600]{1,0:T(8,128)(2,1)} %bitcast.162), kind=kOutput, calls=%fused_computation.46 | convolution fusion | flops 167772160 | bytes 2260992 | tf_op jit(solution)/shard_map/dot_general | solution.py:362
  89.6 1.9 %collective-permute-start.1 = (bf16[128,320]{0,1:T(8,128)(2,1)}, bf16[128,320]{0,1:T(8,128)(2,1)}, u32[]{:S(2)}, u32[]{:S(2)}) collective-permute-start(bf16[128,320]{0,1:T(8,128)(2,1)} %get-tuple-element.308), channel_id=1, source_target_pairs={{0,8},{4,12},{8,0},{12,4},{16,24},{20,28},{24,16},{28,20},{32,40},... | collective-permute-start | bytes 245768 | tf_op jit(solution)/shard_map/ppermute | solution.py:339
  91.5 6.6 %collective-permute-start = (bf16[128,320]{0,1:T(8,128)(2,1)}, bf16[128,320]{0,1:T(8,128)(2,1)}, u32[]{:S(2)}, u32[]{:S(2)}) collective-permute-start(bf16[128,320]{0,1:T(8,128)(2,1)} %get-tuple-element.308), channel_id=1, source_target_pairs={{0,4},{4,0},{8,12},{12,8},{16,20},{20,16},{24,28},{28,24},{32,36},... | collective-permute-start | bytes 245768 | tf_op jit(solution)/shard_map/ppermute | solution.py:339
  98.1 3.7 %collective-permute-start.2 = (bf16[128,320]{0,1:T(8,128)(2,1)}, bf16[128,320]{0,1:T(8,128)(2,1)}, u32[]{:S(2)}, u32[]{:S(2)}) collective-permute-start(bf16[128,320]{0,1:T(8,128)(2,1)} %get-tuple-element.308), channel_id=1, source_target_pairs={{0,12},{4,8},{8,4},{12,0},{16,28},{20,24},{24,20},{28,16},{32,44},... | collective-permute-start | bytes 245768 | tf_op jit(solution)/shard_map/ppermute | solution.py:339
  104.5 1.2 iota_add_fusion.1
  105.7 2.5 %broadcast_compare_fusion = pred[4096]{0:T(1024)(128)(4,1)} fusion(s32[]{:T(128)} %bitcast.2, s32[]{:T(128)} %bitcast.1, s32[]{:T(128)} %bitcast), kind=kLoop, calls=%fused_computation.126 | loop fusion | flops 163840 | bytes 4108 | tf_op jit(solution)/shard_map/lt | solution.py:410
  108.3 2.5 %add_select_fusion = s32[4096]{0:T(1024)} fusion(s32[]{:T(128)} %bitcast.2, s32[]{:T(128)} %bitcast.1, s32[]{:T(128)} %bitcast), kind=kLoop, calls=%fused_computation.103 | loop fusion | flops 159744 | bytes 16396 | tf_op jit(solution)/shard_map/jit(remainder)/select_n | solution.py:402
  110.8 2.3 %fusion.25 = f32[128,640]{1,0:T(8,128)S(1)} fusion(bf16[128,2048]{0,1:T(8,128)(2,1)S(1)} %bitcast.167, bf16[2048,1600]{1,0:T(8,128)(2,1)} %bitcast.163), kind=kOutput, calls=%fused_computation.32 | convolution fusion | flops 335544320 | bytes 3473408 | tf_op jit(solution)/shard_map/dot_general | solution.py:362
  113.2 1.9 %slice_bitcast_fusion.3 = (bf16[320,1024]{1,0:T(8,128)(2,1)S(1)}, bf16[320,1024]{1,0:T(8,128)(2,1)S(1)}, bf16[320,1024]{1,0:T(8,128)(2,1)S(1)}, bf16[320,1024]{1,0:T(8,128)(2,1)S(1)}) fusion(bf16[4,320,1024]{2,1,0:T(8,128)(2,1)} %get-tuple-element.208), kind=kLoop, calls=%fused_computation.68 | loop fusion | bytes 5242880 | tf_op jit(solution)/shard_map/squeeze | solution.py:392
  115.4 1.3 fusion.78
  117.6 1.1 copy.25
  118.9 39.5 %while.5 = (s32[]{:T(128)}, f32[128,2,4,80]{0,3,2,1:T(8,128)}, f32[128,2,4]{0,2,1:T(4,128)S(1)}, f32[128,2,4]{0,2,1:T(4,128)S(1)}, pred[4096]{0:T(1024)(128)(4,1...) while((s32[]{:T(128)}, f32[128,2,4,80]{0,3,2,1:T(8,128)}, ...), condition=%wide.region_4.5_spmd.clone, body=%wide.region_1.4_spmd.clone.sunk | while | flops 174118016 | bytes 10396435 | solution.py:280
  121.7 1.5 fusion.103
  126.6 1.5 fusion.103
  131.5 1.5 fusion.103
  136.4 1.5 fusion.103
  141.3 1.5 fusion.103
  146.2 1.5 fusion.103
  151.2 1.5 fusion.103
  156.2 1.5 fusion.103
  161.4 3.0 %collective-permute-start.5 = (bf16[128,640]{0,1:T(8,128)(2,1)S(1)}, bf16[128,640]{0,1:T(8,128)(2,1)S(1)}, u32[]{:S(2)}, u32[]{:S(2)}) collective-permute-start(bf16[128,640]{0,1:T(8,128)(2,1)S(1)} %bitcast.181), channel_id=1, source_target_pairs={{1,0},{2,1},{3,2},{0,3},{5,4},{6,5},{7,6},{4,7},{9,8},{10,9},{11,1... | collective-permute-start | bytes 491528 | tf_op jit(solution)/shard_map/ppermute | solution.py:288
  164.5 3.0 %collective-permute-start.4 = (bf16[128,640]{0,1:T(8,128)(2,1)S(1)}, bf16[128,640]{0,1:T(8,128)(2,1)S(1)}, u32[]{:S(2)}, u32[]{:S(2)}) collective-permute-start(bf16[128,640]{0,1:T(8,128)(2,1)S(1)} %bitcast.182), channel_id=1, source_target_pairs={{2,0},{3,1},{0,2},{1,3},{6,4},{7,5},{4,6},{5,7},{10,8},{11,9},{8,1... | collective-permute-start | bytes 491528 | tf_op jit(solution)/shard_map/ppermute | solution.py:288
  167.4 2.0 %collective-permute-start.3 = (bf16[128,640]{0,1:T(8,128)(2,1)S(1)}, bf16[128,640]{0,1:T(8,128)(2,1)S(1)}, u32[]{:S(2)}, u32[]{:S(2)}) collective-permute-start(bf16[128,640]{0,1:T(8,128)(2,1)S(1)} %bitcast.183), channel_id=1, source_target_pairs={{3,0},{0,1},{1,2},{2,3},{7,4},{4,5},{5,6},{6,7},{11,8},{8,9},{9,10... | collective-permute-start | bytes 491528 | tf_op jit(solution)/shard_map/ppermute | solution.py:288
  169.4 1.4 fusion.48
  170.8 2.0 %collective-permute-done.4 = bf16[128,640]{0,1:T(8,128)(2,1)S(1)} collective-permute-done((bf16[128,640]{0,1:T(8,128)(2,1)S(1)}, bf16[128,640]{0,1:T(8,128)(2,1)S(1)}, u32[]{:S(2)}, u32[]{:S(2)}) %collective-permute-start.4) | collective-permute-done | bytes 163872 | tf_op jit(solution)/shard_map/ppermute | solution.py:288
  172.8 4.0 %collective-permute-done.3 = bf16[128,640]{0,1:T(8,128)(2,1)S(1)} collective-permute-done((bf16[128,640]{0,1:T(8,128)(2,1)S(1)}, bf16[128,640]{0,1:T(8,128)(2,1)S(1)}, u32[]{:S(2)}, u32[]{:S(2)}) %collective-permute-start.3) | collective-permute-done | bytes 163872 | tf_op jit(solution)/shard_map/ppermute | solution.py:288
  177.4 2.3 %fusion.23 = f32[128,640]{1,0:T(8,128)S(1)} fusion(bf16[128,2048]{0,1:T(8,128)(2,1)S(1)} %bitcast.168, bf16[2048,1600]{1,0:T(8,128)(2,1)} %bitcast.164), kind=kOutput, calls=%fused_computation.30 | convolution fusion | flops 335544320 | bytes 3473408 | tf_op jit(solution)/shard_map/dot_general | solution.py:362
  (189 shorter events, 40.7 us)
Async XLA Ops:
  84.3 2.5 %copy-start.5 = (s32[32]{0:T(128)S(1)}, s32[32]{0:T(128)}, u32[]{:S(2)}) copy-start(s32[32]{0:T(128)} %param.21) | copy-start | bytes 388
  84.4 17.5 %copy-start.6 = (s32[32]{0:T(128)S(1)}, s32[32]{0:T(128)}, u32[]{:S(2)}) copy-start(s32[32]{0:T(128)} %param.23) | copy-start | bytes 388
  84.4 18.8 %copy-start.7 = (s32[32]{0:T(128)S(1)}, s32[32]{0:T(128)}, u32[]{:S(2)}) copy-start(s32[32]{0:T(128)} %param.22) | copy-start | bytes 388
  89.6 69.1 %collective-permute-start.1 = (bf16[128,320]{0,1:T(8,128)(2,1)}, bf16[128,320]{0,1:T(8,128)(2,1)}, u32[]{:S(2)}, u32[]{:S(2)}) collective-permute-start(bf16[128,320]{0,1:T(8,128)(2,1)} %get-tuple-element.308), channel_id=1, source_target_pairs={{0,8},{4,12},{8,0},{12,4},{16,24},{20,28},{24,16},{28,20},{32,40},... | collective-permute-start | bytes 245768 | tf_op jit(solution)/shard_map/ppermute | solution.py:339
  91.5 67.2 %collective-permute-start = (bf16[128,320]{0,1:T(8,128)(2,1)}, bf16[128,320]{0,1:T(8,128)(2,1)}, u32[]{:S(2)}, u32[]{:S(2)}) collective-permute-start(bf16[128,320]{0,1:T(8,128)(2,1)} %get-tuple-element.308), channel_id=1, source_target_pairs={{0,4},{4,0},{8,12},{12,8},{16,20},{20,16},{24,28},{28,24},{32,36},... | collective-permute-start | bytes 245768 | tf_op jit(solution)/shard_map/ppermute | solution.py:339
  98.1 60.6 %collective-permute-start.2 = (bf16[128,320]{0,1:T(8,128)(2,1)}, bf16[128,320]{0,1:T(8,128)(2,1)}, u32[]{:S(2)}, u32[]{:S(2)}) collective-permute-start(bf16[128,320]{0,1:T(8,128)(2,1)} %get-tuple-element.308), channel_id=1, source_target_pairs={{0,12},{4,8},{8,4},{12,0},{16,28},{20,24},{24,20},{28,16},{32,44},... | collective-permute-start | bytes 245768 | tf_op jit(solution)/shard_map/ppermute | solution.py:339
  118.9 39.5 %copy-start.3 = (s32[512]{0:T(512)S(1)}, s32[512]{0:T(512)}, u32[]{:S(2)}) copy-start(s32[512]{0:T(512)} %iota_add_fusion.1) | copy-start | bytes 6148
  118.9 39.5 %copy-start.4 = (s32[128]{0:T(128)S(1)}, s32[128]{0:T(128)}, u32[]{:S(2)}) copy-start(s32[128]{0:T(128)} %get-tuple-element.315) | copy-start | bytes 1540
  118.9 39.8 %copy-start.2 = (bf16[1,128,320]{1,2,0:T(8,128)(2,1)S(1)}, bf16[1,128,320]{1,2,0:T(8,128)(2,1)}, u32[]{:S(2)}) copy-start(bf16[1,128,320]{1,2,0:T(8,128)(2,1)} %get-tuple-element.307) | copy-start | bytes 245764
  120.6 1.0 copy-start.8
  123.1 0.7 copy-start.9
  125.5 1.0 copy-start.8
  128.0 0.7 copy-start.9
  130.4 1.0 copy-start.8
  132.9 0.7 copy-start.9
  135.3 1.0 copy-start.8
  137.8 0.7 copy-start.9
  140.3 1.0 copy-start.8
  142.8 0.7 copy-start.9
  145.2 1.0 copy-start.8
  147.7 0.7 copy-start.9
  150.2 1.0 copy-start.8
  152.7 0.7 copy-start.9
  155.1 1.0 copy-start.8
  157.6 0.7 copy-start.9
  159.9 1.0 copy-start.10
  160.9 8.5 %copy-start = (bf16[160,1024]{1,0:T(8,128)(2,1)S(1)}, bf16[160,1024]{1,0:T(8,128)(2,1)}, u32[]{:S(2)}) copy-start(bf16[160,1024]{1,0:T(8,128)(2,1)} %param.20) | copy-start | bytes 983044
  160.9 8.5 %copy-start.1 = (bf16[160,1024]{1,0:T(8,128)(2,1)S(1)}, bf16[160,1024]{1,0:T(8,128)(2,1)}, u32[]{:S(2)}) copy-start(bf16[160,1024]{1,0:T(8,128)(2,1)} %param.19) | copy-start | bytes 983044
  161.4 9.4 %collective-permute-start.5 = (bf16[128,640]{0,1:T(8,128)(2,1)S(1)}, bf16[128,640]{0,1:T(8,128)(2,1)S(1)}, u32[]{:S(2)}, u32[]{:S(2)}) collective-permute-start(bf16[128,640]{0,1:T(8,128)(2,1)S(1)} %bitcast.181), channel_id=1, source_target_pairs={{1,0},{2,1},{3,2},{0,3},{5,4},{6,5},{7,6},{4,7},{9,8},{10,9},{11,1... | collective-permute-start | bytes 491528 | tf_op jit(solution)/shard_map/ppermute | solution.py:288
  164.5 8.3 %collective-permute-start.4 = (bf16[128,640]{0,1:T(8,128)(2,1)S(1)}, bf16[128,640]{0,1:T(8,128)(2,1)S(1)}, u32[]{:S(2)}, u32[]{:S(2)}) collective-permute-start(bf16[128,640]{0,1:T(8,128)(2,1)S(1)} %bitcast.182), channel_id=1, source_target_pairs={{2,0},{3,1},{0,2},{1,3},{6,4},{7,5},{4,6},{5,7},{10,8},{11,9},{8,1... | collective-permute-start | bytes 491528 | tf_op jit(solution)/shard_map/ppermute | solution.py:288
  167.4 9.4 %collective-permute-start.3 = (bf16[128,640]{0,1:T(8,128)(2,1)S(1)}, bf16[128,640]{0,1:T(8,128)(2,1)S(1)}, u32[]{:S(2)}, u32[]{:S(2)}) collective-permute-start(bf16[128,640]{0,1:T(8,128)(2,1)S(1)} %bitcast.183), channel_id=1, source_target_pairs={{3,0},{0,1},{1,2},{2,3},{7,4},{4,5},{5,6},{6,7},{11,8},{8,9},{9,10... | collective-permute-start | bytes 491528 | tf_op jit(solution)/shard_map/ppermute | solution.py:288

commit v8 on v5

--- a/solution.py
+++ b/solution.py
@@ -391,7 +391,7 @@
         old_values,
         cached_pos,
         cached_pos < length,
-        512,
+        256,
     )
     key_cols = new_keys.T
     value_cols = new_values.T
@@ -405,7 +405,7 @@
         value_cols,
         new_pos,
         jnp.ones((new_count,), dtype=bool),
-        512,
+        256,
     )
     accum, top_score, total = state
     attended = (accum / total[..., None]).astype(jnp.bfloat16).reshape(tok_rows, query_width)

time: 173 us -> 199 us (1.15)
  local copies, waits for them, and re-layouts: 23.7 us -> 45.8 us
  matrix products: 33.3 us -> 35.6 us
    dynamic_slice x8 -> x18, local copies, waits for them, and re-layouts: 0.62 us -> 12.4 us  [step(): block_pos = lax.dynamic_slice_in_dim(key_pos, start, block, 0)]
    dynamic_slice x8 -> x16, local copies, waits for them, and re-layouts: 0.62 us -> 11.4 us  [step(): block_ok = lax.dynamic_slice_in_dim(key_ok, start, block, 0)]
    dot_general x9 -> x18, matrix products: 12 us -> 20.8 us  [step(): jnp.einsum('tgrd,gdk->tgrk', queries, block_keys, preferred_element_type=...]
    dot_general x9 -> x18, matrix products: 12.2 us -> 5.74 us  [step(): jnp.einsum('tgrk,gdk->tgrd', weights.astype(jnp.bfloat16), block_values,...]
    reduce_sum x9 -> x18, other arithmetic: 4 us -> 3.59 us  [step(): sum_new = sum_old * rescale + jnp.sum(weights, axis=-1)]
  transfers between devices with their start and end apart: 6 -> 6, of which waited for: 2 -> 2; matrix products, arithmetic and copies ran while one was open for 24% -> 33% of each run, Pallas kernels for 0% -> 0%
where the time goes in v8:
time: 199 us; the launch traced here: 197 us
  Pallas kernels  67.7 us (34%)
  local copies, waits for them, and re-layouts  45.8 us (23%)
  matrix products  35.6 us (18%)
  starting transfers between devices  19.5 us (10%)
  other arithmetic  17.9 us (9%)
  waiting for transfers between devices  6.03 us (3%)
  between operations  3.1 us (2%)
    pallas_call x1, Pallas kernels, gather_wide(): pl.pallas_call(functools.partial(gather_kernel, nz, nx, nc, nn), out_shap...  67.7 us
    dot_general x18, matrix products, step(): jnp.einsum('tgrd,gdk->tgrk', queries, block_keys, preferred_element_type=...  20.8 us
    reshape x1, local copies, waits for them, and re-layouts, shards(): all_weights = gathered.reshape(-1, joined_width)  15.3 us
    dynamic_slice x18, local copies, waits for them, and re-layouts, step(): block_pos = lax.dynamic_slice_in_dim(key_pos, start, block, 0)  12.4 us
    ppermute x3, starting transfers between devices, group_route_pieces(): pieces.append(lax.ppermute(block, WIDE, route))  11.5 us
    dynamic_slice x16, local copies, waits for them, and re-layouts, step(): block_ok = lax.dynamic_slice_in_dim(key_ok, start, block, 0)  11.4 us
    ppermute x3, starting transfers between devices, exchange(): lax.ppermute(block, axis, [(pairing(d, k), d) for d in range(count)])  7.99 us
    ppermute x3, waiting for transfers between devices, exchange(): lax.ppermute(block, axis, [(pairing(d, k), d) for d in range(count)])  6.02 us
  transfers between devices with their start and end apart: 6, of which 2 were waited for; matrix products, arithmetic and copies ran while one was open for 33% of the time, Pallas kernels for 0%

profile of v8, /device:TPU:1, one launch (start us, length us, event | category | flops | bytes accessed | tf_op | source)
XLA Modules:
  0.0 196.9 jit_solution(9701369134720427046)
XLA Ops:
  2.3 2.0 %pad_maximum_fusion.1.cache_ref = bf16[320,1024]{1,0:T(8,128)(2,1)} fusion(bf16[160,1024]{1,0:T(8,128)(2,1)} %param.22, bf16[160,1024]{1,0:T(8,128)(2,1)} %param.21), kind=kLoop, calls=%fused_computation.66 | loop fusion | flops 1310720 | bytes 1310720 | tf_op jit(solution)/shard_map/concatenate | solution.py:341
  4.3 67.7 %shard_map.130 = (bf16[128,250,128]{2,1,0:T(8,128)(2,1)}, bf16[4,320,1024]{2,1,0:T(8,128)(2,1)}, bf16[4,128,640]{2,1,0:T(8,128)(2,1)}) custom-call(bf16[250,128]{1,0:T(8,128)(2,1)} %reshape.229.blk_ref, bf16[320,1024]{1,0:T(8,128)(2,1)} %pad_maximum_fusion.1.cache_ref, bf16[128,640]{1,0:T(8,128)(2,1)} %tok_ref.1), custom_call_target="tpu_custom_call" | custom-call | bytes 16384000 | tf_op jit(solution)/shard_map/pallas_call | solution.py:168
  72.1 15.3 %reshape.231 = bf16[2560,1600]{1,0:T(8,128)(2,1)} reshape(bf16[128,250,128]{2,1,0:T(8,128)(2,1)} %get-tuple-element.334) | data formatting | bytes 16384000 | tf_op jit(solution)/shard_map/reshape | solution.py:344
  87.7 4.8 %fusion.37 = f32[128,960]{0,1:T(8,128)S(1)} fusion(bf16[2560,1600]{1,0:T(8,128)(2,1)} %reshape.231, f32[2560]{0:T(1024)S(1)} %convert_element_type.46, f32[128]{0:T(128)S(1)} %add_rsqrt_fusion, bf16[128,640]{1,0:T(8,128)(2,1)S(1)} %get-tuple-element.454, bf16[128,640]{1,0:T(8,128)(2,1)S(1)} %get-tuple-element.455, ...), kind=kOutput, calls=%fused_computation.51 | convolution fusion | flops 632750080 | bytes 6400512 | tf_op jit(solution)/shard_map/dot_general | solution.py:355
  95.2 6.0 %collective-permute-start.2 = (bf16[128,320]{0,1:T(8,128)(2,1)}, bf16[128,320]{0,1:T(8,128)(2,1)}, u32[]{:S(2)}, u32[]{:S(2)}) collective-permute-start(bf16[128,320]{0,1:T(8,128)(2,1)} %get-tuple-element.470), channel_id=1, source_target_pairs={{0,12},{4,8},{8,4},{12,0},{16,28},{20,24},{24,20},{28,16},{32,44},... | collective-permute-start | bytes 245768 | tf_op jit(solution)/shard_map/ppermute | solution.py:332
  101.2 3.6 %collective-permute-start.1 = (bf16[128,320]{0,1:T(8,128)(2,1)}, bf16[128,320]{0,1:T(8,128)(2,1)}, u32[]{:S(2)}, u32[]{:S(2)}) collective-permute-start(bf16[128,320]{0,1:T(8,128)(2,1)} %get-tuple-element.470), channel_id=1, source_target_pairs={{0,8},{4,12},{8,0},{12,4},{16,24},{20,28},{24,16},{28,20},{32,40},... | collective-permute-start | bytes 245768 | tf_op jit(solution)/shard_map/ppermute | solution.py:332
  104.8 1.9 collective-permute-start
  107.4 1.3 dynamic_slice.88
  108.6 2.4 %broadcast_compare_fusion = pred[4096]{0:T(1024)(128)(4,1)} fusion(s32[]{:T(128)} %bitcast.2, s32[]{:T(128)} %bitcast.1, s32[]{:T(128)} %bitcast), kind=kLoop, calls=%fused_computation.141 | loop fusion | flops 163840 | bytes 4108 | tf_op jit(solution)/shard_map/lt | solution.py:393
  111.1 2.4 %add_select_fusion = s32[4096]{0:T(1024)} fusion(s32[]{:T(128)} %bitcast.2, s32[]{:T(128)} %bitcast.1, s32[]{:T(128)} %bitcast), kind=kLoop, calls=%fused_computation.122 | loop fusion | flops 159744 | bytes 16396 | tf_op jit(solution)/shard_map/jit(remainder)/select_n | solution.py:385
  116.0 1.3 fusion.87
  117.4 55.9 %while.37 = (s32[]{:T(128)}, f32[128,2,4,80]{0,3,2,1:T(8,128)S(1)}, f32[128,2,4]{0,2,1:T(4,128)S(1)}, f32[128,2,4]{0,2,1:T(4,128)S(1)}, pred[4096]{0:T(1024)(128...) while((s32[]{:T(128)}, f32[128,2,4,80]{0,3,2,1:T(8,128)S(1)}, ...), condition=%wide.region_4.5_spmd.clone, body=%wide.region_1.4_spmd.clone.sunk | while | flops 86660224 | bytes 4330459 | solution.py:273
  119.0 1.3 select_reduce_fusion.5
  122.5 1.3 select_reduce_fusion.5
  125.9 1.3 select_reduce_fusion.5
  129.4 1.3 select_reduce_fusion.5
  132.8 1.3 select_reduce_fusion.5
  136.3 1.3 select_reduce_fusion.5
  139.8 1.3 select_reduce_fusion.5
  143.3 1.3 select_reduce_fusion.5
  146.8 1.3 select_reduce_fusion.5
  153.8 1.3 select_reduce_fusion.5
  167.9 1.3 select_reduce_fusion.5
  171.4 1.3 select_reduce_fusion.5
  174.7 2.4 %while.36 = (s32[]{:T(128)}, f32[128,2,4,80]{0,3,2,1:T(8,128)S(1)}, f32[128,2,4]{0,2,1:T(4,128)S(1)}, f32[128,2,4]{0,2,1:T(4,128)S(1)}, s32[512]{0:T(512)S(1)}, ...) while((s32[]{:T(128)}, f32[128,2,4,80]{0,3,2,1:T(8,128)S(1)}, ...), condition=%wide.region_8.9_spmd.clone, body=%wide.region_5.8_spmd.clone.sunk | while | flops 86542464 | bytes 4329667 | solution.py:273
  177.1 3.1 %collective-permute-start.5 = (bf16[128,640]{0,1:T(8,128)(2,1)S(1)}, bf16[128,640]{0,1:T(8,128)(2,1)S(1)}, u32[]{:S(2)}, u32[]{:S(2)}) collective-permute-start(bf16[128,640]{0,1:T(8,128)(2,1)S(1)} %bitcast.139), channel_id=1, source_target_pairs={{1,0},{2,1},{3,2},{0,3},{5,4},{6,5},{7,6},{4,7},{9,8},{10,9},{11,1... | collective-permute-start | bytes 491528 | tf_op jit(solution)/shard_map/ppermute | solution.py:281
  180.2 2.9 %collective-permute-start.4 = (bf16[128,640]{0,1:T(8,128)(2,1)S(1)}, bf16[128,640]{0,1:T(8,128)(2,1)S(1)}, u32[]{:S(2)}, u32[]{:S(2)}) collective-permute-start(bf16[128,640]{0,1:T(8,128)(2,1)S(1)} %bitcast.140), channel_id=1, source_target_pairs={{2,0},{3,1},{0,2},{1,3},{6,4},{7,5},{4,6},{5,7},{10,8},{11,9},{8,1... | collective-permute-start | bytes 491528 | tf_op jit(solution)/shard_map/ppermute | solution.py:281
  183.1 2.0 %collective-permute-start.3 = (bf16[128,640]{0,1:T(8,128)(2,1)S(1)}, bf16[128,640]{0,1:T(8,128)(2,1)S(1)}, u32[]{:S(2)}, u32[]{:S(2)}) collective-permute-start(bf16[128,640]{0,1:T(8,128)(2,1)S(1)} %bitcast.141), channel_id=1, source_target_pairs={{3,0},{0,1},{1,2},{2,3},{7,4},{4,5},{5,6},{6,7},{11,8},{8,9},{9,10... | collective-permute-start | bytes 491528 | tf_op jit(solution)/shard_map/ppermute | solution.py:281
  185.1 1.4 fusion.60
  186.5 2.0 %collective-permute-done.4 = bf16[128,640]{0,1:T(8,128)(2,1)S(1)} collective-permute-done((bf16[128,640]{0,1:T(8,128)(2,1)S(1)}, bf16[128,640]{0,1:T(8,128)(2,1)S(1)}, u32[]{:S(2)}, u32[]{:S(2)}) %collective-permute-start.4) | collective-permute-done | bytes 163872 | tf_op jit(solution)/shard_map/ppermute | solution.py:281
  188.5 4.0 %collective-permute-done.3 = bf16[128,640]{0,1:T(8,128)(2,1)S(1)} collective-permute-done((bf16[128,640]{0,1:T(8,128)(2,1)S(1)}, bf16[128,640]{0,1:T(8,128)(2,1)S(1)}, u32[]{:S(2)}, u32[]{:S(2)}) %collective-permute-start.3) | collective-permute-done | bytes 163872 | tf_op jit(solution)/shard_map/ppermute | solution.py:281
  192.7 4.2 %fusion.44 = bf16[128,640]{1,0:T(8,128)(2,1)} fusion(bf16[2560,1600]{1,0:T(8,128)(2,1)} %reshape.231, bf16[128,640]{0,1:T(8,128)(2,1)S(1)} %get-tuple-element.450, bf16[128,640]{0,1:T(8,128)(2,1)S(1)} %get-tuple-element.451, bf16[128,640]{0,1:T(8,128)(2,1)S(1)} %get-tuple-element.452, bf16[128,640]{0,1:T(8,128)(2,1)S(1)} %get-tuple-element.449), kind=kOutput, calls=%fused_computation.65 | convolution fusion | flops 422133760 | bytes 4096000 | tf_op jit(solution)/shard_map/dot_general | solution.py:414
  (227 shorter events, 49.0 us)
Async XLA Ops:
  72.1 15.3 %copy-start.7 = (bf16[2560]{0:T(1024)(128)(2,1)S(1)}, bf16[2560]{0:T(1024)(128)(2,1)}, u32[]{:S(2)}) copy-start(bf16[2560]{0:T(1024)(128)(2,1)} %param.16) | copy-start | bytes 15364
  72.1 15.3 %copy-start.4 = (bf16[4,128,640]{2,1,0:T(8,128)(2,1)S(1)}, bf16[4,128,640]{2,1,0:T(8,128)(2,1)}, u32[]{:S(2)}) copy-start(bf16[4,128,640]{2,1,0:T(8,128)(2,1)} %get-tuple-element.333) | copy-start | bytes 1966084
  87.7 4.9 %copy-start.8 = (s32[32]{0:T(128)S(1)}, s32[32]{0:T(128)}, u32[]{:S(2)}) copy-start(s32[32]{0:T(128)} %param.23) | copy-start | bytes 388
  87.7 19.0 %copy-start.9 = (s32[32]{0:T(128)S(1)}, s32[32]{0:T(128)}, u32[]{:S(2)}) copy-start(s32[32]{0:T(128)} %param.24) | copy-start | bytes 388
  87.7 27.7 %copy-start = (bf16[4,320,1024]{2,1,0:T(8,128)(2,1)S(1)}, bf16[4,320,1024]{2,1,0:T(8,128)(2,1)}, u32[]{:S(2)}) copy-start(bf16[4,320,1024]{2,1,0:T(8,128)(2,1)} %get-tuple-element.332) | copy-start | bytes 7864324
  92.6 23.1 %copy-start.3 = (f32[128,960]{0,1:T(8,128)}, f32[128,960]{0,1:T(8,128)S(1)}, u32[]{:S(2)}) copy-start(f32[128,960]{0,1:T(8,128)S(1)} %fusion.37) | copy-start | bytes 1474564
  93.9 0.6 copy-start.5
  95.2 78.3 %collective-permute-start.2 = (bf16[128,320]{0,1:T(8,128)(2,1)}, bf16[128,320]{0,1:T(8,128)(2,1)}, u32[]{:S(2)}, u32[]{:S(2)}) collective-permute-start(bf16[128,320]{0,1:T(8,128)(2,1)} %get-tuple-element.470), channel_id=1, source_target_pairs={{0,12},{4,8},{8,4},{12,0},{16,28},{20,24},{24,20},{28,16},{32,44},... | collective-permute-start | bytes 245768 | tf_op jit(solution)/shard_map/ppermute | solution.py:332
  101.2 72.3 %collective-permute-start.1 = (bf16[128,320]{0,1:T(8,128)(2,1)}, bf16[128,320]{0,1:T(8,128)(2,1)}, u32[]{:S(2)}, u32[]{:S(2)}) collective-permute-start(bf16[128,320]{0,1:T(8,128)(2,1)} %get-tuple-element.470), channel_id=1, source_target_pairs={{0,8},{4,12},{8,0},{12,4},{16,24},{20,28},{24,16},{28,20},{32,40},... | collective-permute-start | bytes 245768 | tf_op jit(solution)/shard_map/ppermute | solution.py:332
  104.8 68.7 %collective-permute-start = (bf16[128,320]{0,1:T(8,128)(2,1)}, bf16[128,320]{0,1:T(8,128)(2,1)}, u32[]{:S(2)}, u32[]{:S(2)}) collective-permute-start(bf16[128,320]{0,1:T(8,128)(2,1)} %get-tuple-element.470), channel_id=1, source_target_pairs={{0,4},{4,0},{8,12},{12,8},{16,20},{20,16},{24,28},{28,24},{32,36},... | collective-permute-start | bytes 245768 | tf_op jit(solution)/shard_map/ppermute | solution.py:332
  116.0 1.3 slice-start
  116.0 1.3 copy-start.6
  174.7 10.4 %copy-start.1 = (bf16[160,1024]{1,0:T(8,128)(2,1)S(1)}, bf16[160,1024]{1,0:T(8,128)(2,1)}, u32[]{:S(2)}) copy-start(bf16[160,1024]{1,0:T(8,128)(2,1)} %param.22) | copy-start | bytes 983044
  174.7 10.4 %copy-start.2 = (bf16[160,1024]{1,0:T(8,128)(2,1)S(1)}, bf16[160,1024]{1,0:T(8,128)(2,1)}, u32[]{:S(2)}) copy-start(bf16[160,1024]{1,0:T(8,128)(2,1)} %param.21) | copy-start | bytes 983044
  177.1 9.4 %collective-permute-start.5 = (bf16[128,640]{0,1:T(8,128)(2,1)S(1)}, bf16[128,640]{0,1:T(8,128)(2,1)S(1)}, u32[]{:S(2)}, u32[]{:S(2)}) collective-permute-start(bf16[128,640]{0,1:T(8,128)(2,1)S(1)} %bitcast.139), channel_id=1, source_target_pairs={{1,0},{2,1},{3,2},{0,3},{5,4},{6,5},{7,6},{4,7},{9,8},{10,9},{11,1... | collective-permute-start | bytes 491528 | tf_op jit(solution)/shard_map/ppermute | solution.py:281
  180.2 8.3 %collective-permute-start.4 = (bf16[128,640]{0,1:T(8,128)(2,1)S(1)}, bf16[128,640]{0,1:T(8,128)(2,1)S(1)}, u32[]{:S(2)}, u32[]{:S(2)}) collective-permute-start(bf16[128,640]{0,1:T(8,128)(2,1)S(1)} %bitcast.140), channel_id=1, source_target_pairs={{2,0},{3,1},{0,2},{1,3},{6,4},{7,5},{4,6},{5,7},{10,8},{11,9},{8,1... | collective-permute-start | bytes 491528 | tf_op jit(solution)/shard_map/ppermute | solution.py:281
  183.1 9.4 %collective-permute-start.3 = (bf16[128,640]{0,1:T(8,128)(2,1)S(1)}, bf16[128,640]{0,1:T(8,128)(2,1)S(1)}, u32[]{:S(2)}, u32[]{:S(2)}) collective-permute-start(bf16[128,640]{0,1:T(8,128)(2,1)S(1)} %bitcast.141), channel_id=1, source_target_pairs={{3,0},{0,1},{1,2},{2,3},{7,4},{4,5},{5,6},{6,7},{11,8},{8,9},{9,10... | collective-permute-start | bytes 491528 | tf_op jit(solution)/shard_map/ppermute | solution.py:281

commit v9 on v7

--- a/solution.py
+++ b/solution.py
@@ -340,27 +340,26 @@
         return jnp.stack(pieces)
 
 
-    q_cols, kv_cols = query_weight.shape[1], key_weight.shape[1]
-    joined = jnp.concatenate([query_weight, out_weight, key_weight, value_weight], axis=1)
+    sizes = (query_weight.shape[1], key_weight.shape[1], value_weight.shape[1], out_weight.shape[1])
+    joined = jnp.concatenate([query_weight, key_weight, value_weight, out_weight], axis=1)
     block_rows, joined_width = joined.shape
+    dims = (lax.psum(1, "z"), lax.psum(1, "x"), lax.psum(1, "c"))
     tiled_rows = block_rows // 16 * 16
-    dims = (lax.psum(1, "z"), lax.psum(1, "x"), lax.psum(1, "c"))
     part_a, part_b, cache_blocks, tok_pieces = gather_wide(
         joined[:tiled_rows], joined[tiled_rows:].reshape(-1, 128),
         jnp.concatenate([cache_keys, cache_values], axis=0), tokens_in, *dims, n_narrow)
     whole = jnp.concatenate([tok_pieces[q] for q in range(n_narrow)], axis=1)
-    weights_a = part_a.reshape(-1, joined_width)
-    weights_b = part_b.reshape(-1, block_rows - tiled_rows, joined_width).reshape(-1, joined_width)
-
-    def split_rows(act):
+    part_b = part_b.reshape(-1, block_rows - tiled_rows, joined_width).reshape(-1, joined_width)
+    all_weights = jnp.concatenate([part_a.reshape(-1, joined_width), part_b], axis=0)
+
+    def rows_order(act):
         grouped = act.reshape(act.shape[0], -1, block_rows)
-        return (grouped[:, :, :tiled_rows].reshape(act.shape[0], -1),
-                grouped[:, :, tiled_rows:].reshape(act.shape[0], -1))
-
-    def project(act, lo, hi):
-        act_a, act_b = split_rows(act)
-        return (jnp.dot(act_a, weights_a[:, lo:hi], preferred_element_type=jnp.float32)
-                + jnp.dot(act_b, weights_b[:, lo:hi], preferred_element_type=jnp.float32))
+        return jnp.concatenate(
+            [grouped[:, :, :tiled_rows].reshape(act.shape[0], -1),
+             grouped[:, :, tiled_rows:].reshape(act.shape[0], -1)], axis=1)
+
+    qkv = all_weights[:, : sum(sizes[:3])]
+    out_rows = all_weights[:, sum(sizes[:3]) :]
 
     normed = rms_normed(whole, norm_gain)
     tok_rows = whole.shape[0]
@@ -369,10 +368,10 @@
     local_heads = query_width // HEAD_DIM
     local_groups = kv_width // HEAD_DIM
     repeats = local_heads // local_groups
-    query_sum = project(normed, 0, q_cols)
-    kv_sum = project(normed, 2 * q_cols, 2 * q_cols + 2 * kv_cols)
-    key_sum = kv_sum[:, :kv_width]
-    value_sum = kv_sum[:, kv_width:]
+    qkv_sum = jnp.dot(rows_order(normed), qkv, preferred_element_type=jnp.float32)
+    query_sum = qkv_sum[:, :query_width]
+    key_sum = qkv_sum[:, query_width : query_width + kv_width]
+    value_sum = qkv_sum[:, query_width + kv_width :]
     length = cached_len[request]
     offset = append_slot[request]
     owner = shard_owner[request]
@@ -428,7 +427,7 @@
     attended = (accum / total[..., None]).astype(jnp.bfloat16).reshape(tok_rows, query_width)
     head_pieces = exchange(attended, "narrow", n_narrow, lambda d, k: (d - k) % n_narrow)
     all_heads = in_member_order(head_pieces, me_narrow, lambda me, q: (me - q) % n_narrow, 1)
-    update = project(all_heads, q_cols, 2 * q_cols).astype(jnp.bfloat16)
+    update = jnp.dot(rows_order(all_heads), out_rows, preferred_element_type=jnp.float32).astype(jnp.bfloat16)
 
     first = ((place - owner) % GROUP * shard_rows - offset) % WIN
     keys_ext = jnp.concatenate(

time: 182 us -> 181 us (level)
    dot_general x6 -> x2, matrix products: 9.08 us -> 8.14 us  [the longest x1 4.08 us: shards(): jnp.dot(rows_order(normed), qkv, preferred_element_type=jnp.float32)]
  transfers between devices with their start and end apart: 6 -> 6, of which waited for: 2 -> 2; matrix products, arithmetic and copies ran while one was open for 28% -> 26% of each run, Pallas kernels for 0% -> 0%
where the time goes in v9:
time: 181 us; the launch traced here: 179 us
  Pallas kernels  70.5 us (39%)
  local copies, waits for them, and re-layouts  32.3 us (18%)
  matrix products  25.1 us (14%)
  other arithmetic  21.6 us (12%)
  starting transfers between devices  20.2 us (11%)
  waiting for transfers between devices  5.84 us (3%)
  between operations  3.19 us (2%)
    pallas_call x1, Pallas kernels, gather_wide(): pl.pallas_call(functools.partial(gather_kernel, nz, nx, nc, nn), out_shap...  70.5 us
    dot_general x9, matrix products, step(): jnp.einsum('tgrk,gdk->tgrd', weights.astype(jnp.bfloat16), block_values,...  12.2 us
    ppermute x3, starting transfers between devices, group_route_pieces(): pieces.append(lax.ppermute(block, WIDE, route))  12 us
    ppermute x3, starting transfers between devices, exchange(): lax.ppermute(block, axis, [(pairing(d, k), d) for d in range(count)])  8.15 us
    dynamic_slice x8, local copies, waits for them, and re-layouts, step(): block_pos = lax.dynamic_slice_in_dim(key_pos, start, block, 0)  6.01 us
    dynamic_slice x8, local copies, waits for them, and re-layouts, step(): block_ok = lax.dynamic_slice_in_dim(key_ok, start, block, 0)  5.91 us
    ppermute x3, waiting for transfers between devices, exchange(): lax.ppermute(block, axis, [(pairing(d, k), d) for d in range(count)])  5.83 us
    while x40, local copies, waits for them, and re-layouts  5.74 us
  transfers between devices with their start and end apart: 6, of which 2 were waited for; matrix products, arithmetic and copies ran while one was open for 26% of the time, Pallas kernels for 0%

profile of v9, /device:TPU:1, one launch (start us, length us, event | category | flops | bytes accessed | tf_op | source)
XLA Modules:
  0.0 179.3 jit_solution(2400153458283655542)
XLA Ops:
  2.2 1.4 reshape.293
  4.3 2.0 %pad_maximum_fusion.5.cache_ref = bf16[320,1024]{1,0:T(8,128)(2,1)} fusion(bf16[160,1024]{1,0:T(8,128)(2,1)} %param.20, bf16[160,1024]{1,0:T(8,128)(2,1)} %param.19), kind=kLoop, calls=%fused_computation.59 | loop fusion | flops 1310720 | bytes 1310720 | tf_op jit(solution)/shard_map/concatenate | solution.py:350
  6.3 70.5 %shard_map.130 = (bf16[128,16,1600]{2,1,0:T(8,128)(2,1)}, bf16[128,50,128]{2,1,0:T(8,128)(2,1)}, bf16[4,320,1024]{2,1,0:T(8,128)(2,1)}, bf16[4,128,640]{2,1,0:T(8,128)(2,1)}) custom-call(bf16[16,1600]{1,0:T(8,128)(2,1)} %slice.109.blk_a, bf16[50,128]{1,0:T(8,128)(2,1)} %reshape.280.blk_b, bf16[320,1024]{1,0:T(8,128)(2,1)} %pad_maximum_fusion.5.cache_ref, ...), custom_call_target="tpu_custom_call" | custom-call | bytes 16384000 | tf_op jit(solution)/shard_map/pallas_call | solution.py:174
  76.8 1.3 slice_bitcast_fusion.9
  79.2 3.1 %multiply_convert_fusion = bf16[128,128,20]{0,2,1:T(8,128)(2,1)S(1)} fusion(bf16[128,32,20]{0,2,1:T(8,128)(2,1)S(1)} %concatenate.75, bf16[128,32,20]{0,2,1:T(8,128)(2,1)S(1)} %concatenate.74, bf16[128,32,20]{0,2,1:T(8,128)(2,1)S(1)} %concatenate.73, bf16[128,32,20]{0,2,1:T(8,128)(2,1)S(1)} %concatenate.72, f32[128,20]{1,0:T(8,128)} %reshape.293, ...), kind=kLoop, calls=%fused_computation.49 | loop fusion | flops 2293760 | bytes 1321472 | tf_op jit(solution)/shard_map/convert_element_type | solution.py:213
  83.8 1.7 reshape_reshape.3
  85.6 4.1 %fusion.24 = f32[128,960]{0,1:T(8,128)S(1)} fusion(bf16[2048,1600]{1,0:T(8,128)(2,1)} %bitcast.156, bf16[512,1600]{1,0:T(8,128)(2,1)S(1)} %reshape_reshape.3, bf16[128,512]{0,1:T(8,128)(2,1)} %bitcast.181, bf16[128,2048]{0,1:T(8,128)(2,1)} %bitcast.169), kind=kOutput, calls=%fused_computation.33 | convolution fusion | flops 640286720 | bytes 9338880 | tf_op jit(solution)/shard_map/dot_general | solution.py:371
  92.4 1.9 %collective-permute-start.1 = (bf16[128,320]{0,1:T(8,128)(2,1)}, bf16[128,320]{0,1:T(8,128)(2,1)}, u32[]{:S(2)}, u32[]{:S(2)}) collective-permute-start(bf16[128,320]{0,1:T(8,128)(2,1)} %get-tuple-element.308), channel_id=1, source_target_pairs={{0,8},{4,12},{8,0},{12,4},{16,24},{20,28},{24,16},{28,20},{32,40},... | collective-permute-start | bytes 245768 | tf_op jit(solution)/shard_map/ppermute | solution.py:339
  94.3 6.6 %collective-permute-start = (bf16[128,320]{0,1:T(8,128)(2,1)}, bf16[128,320]{0,1:T(8,128)(2,1)}, u32[]{:S(2)}, u32[]{:S(2)}) collective-permute-start(bf16[128,320]{0,1:T(8,128)(2,1)} %get-tuple-element.308), channel_id=1, source_target_pairs={{0,4},{4,0},{8,12},{12,8},{16,20},{20,16},{24,28},{28,24},{32,36},... | collective-permute-start | bytes 245768 | tf_op jit(solution)/shard_map/ppermute | solution.py:339
  100.9 3.5 %collective-permute-start.2 = (bf16[128,320]{0,1:T(8,128)(2,1)}, bf16[128,320]{0,1:T(8,128)(2,1)}, u32[]{:S(2)}, u32[]{:S(2)}) collective-permute-start(bf16[128,320]{0,1:T(8,128)(2,1)} %get-tuple-element.308), channel_id=1, source_target_pairs={{0,12},{4,8},{8,4},{12,0},{16,28},{20,24},{24,20},{28,16},{32,44},... | collective-permute-start | bytes 245768 | tf_op jit(solution)/shard_map/ppermute | solution.py:339
  107.0 1.2 iota_add_fusion.1
  108.1 2.5 %broadcast_compare_fusion = pred[4096]{0:T(1024)(128)(4,1)} fusion(s32[]{:T(128)} %bitcast.2, s32[]{:T(128)} %bitcast.1, s32[]{:T(128)} %bitcast), kind=kLoop, calls=%fused_computation.127 | loop fusion | flops 163840 | bytes 4108 | tf_op jit(solution)/shard_map/lt | solution.py:409
  110.6 2.5 %add_select_fusion = s32[4096]{0:T(1024)} fusion(s32[]{:T(128)} %bitcast.2, s32[]{:T(128)} %bitcast.1, s32[]{:T(128)} %bitcast), kind=kLoop, calls=%fused_computation.104 | loop fusion | flops 159744 | bytes 16396 | tf_op jit(solution)/shard_map/jit(remainder)/select_n | solution.py:401
  113.0 1.9 %slice_bitcast_fusion.3 = (bf16[320,1024]{1,0:T(8,128)(2,1)S(1)}, bf16[320,1024]{1,0:T(8,128)(2,1)S(1)}, bf16[320,1024]{1,0:T(8,128)(2,1)S(1)}, bf16[320,1024]{1,0:T(8,128)(2,1)S(1)}) fusion(bf16[4,320,1024]{2,1,0:T(8,128)(2,1)} %get-tuple-element.208), kind=kLoop, calls=%fused_computation.70 | loop fusion | bytes 5242880 | tf_op jit(solution)/shard_map/squeeze | solution.py:391
  115.3 1.3 fusion.82
  116.6 39.6 %while.5 = (s32[]{:T(128)}, f32[128,2,4,80]{0,3,2,1:T(8,128)}, f32[128,2,4]{0,2,1:T(4,128)S(1)}, f32[128,2,4]{0,2,1:T(4,128)S(1)}, pred[4096]{0:T(1024)(128)(4,1...) while((s32[]{:T(128)}, f32[128,2,4,80]{0,3,2,1:T(8,128)}, ...), condition=%wide.region_4.5_spmd.clone, body=%wide.region_1.4_spmd.clone.sunk | while | flops 174118016 | bytes 10396435 | solution.py:280
  119.5 1.5 fusion.101
  124.4 1.5 fusion.101
  129.3 1.5 fusion.101
  134.2 1.5 fusion.101
  139.2 1.5 fusion.101
  144.1 1.5 fusion.101
  149.1 1.5 fusion.101
  154.0 1.5 fusion.101
  156.5 1.0 pad_maximum_fusion.7
  159.3 3.0 %collective-permute-start.5 = (bf16[128,640]{0,1:T(8,128)(2,1)S(1)}, bf16[128,640]{0,1:T(8,128)(2,1)S(1)}, u32[]{:S(2)}, u32[]{:S(2)}) collective-permute-start(bf16[128,640]{0,1:T(8,128)(2,1)S(1)} %bitcast.171), channel_id=1, source_target_pairs={{1,0},{2,1},{3,2},{0,3},{5,4},{6,5},{7,6},{4,7},{9,8},{10,9},{11,1... | collective-permute-start | bytes 491528 | tf_op jit(solution)/shard_map/ppermute | solution.py:288
  162.3 3.0 %collective-permute-start.4 = (bf16[128,640]{0,1:T(8,128)(2,1)S(1)}, bf16[128,640]{0,1:T(8,128)(2,1)S(1)}, u32[]{:S(2)}, u32[]{:S(2)}) collective-permute-start(bf16[128,640]{0,1:T(8,128)(2,1)S(1)} %bitcast.172), channel_id=1, source_target_pairs={{2,0},{3,1},{0,2},{1,3},{6,4},{7,5},{4,6},{5,7},{10,8},{11,9},{8,1... | collective-permute-start | bytes 491528 | tf_op jit(solution)/shard_map/ppermute | solution.py:288
  165.3 2.1 %collective-permute-start.3 = (bf16[128,640]{0,1:T(8,128)(2,1)S(1)}, bf16[128,640]{0,1:T(8,128)(2,1)S(1)}, u32[]{:S(2)}, u32[]{:S(2)}) collective-permute-start(bf16[128,640]{0,1:T(8,128)(2,1)S(1)} %bitcast.173), channel_id=1, source_target_pairs={{3,0},{0,1},{1,2},{2,3},{7,4},{4,5},{5,6},{6,7},{11,8},{8,9},{9,10... | collective-permute-start | bytes 491528 | tf_op jit(solution)/shard_map/ppermute | solution.py:288
  167.5 1.4 fusion.50
  168.9 1.8 %collective-permute-done.4 = bf16[128,640]{0,1:T(8,128)(2,1)S(1)} collective-permute-done((bf16[128,640]{0,1:T(8,128)(2,1)S(1)}, bf16[128,640]{0,1:T(8,128)(2,1)S(1)}, u32[]{:S(2)}, u32[]{:S(2)}) %collective-permute-start.4) | collective-permute-done | bytes 163872 | tf_op jit(solution)/shard_map/ppermute | solution.py:288
  170.7 4.0 %collective-permute-done.3 = bf16[128,640]{0,1:T(8,128)(2,1)S(1)} collective-permute-done((bf16[128,640]{0,1:T(8,128)(2,1)S(1)}, bf16[128,640]{0,1:T(8,128)(2,1)S(1)}, u32[]{:S(2)}, u32[]{:S(2)}) %collective-permute-start.3) | collective-permute-done | bytes 163872 | tf_op jit(solution)/shard_map/ppermute | solution.py:288
  175.3 4.1 %fusion.35 = bf16[128,640]{1,0:T(8,128)(2,1)} fusion(bf16[512,1600]{1,0:T(8,128)(2,1)S(1)} %reshape_reshape.3, bf16[2048,1600]{1,0:T(8,128)(2,1)} %bitcast.157, bf16[128,512]{0,1:T(8,128)(2,1)S(1)} %bitcast.168, bf16[128,2048]{0,1:T(8,128)(2,1)S(1)} %bitcast.159), kind=kOutput, calls=%fused_computation.54 | convolution fusion | flops 427376640 | bytes 9011200 | tf_op jit(solution)/shard_map/dot_general | solution.py:430
  (190 shorter events, 38.0 us)
Async XLA Ops:
  78.7 5.0 %copy-start = (bf16[128,50,128]{2,1,0:T(8,128)(2,1)S(1)}, bf16[128,50,128]{2,1,0:T(8,128)(2,1)}, u32[]{:S(2)}) copy-start(bf16[128,50,128]{2,1,0:T(8,128)(2,1)} %get-tuple-element.211) | copy-start | bytes 4915204
  85.5 4.2 %copy-start.7 = (s32[32]{0:T(128)S(1)}, s32[32]{0:T(128)}, u32[]{:S(2)}) copy-start(s32[32]{0:T(128)} %param.21) | copy-start | bytes 388
  85.6 19.0 %copy-start.8 = (s32[32]{0:T(128)S(1)}, s32[32]{0:T(128)}, u32[]{:S(2)}) copy-start(s32[32]{0:T(128)} %param.23) | copy-start | bytes 388
  85.6 20.1 %copy-start.9 = (s32[32]{0:T(128)S(1)}, s32[32]{0:T(128)}, u32[]{:S(2)}) copy-start(s32[32]{0:T(128)} %param.22) | copy-start | bytes 388
  89.7 25.3 %copy-start.3 = (f32[128,960]{0,1:T(8,128)}, f32[128,960]{0,1:T(8,128)S(1)}, u32[]{:S(2)}) copy-start(f32[128,960]{0,1:T(8,128)S(1)} %fusion.24) | copy-start | bytes 1474564
  92.4 64.1 %collective-permute-start.1 = (bf16[128,320]{0,1:T(8,128)(2,1)}, bf16[128,320]{0,1:T(8,128)(2,1)}, u32[]{:S(2)}, u32[]{:S(2)}) collective-permute-start(bf16[128,320]{0,1:T(8,128)(2,1)} %get-tuple-element.308), channel_id=1, source_target_pairs={{0,8},{4,12},{8,0},{12,4},{16,24},{20,28},{24,16},{28,20},{32,40},... | collective-permute-start | bytes 245768 | tf_op jit(solution)/shard_map/ppermute | solution.py:339
  94.3 62.2 %collective-permute-start = (bf16[128,320]{0,1:T(8,128)(2,1)}, bf16[128,320]{0,1:T(8,128)(2,1)}, u32[]{:S(2)}, u32[]{:S(2)}) collective-permute-start(bf16[128,320]{0,1:T(8,128)(2,1)} %get-tuple-element.308), channel_id=1, source_target_pairs={{0,4},{4,0},{8,12},{12,8},{16,20},{20,16},{24,28},{28,24},{32,36},... | collective-permute-start | bytes 245768 | tf_op jit(solution)/shard_map/ppermute | solution.py:339
  100.9 55.6 %collective-permute-start.2 = (bf16[128,320]{0,1:T(8,128)(2,1)}, bf16[128,320]{0,1:T(8,128)(2,1)}, u32[]{:S(2)}, u32[]{:S(2)}) collective-permute-start(bf16[128,320]{0,1:T(8,128)(2,1)} %get-tuple-element.308), channel_id=1, source_target_pairs={{0,12},{4,8},{8,4},{12,0},{16,28},{20,24},{24,20},{28,16},{32,44},... | collective-permute-start | bytes 245768 | tf_op jit(solution)/shard_map/ppermute | solution.py:339
  115.2 1.3 slice-start
  116.6 39.6 %copy-start.5 = (s32[512]{0:T(512)S(1)}, s32[512]{0:T(512)}, u32[]{:S(2)}) copy-start(s32[512]{0:T(512)} %iota_add_fusion.1) | copy-start | bytes 6148
  116.6 39.6 %copy-start.6 = (s32[128]{0:T(128)S(1)}, s32[128]{0:T(128)}, u32[]{:S(2)}) copy-start(s32[128]{0:T(128)} %get-tuple-element.315) | copy-start | bytes 1540
  116.6 39.9 %copy-start.4 = (bf16[1,128,320]{1,2,0:T(8,128)(2,1)S(1)}, bf16[1,128,320]{1,2,0:T(8,128)(2,1)}, u32[]{:S(2)}) copy-start(bf16[1,128,320]{1,2,0:T(8,128)(2,1)} %get-tuple-element.307) | copy-start | bytes 245764
  118.4 1.0 copy-start.10
  120.9 0.7 copy-start.11
  123.4 1.0 copy-start.10
  125.9 0.7 copy-start.11
  128.3 1.0 copy-start.10
  130.8 0.7 copy-start.11
  133.2 1.0 copy-start.10
  135.7 0.7 copy-start.11
  138.1 1.0 copy-start.10
  140.6 0.7 copy-start.11
  143.1 1.0 copy-start.10
  145.6 0.7 copy-start.11
  148.0 1.0 copy-start.10
  153.0 1.0 copy-start.10
  157.7 1.0 copy-start.12
  158.7 8.7 %copy-start.1 = (bf16[160,1024]{1,0:T(8,128)(2,1)S(1)}, bf16[160,1024]{1,0:T(8,128)(2,1)}, u32[]{:S(2)}) copy-start(bf16[160,1024]{1,0:T(8,128)(2,1)} %param.20) | copy-start | bytes 983044
  158.7 8.7 %copy-start.2 = (bf16[160,1024]{1,0:T(8,128)(2,1)S(1)}, bf16[160,1024]{1,0:T(8,128)(2,1)}, u32[]{:S(2)}) copy-start(bf16[160,1024]{1,0:T(8,128)(2,1)} %param.19) | copy-start | bytes 983044
  159.3 9.6 %collective-permute-start.5 = (bf16[128,640]{0,1:T(8,128)(2,1)S(1)}, bf16[128,640]{0,1:T(8,128)(2,1)S(1)}, u32[]{:S(2)}, u32[]{:S(2)}) collective-permute-start(bf16[128,640]{0,1:T(8,128)(2,1)S(1)} %bitcast.171), channel_id=1, source_target_pairs={{1,0},{2,1},{3,2},{0,3},{5,4},{6,5},{7,6},{4,7},{9,8},{10,9},{11,1... | collective-permute-start | bytes 491528 | tf_op jit(solution)/shard_map/ppermute | solution.py:288
  162.3 8.3 %collective-permute-start.4 = (bf16[128,640]{0,1:T(8,128)(2,1)S(1)}, bf16[128,640]{0,1:T(8,128)(2,1)S(1)}, u32[]{:S(2)}, u32[]{:S(2)}) collective-permute-start(bf16[128,640]{0,1:T(8,128)(2,1)S(1)} %bitcast.172), channel_id=1, source_target_pairs={{2,0},{3,1},{0,2},{1,3},{6,4},{7,5},{4,6},{5,7},{10,8},{11,9},{8,1... | collective-permute-start | bytes 491528 | tf_op jit(solution)/shard_map/ppermute | solution.py:288
  165.3 9.4 %collective-permute-start.3 = (bf16[128,640]{0,1:T(8,128)(2,1)S(1)}, bf16[128,640]{0,1:T(8,128)(2,1)S(1)}, u32[]{:S(2)}, u32[]{:S(2)}) collective-permute-start(bf16[128,640]{0,1:T(8,128)(2,1)S(1)} %bitcast.173), channel_id=1, source_target_pairs={{3,0},{0,1},{1,2},{2,3},{7,4},{4,5},{5,6},{6,7},{11,8},{8,9},{9,10... | collective-permute-start | bytes 491528 | tf_op jit(solution)/shard_map/ppermute | solution.py:288
  (2 other events, 1.5 us)

commit v10 on v5

--- a/solution.py
+++ b/solution.py
@@ -409,8 +409,7 @@
     )
     accum, top_score, total = state
     attended = (accum / total[..., None]).astype(jnp.bfloat16).reshape(tok_rows, query_width)
-    head_pieces = exchange(attended, "narrow", n_narrow, lambda d, k: (d - k) % n_narrow)
-    all_heads = in_member_order(head_pieces, me_narrow, lambda me, q: (me - q) % n_narrow, 1)
+    all_heads = lax.all_gather(attended, "narrow", axis=1, tiled=True)
     update = jnp.dot(all_heads, out_rows, preferred_element_type=jnp.float32).astype(jnp.bfloat16)
 
     first = ((place - owner) % GROUP * shard_rows - offset) % WIN

time: 173 us -> 169 us (0.977)
  blocking collectives: 0 us -> 10.2 us
  starting transfers between devices: 19.5 us -> 11.5 us
  waiting for transfers between devices: 6.03 us -> 0.01 us
    all_gather x0 -> x1, blocking collectives: none -> 10.2 us  [shards(): all_heads = lax.all_gather(attended, 'narrow', axis=1, tiled=True)]
    ppermute x3 -> x0, starting transfers between devices: 7.99 us -> none  [exchange(): lax.ppermute(block, axis, [(pairing(d, k), d) for d in range(count)])]
    ppermute x3 -> x0, waiting for transfers between devices: 6.03 us -> none  [exchange(): lax.ppermute(block, axis, [(pairing(d, k), d) for d in range(count)])]
  transfers between devices with their start and end apart: 6 -> 3, of which waited for: 2 -> 0; matrix products, arithmetic and copies ran while one was open for 24% -> 24% of each run, Pallas kernels for 0% -> 0%
where the time goes in v10:
time: 169 us; the launch traced here: 167 us
  Pallas kernels  67.7 us (40%)
  matrix products  33.4 us (20%)
  local copies, waits for them, and re-layouts  23.5 us (14%)
  other arithmetic  16.9 us (10%)
  starting transfers between devices  11.5 us (7%)
  blocking collectives  10.2 us (6%)
  between operations  2.94 us (2%)
    pallas_call x1, Pallas kernels, gather_wide(): pl.pallas_call(functools.partial(gather_kernel, nz, nx, nc, nn), out_shap...  67.7 us
    reshape x1, local copies, waits for them, and re-layouts, shards(): all_weights = gathered.reshape(-1, joined_width)  15.3 us
    dot_general x9, matrix products, step(): jnp.einsum('tgrk,gdk->tgrd', weights.astype(jnp.bfloat16), block_values,...  12.2 us
    dot_general x9, matrix products, step(): jnp.einsum('tgrd,gdk->tgrk', queries, block_keys, preferred_element_type=...  12 us
    ppermute x3, starting transfers between devices, group_route_pieces(): pieces.append(lax.ppermute(block, WIDE, route))  11.5 us
    all_gather x1, blocking collectives, shards(): all_heads = lax.all_gather(attended, 'narrow', axis=1, tiled=True)  10.2 us
    dot_general x1, matrix products, shards(): qkv_sum = jnp.dot(normed, qkv, preferred_element_type=jnp.float32)  4.81 us
    dot_general x1, matrix products, shards(): jnp.dot(all_heads, out_rows, preferred_element_type=jnp.float32)  4.3 us
  transfers between devices with their start and end apart: 3, of which 0 were waited for; matrix products, arithmetic and copies ran while one was open for 24% of the time, Pallas kernels for 0%

profile of v10, /device:TPU:1, one launch (start us, length us, event | category | flops | bytes accessed | tf_op | source)
XLA Modules:
  0.0 166.7 jit_solution(14774798185879420271)
XLA Ops:
  2.3 2.0 %pad_maximum_fusion.1.cache_ref = bf16[320,1024]{1,0:T(8,128)(2,1)} fusion(bf16[160,1024]{1,0:T(8,128)(2,1)} %param.20, bf16[160,1024]{1,0:T(8,128)(2,1)} %param.19), kind=kLoop, calls=%fused_computation.59 | loop fusion | flops 1310720 | bytes 1310720 | tf_op jit(solution)/shard_map/concatenate | solution.py:341
  4.3 67.7 %shard_map.130 = (bf16[128,250,128]{2,1,0:T(8,128)(2,1)}, bf16[4,320,1024]{2,1,0:T(8,128)(2,1)}, bf16[4,128,640]{2,1,0:T(8,128)(2,1)}) custom-call(bf16[250,128]{1,0:T(8,128)(2,1)} %reshape.239.blk_ref, bf16[320,1024]{1,0:T(8,128)(2,1)} %pad_maximum_fusion.1.cache_ref, bf16[128,640]{1,0:T(8,128)(2,1)} %tok_ref.1), custom_call_target="tpu_custom_call" | custom-call | bytes 16384000 | tf_op jit(solution)/shard_map/pallas_call | solution.py:168
  72.0 15.3 %reshape.241 = bf16[2560,1600]{1,0:T(8,128)(2,1)} reshape(bf16[128,250,128]{2,1,0:T(8,128)(2,1)} %get-tuple-element.209) | data formatting | bytes 16384000 | tf_op jit(solution)/shard_map/reshape | solution.py:344
  87.6 4.8 %fusion.23 = f32[128,960]{0,1:T(8,128)S(1)} fusion(bf16[2560,1600]{1,0:T(8,128)(2,1)} %reshape.241, f32[2560]{0:T(1024)S(1)} %convert_element_type.43, f32[128]{0:T(128)S(1)} %add_rsqrt_fusion, bf16[128,640]{1,0:T(8,128)(2,1)S(1)} %get-tuple-element.282, bf16[128,640]{1,0:T(8,128)(2,1)S(1)} %get-tuple-element.283, ...), kind=kOutput, calls=%fused_computation.30 | convolution fusion | flops 632750080 | bytes 6400512 | tf_op jit(solution)/shard_map/dot_general | solution.py:355
  95.2 6.0 %collective-permute-start.2 = (bf16[128,320]{0,1:T(8,128)(2,1)}, bf16[128,320]{0,1:T(8,128)(2,1)}, u32[]{:S(2)}, u32[]{:S(2)}) collective-permute-start(bf16[128,320]{0,1:T(8,128)(2,1)} %get-tuple-element.298), channel_id=1, source_target_pairs={{0,12},{4,8},{8,4},{12,0},{16,28},{20,24},{24,20},{28,16},{32,44},... | collective-permute-start | bytes 245768 | tf_op jit(solution)/shard_map/ppermute | solution.py:332
  101.2 3.6 %collective-permute-start.1 = (bf16[128,320]{0,1:T(8,128)(2,1)}, bf16[128,320]{0,1:T(8,128)(2,1)}, u32[]{:S(2)}, u32[]{:S(2)}) collective-permute-start(bf16[128,320]{0,1:T(8,128)(2,1)} %get-tuple-element.298), channel_id=1, source_target_pairs={{0,8},{4,12},{8,0},{12,4},{16,24},{20,28},{24,16},{28,20},{32,40},... | collective-permute-start | bytes 245768 | tf_op jit(solution)/shard_map/ppermute | solution.py:332
  104.8 1.9 %collective-permute-start = (bf16[128,320]{0,1:T(8,128)(2,1)}, bf16[128,320]{0,1:T(8,128)(2,1)}, u32[]{:S(2)}, u32[]{:S(2)}) collective-permute-start(bf16[128,320]{0,1:T(8,128)(2,1)} %get-tuple-element.298), channel_id=1, source_target_pairs={{0,4},{4,0},{8,12},{12,8},{16,20},{20,16},{24,28},{28,24},{32,36},... | collective-permute-start | bytes 245768 | tf_op jit(solution)/shard_map/ppermute | solution.py:332
  108.0 1.3 dynamic_slice.61
  109.3 1.8 %broadcast_compare_fusion = pred[4096]{0:T(1024)(128)(4,1)S(1)} fusion(s32[]{:T(128)} %bitcast.2, s32[]{:T(128)} %bitcast.1, s32[]{:T(128)} %bitcast), kind=kLoop, calls=%fused_computation.123 | loop fusion | flops 163840 | bytes 4108 | tf_op jit(solution)/shard_map/lt | solution.py:393
  111.2 1.8 %add_select_fusion = s32[4096]{0:T(1024)S(1)} fusion(s32[]{:T(128)} %bitcast.2, s32[]{:T(128)} %bitcast.1, s32[]{:T(128)} %bitcast), kind=kLoop, calls=%fused_computation.104 | loop fusion | flops 159744 | bytes 16396 | tf_op jit(solution)/shard_map/jit(remainder)/select_n | solution.py:385
  115.5 1.7 %fusion.82 = (bf16[160,4096]{1,0:T(8,128)(2,1)}, bf16[160,4096]{1,0:T(8,128)(2,1)}) fusion(bf16[320,4096]{1,0:T(8,128)(2,1)S(1)} %pad_maximum_fusion), kind=kLoop, calls=%fused_computation.146 | loop fusion | bytes 5242880 | tf_op jit(solution)/shard_map/slice | solution.py:377
  117.3 30.5 %while.5 = (s32[]{:T(128)}, f32[128,2,4,80]{0,3,2,1:T(8,128)S(1)}, f32[128,2,4]{0,2,1:T(4,128)S(1)}, f32[128,2,4]{0,2,1:T(4,128)S(1)}, pred[4096]{0:T(1024)(128)...) while((s32[]{:T(128)}, f32[128,2,4,80]{0,3,2,1:T(8,128)S(1)}, ...), condition=%wide.region_4.5_spmd.clone, body=%wide.region_1.4_spmd.clone.sunk | while | flops 174118016 | bytes 7774939 | solution.py:273
  117.7 1.4 fusion.99
  119.6 1.5 fusion.102
  121.5 1.4 fusion.99
  123.4 1.5 fusion.102
  125.3 1.4 fusion.99
  127.2 1.5 fusion.102
  129.1 1.4 fusion.99
  131.1 1.5 fusion.102
  132.9 1.4 fusion.99
  134.9 1.5 fusion.102
  136.8 1.4 fusion.99
  138.7 1.5 fusion.102
  140.6 1.4 fusion.99
  142.5 1.5 fusion.102
  144.4 1.4 fusion.99
  146.3 1.5 fusion.102
  148.2 1.0 pad_maximum_fusion.3
  150.8 10.2 %all_gather.3 = bf16[128,2560]{0,1:T(8,128)(2,1)S(1)} all-gather(bf16[128,640]{0,1:T(8,128)(2,1)S(1)} %bitcast.142), channel_id=1, replica_groups=mesh['z'=16,'x'=4,'c'=2,'narrow'=4] {'narrow'}, dimensions={1}, use_global_device_ids=true | all-gather | bytes 819200 | tf_op jit(solution)/shard_map/all_gather | solution.py:412
  161.0 4.3 %fusion.38 = bf16[128,640]{1,0:T(8,128)(2,1)} fusion(bf16[128,2560]{0,1:T(8,128)(2,1)S(1)} %all_gather.3, bf16[2560,1600]{1,0:T(8,128)(2,1)} %reshape.241), kind=kOutput, calls=%fused_computation.55 | convolution fusion | flops 419512320 | bytes 4096000 | tf_op jit(solution)/shard_map/dot_general | solution.py:413
  165.3 1.4 fusion.51
  (123 shorter events, 15.1 us)
Async XLA Ops:
  72.0 15.3 %copy-start.5 = (bf16[2560]{0:T(1024)(128)(2,1)S(1)}, bf16[2560]{0:T(1024)(128)(2,1)}, u32[]{:S(2)}) copy-start(bf16[2560]{0:T(1024)(128)(2,1)} %param.14) | copy-start | bytes 15364
  72.0 15.3 %copy-start.3 = (bf16[4,128,640]{2,1,0:T(8,128)(2,1)S(1)}, bf16[4,128,640]{2,1,0:T(8,128)(2,1)}, u32[]{:S(2)}) copy-start(bf16[4,128,640]{2,1,0:T(8,128)(2,1)} %get-tuple-element.208) | copy-start | bytes 1966084
  87.6 4.9 %copy-start.6 = (s32[32]{0:T(128)S(1)}, s32[32]{0:T(128)}, u32[]{:S(2)}) copy-start(s32[32]{0:T(128)} %param.21) | copy-start | bytes 388
  87.6 19.8 %copy-start.7 = (s32[32]{0:T(128)S(1)}, s32[32]{0:T(128)}, u32[]{:S(2)}) copy-start(s32[32]{0:T(128)} %param.22) | copy-start | bytes 388
  87.6 27.4 %copy-start = (bf16[4,320,1024]{2,1,0:T(8,128)(2,1)S(1)}, bf16[4,320,1024]{2,1,0:T(8,128)(2,1)}, u32[]{:S(2)}) copy-start(bf16[4,320,1024]{2,1,0:T(8,128)(2,1)} %get-tuple-element.207) | copy-start | bytes 7864324
  94.0 0.6 copy-start.4
  95.2 52.9 %collective-permute-start.2 = (bf16[128,320]{0,1:T(8,128)(2,1)}, bf16[128,320]{0,1:T(8,128)(2,1)}, u32[]{:S(2)}, u32[]{:S(2)}) collective-permute-start(bf16[128,320]{0,1:T(8,128)(2,1)} %get-tuple-element.298), channel_id=1, source_target_pairs={{0,12},{4,8},{8,4},{12,0},{16,28},{20,24},{24,20},{28,16},{32,44},... | collective-permute-start | bytes 245768 | tf_op jit(solution)/shard_map/ppermute | solution.py:332
  101.2 46.9 %collective-permute-start.1 = (bf16[128,320]{0,1:T(8,128)(2,1)}, bf16[128,320]{0,1:T(8,128)(2,1)}, u32[]{:S(2)}, u32[]{:S(2)}) collective-permute-start(bf16[128,320]{0,1:T(8,128)(2,1)} %get-tuple-element.298), channel_id=1, source_target_pairs={{0,8},{4,12},{8,0},{12,4},{16,24},{20,28},{24,16},{28,20},{32,40},... | collective-permute-start | bytes 245768 | tf_op jit(solution)/shard_map/ppermute | solution.py:332
  104.8 43.4 %collective-permute-start = (bf16[128,320]{0,1:T(8,128)(2,1)}, bf16[128,320]{0,1:T(8,128)(2,1)}, u32[]{:S(2)}, u32[]{:S(2)}) collective-permute-start(bf16[128,320]{0,1:T(8,128)(2,1)} %get-tuple-element.298), channel_id=1, source_target_pairs={{0,4},{4,0},{8,12},{12,8},{16,20},{20,16},{24,28},{28,24},{32,36},... | collective-permute-start | bytes 245768 | tf_op jit(solution)/shard_map/ppermute | solution.py:332
  115.5 1.8 %copy-start.8 = (f32[128,2,4,80]{0,3,2,1:T(8,128)S(1)}, f32[128,2,4,80]{0,3,2,1:T(8,128)}, u32[]{:S(2)}) copy-start(f32[128,2,4,80]{0,3,2,1:T(8,128)} %custom-call) | copy-start | bytes 983044
  161.0 4.3 %copy-start.1 = (bf16[160,1024]{1,0:T(8,128)(2,1)S(1)}, bf16[160,1024]{1,0:T(8,128)(2,1)}, u32[]{:S(2)}) copy-start(bf16[160,1024]{1,0:T(8,128)(2,1)} %param.20) | copy-start | bytes 983044
  161.0 4.3 %copy-start.2 = (bf16[160,1024]{1,0:T(8,128)(2,1)S(1)}, bf16[160,1024]{1,0:T(8,128)(2,1)}, u32[]{:S(2)}) copy-start(bf16[160,1024]{1,0:T(8,128)(2,1)} %param.19) | copy-start | bytes 983044

commit v11 on v10

--- a/solution.py
+++ b/solution.py
@@ -334,7 +334,10 @@
 
 
     sizes = (query_weight.shape[1], key_weight.shape[1], value_weight.shape[1], out_weight.shape[1])
-    joined = jnp.concatenate([query_weight, key_weight, value_weight, out_weight], axis=1)
+    pad_cols = -sum(sizes) % 128
+    joined = jnp.concatenate(
+        [query_weight, key_weight, value_weight, out_weight,
+         jnp.zeros((query_weight.shape[0], pad_cols), query_weight.dtype)], axis=1)
     block_rows, joined_width = joined.shape
     dims = (lax.psum(1, "z"), lax.psum(1, "x"), lax.psum(1, "c"))
     gathered, cache_blocks, tok_pieces = gather_wide(
@@ -343,7 +346,7 @@
     whole = jnp.concatenate([tok_pieces[q] for q in range(n_narrow)], axis=1)
     all_weights = gathered.reshape(-1, joined_width)
     qkv = all_weights[:, : sum(sizes[:3])]
-    out_rows = all_weights[:, sum(sizes[:3]) :]
+    out_rows = all_weights[:, sum(sizes[:3]) : sum(sizes)]
 
     normed = rms_normed(whole, norm_gain)
     tok_rows = whole.shape[0]

time: 169 us -> 172 us (1.018)
  transfers between devices with their start and end apart: 3 -> 3, of which waited for: 0 -> 0; matrix products, arithmetic and copies ran while one was open for 24% -> 23% of each run, Pallas kernels for 0% -> 0%
where the time goes in v11:
time: 172 us; the launch traced here: 169 us
  Pallas kernels  69.3 us (40%)
  matrix products  33.4 us (19%)
  local copies, waits for them, and re-layouts  24.7 us (14%)
  other arithmetic  16.9 us (10%)
  starting transfers between devices  11.5 us (7%)
  blocking collectives  10.2 us (6%)
  between operations  2.93 us (2%)
    pallas_call x1, Pallas kernels, gather_wide(): pl.pallas_call(functools.partial(gather_kernel, nz, nx, nc, nn), out_shap...  69.3 us
    reshape x1, local copies, waits for them, and re-layouts, shards(): all_weights = gathered.reshape(-1, joined_width)  16.5 us
    dot_general x9, matrix products, step(): jnp.einsum('tgrk,gdk->tgrd', weights.astype(jnp.bfloat16), block_values,...  12.2 us
    dot_general x9, matrix products, step(): jnp.einsum('tgrd,gdk->tgrk', queries, block_keys, preferred_element_type=...  12 us
    ppermute x3, starting transfers between devices, group_route_pieces(): pieces.append(lax.ppermute(block, WIDE, route))  11.5 us
    all_gather x1, blocking collectives, shards(): all_heads = lax.all_gather(attended, 'narrow', axis=1, tiled=True)  10.2 us
    dot_general x1, matrix products, shards(): qkv_sum = jnp.dot(normed, qkv, preferred_element_type=jnp.float32)  4.81 us
    dot_general x1, matrix products, shards(): jnp.dot(all_heads, out_rows, preferred_element_type=jnp.float32)  4.31 us
  transfers between devices with their start and end apart: 3, of which 0 were waited for; matrix products, arithmetic and copies ran while one was open for 23% of the time, Pallas kernels for 0%

profile of v11, /device:TPU:1, one launch (start us, length us, event | category | flops | bytes accessed | tf_op | source)
XLA Modules:
  0.0 169.4 jit_solution(1974729172723209589)
XLA Ops:
  2.3 2.0 %pad_maximum_fusion.1.cache_ref = bf16[320,1024]{1,0:T(8,128)(2,1)} fusion(bf16[160,1024]{1,0:T(8,128)(2,1)} %param.20, bf16[160,1024]{1,0:T(8,128)(2,1)} %param.19), kind=kLoop, calls=%fused_computation.59 | loop fusion | flops 1310720 | bytes 1310720 | tf_op jit(solution)/shard_map/concatenate | solution.py:344
  4.3 69.3 %shard_map.130 = (bf16[128,260,128]{2,1,0:T(8,128)(2,1)}, bf16[4,320,1024]{2,1,0:T(8,128)(2,1)}, bf16[4,128,640]{2,1,0:T(8,128)(2,1)}) custom-call(bf16[260,128]{1,0:T(8,128)(2,1)} %reshape.239.blk_ref, bf16[320,1024]{1,0:T(8,128)(2,1)} %pad_maximum_fusion.1.cache_ref, bf16[128,640]{1,0:T(8,128)(2,1)} %tok_ref.1), custom_call_target="tpu_custom_call" | custom-call | bytes 17039360 | tf_op jit(solution)/shard_map/pallas_call | solution.py:168
  73.7 16.5 %reshape.241 = bf16[2560,1664]{1,0:T(8,128)(2,1)} reshape(bf16[128,260,128]{2,1,0:T(8,128)(2,1)} %get-tuple-element.209) | data formatting | bytes 17039360 | tf_op jit(solution)/shard_map/reshape | solution.py:347
  90.5 4.8 %fusion.23 = f32[128,960]{0,1:T(8,128)S(1)} fusion(bf16[2560,1664]{1,0:T(8,128)(2,1)} %reshape.241, f32[2560]{0:T(1024)S(1)} %convert_element_type.43, f32[128]{0:T(128)S(1)} %add_rsqrt_fusion, bf16[128,640]{1,0:T(8,128)(2,1)S(1)} %get-tuple-element.282, bf16[128,640]{1,0:T(8,128)(2,1)S(1)} %get-tuple-element.283, ...), kind=kOutput, calls=%fused_computation.30 | convolution fusion | flops 632750080 | bytes 6400512 | tf_op jit(solution)/shard_map/dot_general | solution.py:358
  98.1 5.9 %collective-permute-start.2 = (bf16[128,320]{0,1:T(8,128)(2,1)}, bf16[128,320]{0,1:T(8,128)(2,1)}, u32[]{:S(2)}, u32[]{:S(2)}) collective-permute-start(bf16[128,320]{0,1:T(8,128)(2,1)} %get-tuple-element.298), channel_id=1, source_target_pairs={{0,12},{4,8},{8,4},{12,0},{16,28},{20,24},{24,20},{28,16},{32,44},... | collective-permute-start | bytes 245768 | tf_op jit(solution)/shard_map/ppermute | solution.py:332
  104.0 3.6 %collective-permute-start.1 = (bf16[128,320]{0,1:T(8,128)(2,1)}, bf16[128,320]{0,1:T(8,128)(2,1)}, u32[]{:S(2)}, u32[]{:S(2)}) collective-permute-start(bf16[128,320]{0,1:T(8,128)(2,1)} %get-tuple-element.298), channel_id=1, source_target_pairs={{0,8},{4,12},{8,0},{12,4},{16,24},{20,28},{24,16},{28,20},{32,40},... | collective-permute-start | bytes 245768 | tf_op jit(solution)/shard_map/ppermute | solution.py:332
  107.7 1.9 %collective-permute-start = (bf16[128,320]{0,1:T(8,128)(2,1)}, bf16[128,320]{0,1:T(8,128)(2,1)}, u32[]{:S(2)}, u32[]{:S(2)}) collective-permute-start(bf16[128,320]{0,1:T(8,128)(2,1)} %get-tuple-element.298), channel_id=1, source_target_pairs={{0,4},{4,0},{8,12},{12,8},{16,20},{20,16},{24,28},{28,24},{32,36},... | collective-permute-start | bytes 245768 | tf_op jit(solution)/shard_map/ppermute | solution.py:332
  110.9 1.2 dynamic_slice.61
  112.1 1.8 %broadcast_compare_fusion = pred[4096]{0:T(1024)(128)(4,1)S(1)} fusion(s32[]{:T(128)} %bitcast.2, s32[]{:T(128)} %bitcast.1, s32[]{:T(128)} %bitcast), kind=kLoop, calls=%fused_computation.123 | loop fusion | flops 163840 | bytes 4108 | tf_op jit(solution)/shard_map/lt | solution.py:396
  114.0 1.8 %add_select_fusion = s32[4096]{0:T(1024)S(1)} fusion(s32[]{:T(128)} %bitcast.2, s32[]{:T(128)} %bitcast.1, s32[]{:T(128)} %bitcast), kind=kLoop, calls=%fused_computation.104 | loop fusion | flops 159744 | bytes 16396 | tf_op jit(solution)/shard_map/jit(remainder)/select_n | solution.py:388
  118.3 1.7 fusion.82
  120.0 30.5 %while.5 = (s32[]{:T(128)}, f32[128,2,4,80]{0,3,2,1:T(8,128)S(1)}, f32[128,2,4]{0,2,1:T(4,128)S(1)}, f32[128,2,4]{0,2,1:T(4,128)S(1)}, pred[4096]{0:T(1024)(128)...) while((s32[]{:T(128)}, f32[128,2,4,80]{0,3,2,1:T(8,128)S(1)}, ...), condition=%wide.region_4.5_spmd.clone, body=%wide.region_1.4_spmd.clone.sunk | while | flops 174118016 | bytes 7774939 | solution.py:273
  120.4 1.4 fusion.99
  122.3 1.5 fusion.102
  124.2 1.4 fusion.99
  126.1 1.5 fusion.102
  128.0 1.4 fusion.99
  130.0 1.5 fusion.102
  131.8 1.4 fusion.99
  133.8 1.5 fusion.102
  135.7 1.4 fusion.99
  137.6 1.5 fusion.102
  139.5 1.4 fusion.99
  141.4 1.5 fusion.102
  143.3 1.4 fusion.99
  145.2 1.5 fusion.102
  147.1 1.4 fusion.99
  149.0 1.5 fusion.102
  150.9 1.0 pad_maximum_fusion.3
  153.6 10.2 %all_gather.3 = bf16[128,2560]{0,1:T(8,128)(2,1)S(1)} all-gather(bf16[128,640]{0,1:T(8,128)(2,1)S(1)} %bitcast.142), channel_id=1, replica_groups=mesh['z'=16,'x'=4,'c'=2,'narrow'=4] {'narrow'}, dimensions={1}, use_global_device_ids=true | all-gather | bytes 819200 | tf_op jit(solution)/shard_map/all_gather | solution.py:415
  163.7 4.3 %fusion.38 = bf16[128,640]{1,0:T(8,128)(2,1)} fusion(bf16[128,2560]{0,1:T(8,128)(2,1)S(1)} %all_gather.3, bf16[2560,1664]{1,0:T(8,128)(2,1)} %reshape.241), kind=kOutput, calls=%fused_computation.55 | convolution fusion | flops 419512320 | bytes 4096000 | tf_op jit(solution)/shard_map/dot_general | solution.py:416
  168.0 1.4 fusion.51
  (124 shorter events, 15.2 us)
Async XLA Ops:
  73.6 16.5 %copy-start.5 = (bf16[2560]{0:T(1024)(128)(2,1)S(1)}, bf16[2560]{0:T(1024)(128)(2,1)}, u32[]{:S(2)}) copy-start(bf16[2560]{0:T(1024)(128)(2,1)} %param.14) | copy-start | bytes 15364
  73.7 16.5 %copy-start.3 = (bf16[4,128,640]{2,1,0:T(8,128)(2,1)S(1)}, bf16[4,128,640]{2,1,0:T(8,128)(2,1)}, u32[]{:S(2)}) copy-start(bf16[4,128,640]{2,1,0:T(8,128)(2,1)} %get-tuple-element.208) | copy-start | bytes 1966084
  90.5 4.9 %copy-start.6 = (s32[32]{0:T(128)S(1)}, s32[32]{0:T(128)}, u32[]{:S(2)}) copy-start(s32[32]{0:T(128)} %param.21) | copy-start | bytes 388
  90.5 19.8 %copy-start.7 = (s32[32]{0:T(128)S(1)}, s32[32]{0:T(128)}, u32[]{:S(2)}) copy-start(s32[32]{0:T(128)} %param.22) | copy-start | bytes 388
  90.5 27.3 %copy-start = (bf16[4,320,1024]{2,1,0:T(8,128)(2,1)S(1)}, bf16[4,320,1024]{2,1,0:T(8,128)(2,1)}, u32[]{:S(2)}) copy-start(bf16[4,320,1024]{2,1,0:T(8,128)(2,1)} %get-tuple-element.207) | copy-start | bytes 7864324
  96.8 0.6 copy-start.4
  98.1 52.7 %collective-permute-start.2 = (bf16[128,320]{0,1:T(8,128)(2,1)}, bf16[128,320]{0,1:T(8,128)(2,1)}, u32[]{:S(2)}, u32[]{:S(2)}) collective-permute-start(bf16[128,320]{0,1:T(8,128)(2,1)} %get-tuple-element.298), channel_id=1, source_target_pairs={{0,12},{4,8},{8,4},{12,0},{16,28},{20,24},{24,20},{28,16},{32,44},... | collective-permute-start | bytes 245768 | tf_op jit(solution)/shard_map/ppermute | solution.py:332
  104.0 46.8 %collective-permute-start.1 = (bf16[128,320]{0,1:T(8,128)(2,1)}, bf16[128,320]{0,1:T(8,128)(2,1)}, u32[]{:S(2)}, u32[]{:S(2)}) collective-permute-start(bf16[128,320]{0,1:T(8,128)(2,1)} %get-tuple-element.298), channel_id=1, source_target_pairs={{0,8},{4,12},{8,0},{12,4},{16,24},{20,28},{24,16},{28,20},{32,40},... | collective-permute-start | bytes 245768 | tf_op jit(solution)/shard_map/ppermute | solution.py:332
  107.7 43.2 %collective-permute-start = (bf16[128,320]{0,1:T(8,128)(2,1)}, bf16[128,320]{0,1:T(8,128)(2,1)}, u32[]{:S(2)}, u32[]{:S(2)}) collective-permute-start(bf16[128,320]{0,1:T(8,128)(2,1)} %get-tuple-element.298), channel_id=1, source_target_pairs={{0,4},{4,0},{8,12},{12,8},{16,20},{20,16},{24,28},{28,24},{32,36},... | collective-permute-start | bytes 245768 | tf_op jit(solution)/shard_map/ppermute | solution.py:332
  118.3 1.7 %copy-start.8 = (f32[128,2,4,80]{0,3,2,1:T(8,128)S(1)}, f32[128,2,4,80]{0,3,2,1:T(8,128)}, u32[]{:S(2)}) copy-start(f32[128,2,4,80]{0,3,2,1:T(8,128)} %custom-call) | copy-start | bytes 983044
  163.7 4.3 %copy-start.1 = (bf16[160,1024]{1,0:T(8,128)(2,1)S(1)}, bf16[160,1024]{1,0:T(8,128)(2,1)}, u32[]{:S(2)}) copy-start(bf16[160,1024]{1,0:T(8,128)(2,1)} %param.20) | copy-start | bytes 983044
  163.7 4.3 %copy-start.2 = (bf16[160,1024]{1,0:T(8,128)(2,1)S(1)}, bf16[160,1024]{1,0:T(8,128)(2,1)}, u32[]{:S(2)}) copy-start(bf16[160,1024]{1,0:T(8,128)(2,1)} %param.19) | copy-start | bytes 983044

commit v12 on v10

--- a/solution.py
+++ b/solution.py
@@ -84,12 +84,6 @@
             device_id=(z, peer // nc, lax.rem(peer, nc), n), device_id_type=MESH_ID)
         cp.start()
         sends.append(cp)
-    for k in range(1, per_plane):
-        sender = lax.rem(me_xc - k + per_plane, per_plane)
-        pltpu.make_async_remote_copy(
-            src_ref=blk_ref, dst_ref=out_ref.at[z * per_plane + sender],
-            send_sem=plane_send.at[k], recv_sem=plane_recv.at[k],
-            device_id=(z, x, c, n), device_id_type=MESH_ID).wait_recv()
     locals_[0].wait()
     for k in range(1, 2 * nc):
         cp = pltpu.make_async_remote_copy(
@@ -127,6 +121,17 @@
     for s in range(1, half + 1):
         send_z = lax.rem(z - step_dir * (s - 1) + 2 * nz, nz)
         for j in range(subs):
+            if s == 1:
+                for b in range(sub_len):
+                    held = j * sub_len + b
+                    k = lax.rem(me_xc - held + per_plane, per_plane)
+
+                    @pl.when(k != 0)
+                    def _():
+                        pltpu.make_async_remote_copy(
+                            src_ref=blk_ref, dst_ref=out_ref.at[z * per_plane + held],
+                            send_sem=plane_send.at[k], recv_sem=plane_recv.at[k],
+                            device_id=(z, x, c, n), device_id_type=MESH_ID).wait_recv()
             if s > 1:
                 ring_copy(s - 1, j, send_z, (src_z, x, c, n)).wait_recv()
                 if s - 1 < half:

time: 169 us -> 168 us (level)
  the two profiles are of different devices: /device:TPU:1 before, /device:TPU:12 now
where the time goes in v12:
time: 168 us; the launch traced here: 167 us
  Pallas kernels  68.2 us (41%)
  matrix products  33.4 us (20%)
  local copies, waits for them, and re-layouts  23.5 us (14%)
  other arithmetic  16.9 us (10%)
  blocking collectives  13.9 us (8%)
  starting transfers between devices  7.58 us (5%)
  between operations  2.94 us (2%)
    pallas_call x1, Pallas kernels, gather_wide(): pl.pallas_call(functools.partial(gather_kernel, nz, nx, nc, nn), out_shap...  68.2 us
    reshape x1, local copies, waits for them, and re-layouts, shards(): all_weights = gathered.reshape(-1, joined_width)  15.3 us
    all_gather x1, blocking collectives, shards(): all_heads = lax.all_gather(attended, 'narrow', axis=1, tiled=True)  13.9 us
    dot_general x9, matrix products, step(): jnp.einsum('tgrk,gdk->tgrd', weights.astype(jnp.bfloat16), block_values,...  12.2 us
    dot_general x9, matrix products, step(): jnp.einsum('tgrd,gdk->tgrk', queries, block_keys, preferred_element_type=...  12 us
    ppermute x3, starting transfers between devices, group_route_pieces(): pieces.append(lax.ppermute(block, WIDE, route))  7.58 us
    dot_general x1, matrix products, shards(): qkv_sum = jnp.dot(normed, qkv, preferred_element_type=jnp.float32)  4.81 us
    dot_general x1, matrix products, shards(): jnp.dot(all_heads, out_rows, preferred_element_type=jnp.float32)  4.3 us
  transfers between devices with their start and end apart: 3, of which 0 were waited for; matrix products, arithmetic and copies ran while one was open for 24% of the time, Pallas kernels for 0%

profile of v12, /device:TPU:12, one launch (start us, length us, event | category | flops | bytes accessed | tf_op | source)
XLA Modules:
  0.0 167.0 jit_solution(5582529522194580069)
XLA Ops:
  2.3 2.0 %pad_maximum_fusion.1.cache_ref = bf16[320,1024]{1,0:T(8,128)(2,1)} fusion(bf16[160,1024]{1,0:T(8,128)(2,1)} %param.20, bf16[160,1024]{1,0:T(8,128)(2,1)} %param.19), kind=kLoop, calls=%fused_computation.59 | loop fusion | flops 1310720 | bytes 1310720 | tf_op jit(solution)/shard_map/concatenate | solution.py:346
  4.3 68.2 %shard_map.130 = (bf16[128,250,128]{2,1,0:T(8,128)(2,1)}, bf16[4,320,1024]{2,1,0:T(8,128)(2,1)}, bf16[4,128,640]{2,1,0:T(8,128)(2,1)}) custom-call(bf16[250,128]{1,0:T(8,128)(2,1)} %reshape.239.blk_ref, bf16[320,1024]{1,0:T(8,128)(2,1)} %pad_maximum_fusion.1.cache_ref, bf16[128,640]{1,0:T(8,128)(2,1)} %tok_ref.1), custom_call_target="tpu_custom_call" | custom-call | bytes 16384000 | tf_op jit(solution)/shard_map/pallas_call | solution.py:173
  72.5 15.3 %reshape.241 = bf16[2560,1600]{1,0:T(8,128)(2,1)} reshape(bf16[128,250,128]{2,1,0:T(8,128)(2,1)} %get-tuple-element.209) | data formatting | bytes 16384000 | tf_op jit(solution)/shard_map/reshape | solution.py:349
  88.1 4.8 %fusion.23 = f32[128,960]{0,1:T(8,128)S(1)} fusion(bf16[2560,1600]{1,0:T(8,128)(2,1)} %reshape.241, f32[2560]{0:T(1024)S(1)} %convert_element_type.43, f32[128]{0:T(128)S(1)} %add_rsqrt_fusion, bf16[128,640]{1,0:T(8,128)(2,1)S(1)} %get-tuple-element.282, bf16[128,640]{1,0:T(8,128)(2,1)S(1)} %get-tuple-element.283, ...), kind=kOutput, calls=%fused_computation.30 | convolution fusion | flops 632750080 | bytes 6400512 | tf_op jit(solution)/shard_map/dot_general | solution.py:360
  95.7 1.9 %collective-permute-start.2 = (bf16[128,320]{0,1:T(8,128)(2,1)}, bf16[128,320]{0,1:T(8,128)(2,1)}, u32[]{:S(2)}, u32[]{:S(2)}) collective-permute-start(bf16[128,320]{0,1:T(8,128)(2,1)} %get-tuple-element.298), channel_id=1, source_target_pairs={{0,12},{4,8},{8,4},{12,0},{16,28},{20,24},{24,20},{28,16},{32,44},... | collective-permute-start | bytes 245768 | tf_op jit(solution)/shard_map/ppermute | solution.py:337
  97.6 2.8 %collective-permute-start.1 = (bf16[128,320]{0,1:T(8,128)(2,1)}, bf16[128,320]{0,1:T(8,128)(2,1)}, u32[]{:S(2)}, u32[]{:S(2)}) collective-permute-start(bf16[128,320]{0,1:T(8,128)(2,1)} %get-tuple-element.298), channel_id=1, source_target_pairs={{0,8},{4,12},{8,0},{12,4},{16,24},{20,28},{24,16},{28,20},{32,40},... | collective-permute-start | bytes 245768 | tf_op jit(solution)/shard_map/ppermute | solution.py:337
  100.4 2.9 %collective-permute-start = (bf16[128,320]{0,1:T(8,128)(2,1)}, bf16[128,320]{0,1:T(8,128)(2,1)}, u32[]{:S(2)}, u32[]{:S(2)}) collective-permute-start(bf16[128,320]{0,1:T(8,128)(2,1)} %get-tuple-element.298), channel_id=1, source_target_pairs={{0,4},{4,0},{8,12},{12,8},{16,20},{20,16},{24,28},{28,24},{32,36},... | collective-permute-start | bytes 245768 | tf_op jit(solution)/shard_map/ppermute | solution.py:337
  104.6 1.3 dynamic_slice.61
  105.9 1.8 %broadcast_compare_fusion = pred[4096]{0:T(1024)(128)(4,1)S(1)} fusion(s32[]{:T(128)} %bitcast.2, s32[]{:T(128)} %bitcast.1, s32[]{:T(128)} %bitcast), kind=kLoop, calls=%fused_computation.123 | loop fusion | flops 163840 | bytes 4108 | tf_op jit(solution)/shard_map/lt | solution.py:398
  107.7 1.8 %add_select_fusion = s32[4096]{0:T(1024)S(1)} fusion(s32[]{:T(128)} %bitcast.2, s32[]{:T(128)} %bitcast.1, s32[]{:T(128)} %bitcast), kind=kLoop, calls=%fused_computation.104 | loop fusion | flops 159744 | bytes 16396 | tf_op jit(solution)/shard_map/jit(remainder)/select_n | solution.py:390
  112.1 1.7 %fusion.82 = (bf16[160,4096]{1,0:T(8,128)(2,1)}, bf16[160,4096]{1,0:T(8,128)(2,1)}) fusion(bf16[320,4096]{1,0:T(8,128)(2,1)S(1)} %pad_maximum_fusion), kind=kLoop, calls=%fused_computation.146 | loop fusion | bytes 5242880 | tf_op jit(solution)/shard_map/slice | solution.py:382
  113.9 30.5 %while.5 = (s32[]{:T(128)}, f32[128,2,4,80]{0,3,2,1:T(8,128)S(1)}, f32[128,2,4]{0,2,1:T(4,128)S(1)}, f32[128,2,4]{0,2,1:T(4,128)S(1)}, pred[4096]{0:T(1024)(128)...) while((s32[]{:T(128)}, f32[128,2,4,80]{0,3,2,1:T(8,128)S(1)}, ...), condition=%wide.region_4.5_spmd.clone, body=%wide.region_1.4_spmd.clone.sunk | while | flops 174118016 | bytes 7774939 | solution.py:278
  114.3 1.4 fusion.99
  116.2 1.5 fusion.102
  118.1 1.4 fusion.99
  120.0 1.5 fusion.102
  121.9 1.4 fusion.99
  123.8 1.5 fusion.102
  125.7 1.4 fusion.99
  127.6 1.5 fusion.102
  129.5 1.4 fusion.99
  131.4 1.5 fusion.102
  133.3 1.4 fusion.99
  135.3 1.5 fusion.102
  137.1 1.4 fusion.99
  139.1 1.5 fusion.102
  141.0 1.4 fusion.99
  142.9 1.5 fusion.102
  144.7 1.0 pad_maximum_fusion.3
  147.4 13.9 %all_gather.3 = bf16[128,2560]{0,1:T(8,128)(2,1)S(1)} all-gather(bf16[128,640]{0,1:T(8,128)(2,1)S(1)} %bitcast.142), channel_id=1, replica_groups=mesh['z'=16,'x'=4,'c'=2,'narrow'=4] {'narrow'}, dimensions={1}, use_global_device_ids=true | all-gather | bytes 819200 | tf_op jit(solution)/shard_map/all_gather | solution.py:417
  161.3 4.3 %fusion.38 = bf16[128,640]{1,0:T(8,128)(2,1)} fusion(bf16[128,2560]{0,1:T(8,128)(2,1)S(1)} %all_gather.3, bf16[2560,1600]{1,0:T(8,128)(2,1)} %reshape.241), kind=kOutput, calls=%fused_computation.55 | convolution fusion | flops 419512320 | bytes 4096000 | tf_op jit(solution)/shard_map/dot_general | solution.py:418
  165.6 1.4 fusion.51
  (123 shorter events, 15.1 us)
Async XLA Ops:
  72.5 15.3 %copy-start.5 = (bf16[2560]{0:T(1024)(128)(2,1)S(1)}, bf16[2560]{0:T(1024)(128)(2,1)}, u32[]{:S(2)}) copy-start(bf16[2560]{0:T(1024)(128)(2,1)} %param.14) | copy-start | bytes 15364
  72.5 15.3 %copy-start.3 = (bf16[4,128,640]{2,1,0:T(8,128)(2,1)S(1)}, bf16[4,128,640]{2,1,0:T(8,128)(2,1)}, u32[]{:S(2)}) copy-start(bf16[4,128,640]{2,1,0:T(8,128)(2,1)} %get-tuple-element.208) | copy-start | bytes 1966084
  88.1 4.9 %copy-start.6 = (s32[32]{0:T(128)S(1)}, s32[32]{0:T(128)}, u32[]{:S(2)}) copy-start(s32[32]{0:T(128)} %param.21) | copy-start | bytes 388
  88.1 15.9 %copy-start.7 = (s32[32]{0:T(128)S(1)}, s32[32]{0:T(128)}, u32[]{:S(2)}) copy-start(s32[32]{0:T(128)} %param.22) | copy-start | bytes 388
  88.1 23.5 %copy-start = (bf16[4,320,1024]{2,1,0:T(8,128)(2,1)S(1)}, bf16[4,320,1024]{2,1,0:T(8,128)(2,1)}, u32[]{:S(2)}) copy-start(bf16[4,320,1024]{2,1,0:T(8,128)(2,1)} %get-tuple-element.207) | copy-start | bytes 7864324
  94.4 0.6 copy-start.4
  95.7 49.0 %collective-permute-start.2 = (bf16[128,320]{0,1:T(8,128)(2,1)}, bf16[128,320]{0,1:T(8,128)(2,1)}, u32[]{:S(2)}, u32[]{:S(2)}) collective-permute-start(bf16[128,320]{0,1:T(8,128)(2,1)} %get-tuple-element.298), channel_id=1, source_target_pairs={{0,12},{4,8},{8,4},{12,0},{16,28},{20,24},{24,20},{28,16},{32,44},... | collective-permute-start | bytes 245768 | tf_op jit(solution)/shard_map/ppermute | solution.py:337
  97.6 47.1 %collective-permute-start.1 = (bf16[128,320]{0,1:T(8,128)(2,1)}, bf16[128,320]{0,1:T(8,128)(2,1)}, u32[]{:S(2)}, u32[]{:S(2)}) collective-permute-start(bf16[128,320]{0,1:T(8,128)(2,1)} %get-tuple-element.298), channel_id=1, source_target_pairs={{0,8},{4,12},{8,0},{12,4},{16,24},{20,28},{24,16},{28,20},{32,40},... | collective-permute-start | bytes 245768 | tf_op jit(solution)/shard_map/ppermute | solution.py:337
  100.4 44.4 %collective-permute-start = (bf16[128,320]{0,1:T(8,128)(2,1)}, bf16[128,320]{0,1:T(8,128)(2,1)}, u32[]{:S(2)}, u32[]{:S(2)}) collective-permute-start(bf16[128,320]{0,1:T(8,128)(2,1)} %get-tuple-element.298), channel_id=1, source_target_pairs={{0,4},{4,0},{8,12},{12,8},{16,20},{20,16},{24,28},{28,24},{32,36},... | collective-permute-start | bytes 245768 | tf_op jit(solution)/shard_map/ppermute | solution.py:337
  112.1 1.8 %copy-start.8 = (f32[128,2,4,80]{0,3,2,1:T(8,128)S(1)}, f32[128,2,4,80]{0,3,2,1:T(8,128)}, u32[]{:S(2)}) copy-start(f32[128,2,4,80]{0,3,2,1:T(8,128)} %custom-call) | copy-start | bytes 983044
  161.3 4.3 %copy-start.1 = (bf16[160,1024]{1,0:T(8,128)(2,1)S(1)}, bf16[160,1024]{1,0:T(8,128)(2,1)}, u32[]{:S(2)}) copy-start(bf16[160,1024]{1,0:T(8,128)(2,1)} %param.20) | copy-start | bytes 983044
  161.3 4.3 %copy-start.2 = (bf16[160,1024]{1,0:T(8,128)(2,1)S(1)}, bf16[160,1024]{1,0:T(8,128)(2,1)}, u32[]{:S(2)}) copy-start(bf16[160,1024]{1,0:T(8,128)(2,1)} %param.19) | copy-start | bytes 983044

commit v13 on v12

--- a/solution.py
+++ b/solution.py
@@ -33,7 +33,7 @@
 
 
 WIDE = ("z", "x", "c")
-RING_SUBS = 4
+RING_SUBS = 8
 
 
 def gather_kernel(nz, nx, nc, nn, blk_ref, cache_ref, tok_ref, out_ref, cache_out, tok_out,

time: 168 us -> 169 us (level)
  transfers between devices with their start and end apart: 3 -> 3, of which waited for: 0 -> 0; matrix products, arithmetic and copies ran while one was open for 24% -> 23% of each run, Pallas kernels for 0% -> 0%
where the time goes in v13:
time: 169 us; the launch traced here: 168 us
  Pallas kernels  69.5 us (41%)
  matrix products  33.4 us (20%)
  local copies, waits for them, and re-layouts  23.5 us (14%)
  other arithmetic  16.9 us (10%)
  blocking collectives  13.9 us (8%)
  starting transfers between devices  7.58 us (4%)
  between operations  2.94 us (2%)
    pallas_call x1, Pallas kernels, gather_wide(): pl.pallas_call(functools.partial(gather_kernel, nz, nx, nc, nn), out_shap...  69.5 us
    reshape x1, local copies, waits for them, and re-layouts, shards(): all_weights = gathered.reshape(-1, joined_width)  15.3 us
    all_gather x1, blocking collectives, shards(): all_heads = lax.all_gather(attended, 'narrow', axis=1, tiled=True)  13.9 us
    dot_general x9, matrix products, step(): jnp.einsum('tgrk,gdk->tgrd', weights.astype(jnp.bfloat16), block_values,...  12.2 us
    dot_general x9, matrix products, step(): jnp.einsum('tgrd,gdk->tgrk', queries, block_keys, preferred_element_type=...  12 us
    ppermute x3, starting transfers between devices, group_route_pieces(): pieces.append(lax.ppermute(block, WIDE, route))  7.58 us
    dot_general x1, matrix products, shards(): qkv_sum = jnp.dot(normed, qkv, preferred_element_type=jnp.float32)  4.81 us
    dot_general x1, matrix products, shards(): jnp.dot(all_heads, out_rows, preferred_element_type=jnp.float32)  4.3 us
  transfers between devices with their start and end apart: 3, of which 0 were waited for; matrix products, arithmetic and copies ran while one was open for 23% of the time, Pallas kernels for 0%

profile of v13, /device:TPU:12, one launch (start us, length us, event | category | flops | bytes accessed | tf_op | source)
XLA Modules:
  0.0 168.3 jit_solution(3756073614853510537)
XLA Ops:
  2.3 2.0 %pad_maximum_fusion.1.cache_ref = bf16[320,1024]{1,0:T(8,128)(2,1)} fusion(bf16[160,1024]{1,0:T(8,128)(2,1)} %param.20, bf16[160,1024]{1,0:T(8,128)(2,1)} %param.19), kind=kLoop, calls=%fused_computation.59 | loop fusion | flops 1310720 | bytes 1310720 | tf_op jit(solution)/shard_map/concatenate | solution.py:346
  4.3 69.5 %shard_map.130 = (bf16[128,250,128]{2,1,0:T(8,128)(2,1)}, bf16[4,320,1024]{2,1,0:T(8,128)(2,1)}, bf16[4,128,640]{2,1,0:T(8,128)(2,1)}) custom-call(bf16[250,128]{1,0:T(8,128)(2,1)} %reshape.239.blk_ref, bf16[320,1024]{1,0:T(8,128)(2,1)} %pad_maximum_fusion.1.cache_ref, bf16[128,640]{1,0:T(8,128)(2,1)} %tok_ref.1), custom_call_target="tpu_custom_call" | custom-call | bytes 16384000 | tf_op jit(solution)/shard_map/pallas_call | solution.py:173
  73.8 15.3 %reshape.241 = bf16[2560,1600]{1,0:T(8,128)(2,1)} reshape(bf16[128,250,128]{2,1,0:T(8,128)(2,1)} %get-tuple-element.209) | data formatting | bytes 16384000 | tf_op jit(solution)/shard_map/reshape | solution.py:349
  89.4 4.8 %fusion.23 = f32[128,960]{0,1:T(8,128)S(1)} fusion(bf16[2560,1600]{1,0:T(8,128)(2,1)} %reshape.241, f32[2560]{0:T(1024)S(1)} %convert_element_type.43, f32[128]{0:T(128)S(1)} %add_rsqrt_fusion, bf16[128,640]{1,0:T(8,128)(2,1)S(1)} %get-tuple-element.282, bf16[128,640]{1,0:T(8,128)(2,1)S(1)} %get-tuple-element.283, ...), kind=kOutput, calls=%fused_computation.30 | convolution fusion | flops 632750080 | bytes 6400512 | tf_op jit(solution)/shard_map/dot_general | solution.py:360
  97.0 1.9 %collective-permute-start.2 = (bf16[128,320]{0,1:T(8,128)(2,1)}, bf16[128,320]{0,1:T(8,128)(2,1)}, u32[]{:S(2)}, u32[]{:S(2)}) collective-permute-start(bf16[128,320]{0,1:T(8,128)(2,1)} %get-tuple-element.298), channel_id=1, source_target_pairs={{0,12},{4,8},{8,4},{12,0},{16,28},{20,24},{24,20},{28,16},{32,44},... | collective-permute-start | bytes 245768 | tf_op jit(solution)/shard_map/ppermute | solution.py:337
  98.9 2.8 %collective-permute-start.1 = (bf16[128,320]{0,1:T(8,128)(2,1)}, bf16[128,320]{0,1:T(8,128)(2,1)}, u32[]{:S(2)}, u32[]{:S(2)}) collective-permute-start(bf16[128,320]{0,1:T(8,128)(2,1)} %get-tuple-element.298), channel_id=1, source_target_pairs={{0,8},{4,12},{8,0},{12,4},{16,24},{20,28},{24,16},{28,20},{32,40},... | collective-permute-start | bytes 245768 | tf_op jit(solution)/shard_map/ppermute | solution.py:337
  101.6 2.9 %collective-permute-start = (bf16[128,320]{0,1:T(8,128)(2,1)}, bf16[128,320]{0,1:T(8,128)(2,1)}, u32[]{:S(2)}, u32[]{:S(2)}) collective-permute-start(bf16[128,320]{0,1:T(8,128)(2,1)} %get-tuple-element.298), channel_id=1, source_target_pairs={{0,4},{4,0},{8,12},{12,8},{16,20},{20,16},{24,28},{28,24},{32,36},... | collective-permute-start | bytes 245768 | tf_op jit(solution)/shard_map/ppermute | solution.py:337
  105.9 1.3 dynamic_slice.61
  107.2 1.8 %broadcast_compare_fusion = pred[4096]{0:T(1024)(128)(4,1)S(1)} fusion(s32[]{:T(128)} %bitcast.2, s32[]{:T(128)} %bitcast.1, s32[]{:T(128)} %bitcast), kind=kLoop, calls=%fused_computation.123 | loop fusion | flops 163840 | bytes 4108 | tf_op jit(solution)/shard_map/lt | solution.py:398
  109.0 1.8 %add_select_fusion = s32[4096]{0:T(1024)S(1)} fusion(s32[]{:T(128)} %bitcast.2, s32[]{:T(128)} %bitcast.1, s32[]{:T(128)} %bitcast), kind=kLoop, calls=%fused_computation.104 | loop fusion | flops 159744 | bytes 16396 | tf_op jit(solution)/shard_map/jit(remainder)/select_n | solution.py:390
  113.4 1.7 %fusion.82 = (bf16[160,4096]{1,0:T(8,128)(2,1)}, bf16[160,4096]{1,0:T(8,128)(2,1)}) fusion(bf16[320,4096]{1,0:T(8,128)(2,1)S(1)} %pad_maximum_fusion), kind=kLoop, calls=%fused_computation.146 | loop fusion | bytes 5242880 | tf_op jit(solution)/shard_map/slice | solution.py:382
  115.1 30.5 %while.5 = (s32[]{:T(128)}, f32[128,2,4,80]{0,3,2,1:T(8,128)S(1)}, f32[128,2,4]{0,2,1:T(4,128)S(1)}, f32[128,2,4]{0,2,1:T(4,128)S(1)}, pred[4096]{0:T(1024)(128)...) while((s32[]{:T(128)}, f32[128,2,4,80]{0,3,2,1:T(8,128)S(1)}, ...), condition=%wide.region_4.5_spmd.clone, body=%wide.region_1.4_spmd.clone.sunk | while | flops 174118016 | bytes 7774939 | solution.py:278
  115.5 1.4 fusion.99
  117.5 1.5 fusion.102
  119.4 1.4 fusion.99
  121.3 1.5 fusion.102
  123.2 1.4 fusion.99
  125.1 1.5 fusion.102
  127.0 1.4 fusion.99
  128.9 1.5 fusion.102
  130.8 1.4 fusion.99
  132.7 1.5 fusion.102
  134.6 1.4 fusion.99
  136.5 1.5 fusion.102
  138.4 1.4 fusion.99
  140.4 1.5 fusion.102
  142.2 1.4 fusion.99
  144.2 1.5 fusion.102
  146.0 1.0 pad_maximum_fusion.3
  148.7 13.9 %all_gather.3 = bf16[128,2560]{0,1:T(8,128)(2,1)S(1)} all-gather(bf16[128,640]{0,1:T(8,128)(2,1)S(1)} %bitcast.142), channel_id=1, replica_groups=mesh['z'=16,'x'=4,'c'=2,'narrow'=4] {'narrow'}, dimensions={1}, use_global_device_ids=true | all-gather | bytes 819200 | tf_op jit(solution)/shard_map/all_gather | solution.py:417
  162.6 4.3 %fusion.38 = bf16[128,640]{1,0:T(8,128)(2,1)} fusion(bf16[128,2560]{0,1:T(8,128)(2,1)S(1)} %all_gather.3, bf16[2560,1600]{1,0:T(8,128)(2,1)} %reshape.241), kind=kOutput, calls=%fused_computation.55 | convolution fusion | flops 419512320 | bytes 4096000 | tf_op jit(solution)/shard_map/dot_general | solution.py:418
  166.9 1.4 fusion.51
  (123 shorter events, 15.1 us)
Async XLA Ops:
  73.8 15.3 %copy-start.5 = (bf16[2560]{0:T(1024)(128)(2,1)S(1)}, bf16[2560]{0:T(1024)(128)(2,1)}, u32[]{:S(2)}) copy-start(bf16[2560]{0:T(1024)(128)(2,1)} %param.14) | copy-start | bytes 15364
  73.8 15.3 %copy-start.3 = (bf16[4,128,640]{2,1,0:T(8,128)(2,1)S(1)}, bf16[4,128,640]{2,1,0:T(8,128)(2,1)}, u32[]{:S(2)}) copy-start(bf16[4,128,640]{2,1,0:T(8,128)(2,1)} %get-tuple-element.208) | copy-start | bytes 1966084
  89.4 4.9 %copy-start.6 = (s32[32]{0:T(128)S(1)}, s32[32]{0:T(128)}, u32[]{:S(2)}) copy-start(s32[32]{0:T(128)} %param.21) | copy-start | bytes 388
  89.4 15.9 %copy-start.7 = (s32[32]{0:T(128)S(1)}, s32[32]{0:T(128)}, u32[]{:S(2)}) copy-start(s32[32]{0:T(128)} %param.22) | copy-start | bytes 388
  89.4 23.5 %copy-start = (bf16[4,320,1024]{2,1,0:T(8,128)(2,1)S(1)}, bf16[4,320,1024]{2,1,0:T(8,128)(2,1)}, u32[]{:S(2)}) copy-start(bf16[4,320,1024]{2,1,0:T(8,128)(2,1)} %get-tuple-element.207) | copy-start | bytes 7864324
  95.7 0.6 copy-start.4
  97.0 49.0 %collective-permute-start.2 = (bf16[128,320]{0,1:T(8,128)(2,1)}, bf16[128,320]{0,1:T(8,128)(2,1)}, u32[]{:S(2)}, u32[]{:S(2)}) collective-permute-start(bf16[128,320]{0,1:T(8,128)(2,1)} %get-tuple-element.298), channel_id=1, source_target_pairs={{0,12},{4,8},{8,4},{12,0},{16,28},{20,24},{24,20},{28,16},{32,44},... | collective-permute-start | bytes 245768 | tf_op jit(solution)/shard_map/ppermute | solution.py:337
  98.9 47.1 %collective-permute-start.1 = (bf16[128,320]{0,1:T(8,128)(2,1)}, bf16[128,320]{0,1:T(8,128)(2,1)}, u32[]{:S(2)}, u32[]{:S(2)}) collective-permute-start(bf16[128,320]{0,1:T(8,128)(2,1)} %get-tuple-element.298), channel_id=1, source_target_pairs={{0,8},{4,12},{8,0},{12,4},{16,24},{20,28},{24,16},{28,20},{32,40},... | collective-permute-start | bytes 245768 | tf_op jit(solution)/shard_map/ppermute | solution.py:337
  101.6 44.4 %collective-permute-start = (bf16[128,320]{0,1:T(8,128)(2,1)}, bf16[128,320]{0,1:T(8,128)(2,1)}, u32[]{:S(2)}, u32[]{:S(2)}) collective-permute-start(bf16[128,320]{0,1:T(8,128)(2,1)} %get-tuple-element.298), channel_id=1, source_target_pairs={{0,4},{4,0},{8,12},{12,8},{16,20},{20,16},{24,28},{28,24},{32,36},... | collective-permute-start | bytes 245768 | tf_op jit(solution)/shard_map/ppermute | solution.py:337
  113.4 1.8 %copy-start.8 = (f32[128,2,4,80]{0,3,2,1:T(8,128)S(1)}, f32[128,2,4,80]{0,3,2,1:T(8,128)}, u32[]{:S(2)}) copy-start(f32[128,2,4,80]{0,3,2,1:T(8,128)} %custom-call) | copy-start | bytes 983044
  162.6 4.3 %copy-start.1 = (bf16[160,1024]{1,0:T(8,128)(2,1)S(1)}, bf16[160,1024]{1,0:T(8,128)(2,1)}, u32[]{:S(2)}) copy-start(bf16[160,1024]{1,0:T(8,128)(2,1)} %param.20) | copy-start | bytes 983044
  162.6 4.3 %copy-start.2 = (bf16[160,1024]{1,0:T(8,128)(2,1)S(1)}, bf16[160,1024]{1,0:T(8,128)(2,1)}, u32[]{:S(2)}) copy-start(bf16[160,1024]{1,0:T(8,128)(2,1)} %param.19) | copy-start | bytes 983044

commit v14 on v12

--- a/solution.py
+++ b/solution.py
@@ -134,13 +134,13 @@
                             device_id=(z, x, c, n), device_id_type=MESH_ID).wait_recv()
             if s > 1:
                 ring_copy(s - 1, j, send_z, (src_z, x, c, n)).wait_recv()
-                if s - 1 < half:
-                    dp = die_copy(s - 1, j, send_z)
-                    dp.start()
-                    sends.append(dp)
             cp = ring_copy(s, j, send_z, (dst_z, x, c, n))
             cp.start()
             sends.append(cp)
+            if s > 1:
+                dp = die_copy(s - 1, j, send_z)
+                dp.start()
+                sends.append(dp)
     last_z = lax.rem(z - step_dir * half + 2 * nz, nz)
     for j in range(subs):
         ring_copy(half, j, last_z, (src_z, x, c, n)).wait_recv()

time: 168 us -> 168 us (level)
  no operation moved by 1% of the time
where the time goes in v14:
time: 168 us; the launch traced here: 167 us
  Pallas kernels  68.2 us (41%)
  matrix products  33.4 us (20%)
  local copies, waits for them, and re-layouts  23.5 us (14%)
  other arithmetic  16.9 us (10%)
  blocking collectives  13.9 us (8%)
  starting transfers between devices  7.58 us (5%)
  between operations  2.94 us (2%)
    pallas_call x1, Pallas kernels, gather_wide(): pl.pallas_call(functools.partial(gather_kernel, nz, nx, nc, nn), out_shap...  68.2 us
    reshape x1, local copies, waits for them, and re-layouts, shards(): all_weights = gathered.reshape(-1, joined_width)  15.3 us
    all_gather x1, blocking collectives, shards(): all_heads = lax.all_gather(attended, 'narrow', axis=1, tiled=True)  13.9 us
    dot_general x9, matrix products, step(): jnp.einsum('tgrk,gdk->tgrd', weights.astype(jnp.bfloat16), block_values,...  12.2 us
    dot_general x9, matrix products, step(): jnp.einsum('tgrd,gdk->tgrk', queries, block_keys, preferred_element_type=...  12 us
    ppermute x3, starting transfers between devices, group_route_pieces(): pieces.append(lax.ppermute(block, WIDE, route))  7.58 us
    dot_general x1, matrix products, shards(): qkv_sum = jnp.dot(normed, qkv, preferred_element_type=jnp.float32)  4.81 us
    dot_general x1, matrix products, shards(): jnp.dot(all_heads, out_rows, preferred_element_type=jnp.float32)  4.3 us
  transfers between devices with their start and end apart: 3, of which 0 were waited for; matrix products, arithmetic and copies ran while one was open for 24% of the time, Pallas kernels for 0%

profile of v14, /device:TPU:12, one launch (start us, length us, event | category | flops | bytes accessed | tf_op | source)
XLA Modules:
  0.0 167.0 jit_solution(10350952742885197305)
XLA Ops:
  2.3 2.0 %pad_maximum_fusion.1.cache_ref = bf16[320,1024]{1,0:T(8,128)(2,1)} fusion(bf16[160,1024]{1,0:T(8,128)(2,1)} %param.20, bf16[160,1024]{1,0:T(8,128)(2,1)} %param.19), kind=kLoop, calls=%fused_computation.59 | loop fusion | flops 1310720 | bytes 1310720 | tf_op jit(solution)/shard_map/concatenate | solution.py:346
  4.3 68.2 %shard_map.130 = (bf16[128,250,128]{2,1,0:T(8,128)(2,1)}, bf16[4,320,1024]{2,1,0:T(8,128)(2,1)}, bf16[4,128,640]{2,1,0:T(8,128)(2,1)}) custom-call(bf16[250,128]{1,0:T(8,128)(2,1)} %reshape.239.blk_ref, bf16[320,1024]{1,0:T(8,128)(2,1)} %pad_maximum_fusion.1.cache_ref, bf16[128,640]{1,0:T(8,128)(2,1)} %tok_ref.1), custom_call_target="tpu_custom_call" | custom-call | bytes 16384000 | tf_op jit(solution)/shard_map/pallas_call | solution.py:173
  72.5 15.3 %reshape.241 = bf16[2560,1600]{1,0:T(8,128)(2,1)} reshape(bf16[128,250,128]{2,1,0:T(8,128)(2,1)} %get-tuple-element.209) | data formatting | bytes 16384000 | tf_op jit(solution)/shard_map/reshape | solution.py:349
  88.1 4.8 %fusion.23 = f32[128,960]{0,1:T(8,128)S(1)} fusion(bf16[2560,1600]{1,0:T(8,128)(2,1)} %reshape.241, f32[2560]{0:T(1024)S(1)} %convert_element_type.43, f32[128]{0:T(128)S(1)} %add_rsqrt_fusion, bf16[128,640]{1,0:T(8,128)(2,1)S(1)} %get-tuple-element.282, bf16[128,640]{1,0:T(8,128)(2,1)S(1)} %get-tuple-element.283, ...), kind=kOutput, calls=%fused_computation.30 | convolution fusion | flops 632750080 | bytes 6400512 | tf_op jit(solution)/shard_map/dot_general | solution.py:360
  95.7 1.9 %collective-permute-start.2 = (bf16[128,320]{0,1:T(8,128)(2,1)}, bf16[128,320]{0,1:T(8,128)(2,1)}, u32[]{:S(2)}, u32[]{:S(2)}) collective-permute-start(bf16[128,320]{0,1:T(8,128)(2,1)} %get-tuple-element.298), channel_id=1, source_target_pairs={{0,12},{4,8},{8,4},{12,0},{16,28},{20,24},{24,20},{28,16},{32,44},... | collective-permute-start | bytes 245768 | tf_op jit(solution)/shard_map/ppermute | solution.py:337
  97.6 2.8 %collective-permute-start.1 = (bf16[128,320]{0,1:T(8,128)(2,1)}, bf16[128,320]{0,1:T(8,128)(2,1)}, u32[]{:S(2)}, u32[]{:S(2)}) collective-permute-start(bf16[128,320]{0,1:T(8,128)(2,1)} %get-tuple-element.298), channel_id=1, source_target_pairs={{0,8},{4,12},{8,0},{12,4},{16,24},{20,28},{24,16},{28,20},{32,40},... | collective-permute-start | bytes 245768 | tf_op jit(solution)/shard_map/ppermute | solution.py:337
  100.4 2.9 %collective-permute-start = (bf16[128,320]{0,1:T(8,128)(2,1)}, bf16[128,320]{0,1:T(8,128)(2,1)}, u32[]{:S(2)}, u32[]{:S(2)}) collective-permute-start(bf16[128,320]{0,1:T(8,128)(2,1)} %get-tuple-element.298), channel_id=1, source_target_pairs={{0,4},{4,0},{8,12},{12,8},{16,20},{20,16},{24,28},{28,24},{32,36},... | collective-permute-start | bytes 245768 | tf_op jit(solution)/shard_map/ppermute | solution.py:337
  104.6 1.3 dynamic_slice.61
  105.9 1.8 %broadcast_compare_fusion = pred[4096]{0:T(1024)(128)(4,1)S(1)} fusion(s32[]{:T(128)} %bitcast.2, s32[]{:T(128)} %bitcast.1, s32[]{:T(128)} %bitcast), kind=kLoop, calls=%fused_computation.123 | loop fusion | flops 163840 | bytes 4108 | tf_op jit(solution)/shard_map/lt | solution.py:398
  107.7 1.8 %add_select_fusion = s32[4096]{0:T(1024)S(1)} fusion(s32[]{:T(128)} %bitcast.2, s32[]{:T(128)} %bitcast.1, s32[]{:T(128)} %bitcast), kind=kLoop, calls=%fused_computation.104 | loop fusion | flops 159744 | bytes 16396 | tf_op jit(solution)/shard_map/jit(remainder)/select_n | solution.py:390
  112.1 1.7 %fusion.82 = (bf16[160,4096]{1,0:T(8,128)(2,1)}, bf16[160,4096]{1,0:T(8,128)(2,1)}) fusion(bf16[320,4096]{1,0:T(8,128)(2,1)S(1)} %pad_maximum_fusion), kind=kLoop, calls=%fused_computation.146 | loop fusion | bytes 5242880 | tf_op jit(solution)/shard_map/slice | solution.py:382
  113.9 30.5 %while.5 = (s32[]{:T(128)}, f32[128,2,4,80]{0,3,2,1:T(8,128)S(1)}, f32[128,2,4]{0,2,1:T(4,128)S(1)}, f32[128,2,4]{0,2,1:T(4,128)S(1)}, pred[4096]{0:T(1024)(128)...) while((s32[]{:T(128)}, f32[128,2,4,80]{0,3,2,1:T(8,128)S(1)}, ...), condition=%wide.region_4.5_spmd.clone, body=%wide.region_1.4_spmd.clone.sunk | while | flops 174118016 | bytes 7774939 | solution.py:278
  114.3 1.4 fusion.99
  116.2 1.5 fusion.102
  118.1 1.4 fusion.99
  120.0 1.5 fusion.102
  121.9 1.4 fusion.99
  123.8 1.5 fusion.102
  125.7 1.4 fusion.99
  127.6 1.5 fusion.102
  129.5 1.4 fusion.99
  131.4 1.5 fusion.102
  133.3 1.4 fusion.99
  135.3 1.5 fusion.102
  137.1 1.4 fusion.99
  139.1 1.5 fusion.102
  141.0 1.4 fusion.99
  142.9 1.5 fusion.102
  144.7 1.0 pad_maximum_fusion.3
  147.4 13.9 %all_gather.3 = bf16[128,2560]{0,1:T(8,128)(2,1)S(1)} all-gather(bf16[128,640]{0,1:T(8,128)(2,1)S(1)} %bitcast.142), channel_id=1, replica_groups=mesh['z'=16,'x'=4,'c'=2,'narrow'=4] {'narrow'}, dimensions={1}, use_global_device_ids=true | all-gather | bytes 819200 | tf_op jit(solution)/shard_map/all_gather | solution.py:417
  161.3 4.3 %fusion.38 = bf16[128,640]{1,0:T(8,128)(2,1)} fusion(bf16[128,2560]{0,1:T(8,128)(2,1)S(1)} %all_gather.3, bf16[2560,1600]{1,0:T(8,128)(2,1)} %reshape.241), kind=kOutput, calls=%fused_computation.55 | convolution fusion | flops 419512320 | bytes 4096000 | tf_op jit(solution)/shard_map/dot_general | solution.py:418
  165.6 1.4 fusion.51
  (123 shorter events, 15.1 us)
Async XLA Ops:
  72.5 15.3 %copy-start.5 = (bf16[2560]{0:T(1024)(128)(2,1)S(1)}, bf16[2560]{0:T(1024)(128)(2,1)}, u32[]{:S(2)}) copy-start(bf16[2560]{0:T(1024)(128)(2,1)} %param.14) | copy-start | bytes 15364
  72.5 15.3 %copy-start.3 = (bf16[4,128,640]{2,1,0:T(8,128)(2,1)S(1)}, bf16[4,128,640]{2,1,0:T(8,128)(2,1)}, u32[]{:S(2)}) copy-start(bf16[4,128,640]{2,1,0:T(8,128)(2,1)} %get-tuple-element.208) | copy-start | bytes 1966084
  88.1 4.9 %copy-start.6 = (s32[32]{0:T(128)S(1)}, s32[32]{0:T(128)}, u32[]{:S(2)}) copy-start(s32[32]{0:T(128)} %param.21) | copy-start | bytes 388
  88.1 15.9 %copy-start.7 = (s32[32]{0:T(128)S(1)}, s32[32]{0:T(128)}, u32[]{:S(2)}) copy-start(s32[32]{0:T(128)} %param.22) | copy-start | bytes 388
  88.1 23.5 %copy-start = (bf16[4,320,1024]{2,1,0:T(8,128)(2,1)S(1)}, bf16[4,320,1024]{2,1,0:T(8,128)(2,1)}, u32[]{:S(2)}) copy-start(bf16[4,320,1024]{2,1,0:T(8,128)(2,1)} %get-tuple-element.207) | copy-start | bytes 7864324
  94.4 0.6 copy-start.4
  95.7 49.0 %collective-permute-start.2 = (bf16[128,320]{0,1:T(8,128)(2,1)}, bf16[128,320]{0,1:T(8,128)(2,1)}, u32[]{:S(2)}, u32[]{:S(2)}) collective-permute-start(bf16[128,320]{0,1:T(8,128)(2,1)} %get-tuple-element.298), channel_id=1, source_target_pairs={{0,12},{4,8},{8,4},{12,0},{16,28},{20,24},{24,20},{28,16},{32,44},... | collective-permute-start | bytes 245768 | tf_op jit(solution)/shard_map/ppermute | solution.py:337
  97.6 47.1 %collective-permute-start.1 = (bf16[128,320]{0,1:T(8,128)(2,1)}, bf16[128,320]{0,1:T(8,128)(2,1)}, u32[]{:S(2)}, u32[]{:S(2)}) collective-permute-start(bf16[128,320]{0,1:T(8,128)(2,1)} %get-tuple-element.298), channel_id=1, source_target_pairs={{0,8},{4,12},{8,0},{12,4},{16,24},{20,28},{24,16},{28,20},{32,40},... | collective-permute-start | bytes 245768 | tf_op jit(solution)/shard_map/ppermute | solution.py:337
  100.4 44.4 %collective-permute-start = (bf16[128,320]{0,1:T(8,128)(2,1)}, bf16[128,320]{0,1:T(8,128)(2,1)}, u32[]{:S(2)}, u32[]{:S(2)}) collective-permute-start(bf16[128,320]{0,1:T(8,128)(2,1)} %get-tuple-element.298), channel_id=1, source_target_pairs={{0,4},{4,0},{8,12},{12,8},{16,20},{20,16},{24,28},{28,24},{32,36},... | collective-permute-start | bytes 245768 | tf_op jit(solution)/shard_map/ppermute | solution.py:337
  112.1 1.8 %copy-start.8 = (f32[128,2,4,80]{0,3,2,1:T(8,128)S(1)}, f32[128,2,4,80]{0,3,2,1:T(8,128)}, u32[]{:S(2)}) copy-start(f32[128,2,4,80]{0,3,2,1:T(8,128)} %custom-call) | copy-start | bytes 983044
  161.3 4.3 %copy-start.1 = (bf16[160,1024]{1,0:T(8,128)(2,1)S(1)}, bf16[160,1024]{1,0:T(8,128)(2,1)}, u32[]{:S(2)}) copy-start(bf16[160,1024]{1,0:T(8,128)(2,1)} %param.20) | copy-start | bytes 983044
  161.3 4.3 %copy-start.2 = (bf16[160,1024]{1,0:T(8,128)(2,1)S(1)}, bf16[160,1024]{1,0:T(8,128)(2,1)}, u32[]{:S(2)}) copy-start(bf16[160,1024]{1,0:T(8,128)(2,1)} %param.19) | copy-start | bytes 983044

commit v15 on v13

--- a/solution.py
+++ b/solution.py
@@ -33,7 +33,7 @@
 
 
 WIDE = ("z", "x", "c")
-RING_SUBS = 8
+RING_SUBS = 2
 
 
 def gather_kernel(nz, nx, nc, nn, blk_ref, cache_ref, tok_ref, out_ref, cache_out, tok_out,

time: 169 us -> 169 us (level)
  the two profiles are of different devices: /device:TPU:12 before, /device:TPU:1 now
where the time goes in v15:
time: 169 us; the launch traced here: 167 us
  Pallas kernels  67.9 us (40%)
  matrix products  33.4 us (20%)
  local copies, waits for them, and re-layouts  23.5 us (14%)
  other arithmetic  16.9 us (10%)
  starting transfers between devices  11.3 us (7%)
  blocking collectives  10.6 us (6%)
  between operations  2.94 us (2%)
    pallas_call x1, Pallas kernels, gather_wide(): pl.pallas_call(functools.partial(gather_kernel, nz, nx, nc, nn), out_shap...  67.9 us
    reshape x1, local copies, waits for them, and re-layouts, shards(): all_weights = gathered.reshape(-1, joined_width)  15.3 us
    dot_general x9, matrix products, step(): jnp.einsum('tgrk,gdk->tgrd', weights.astype(jnp.bfloat16), block_values,...  12.2 us
    dot_general x9, matrix products, step(): jnp.einsum('tgrd,gdk->tgrk', queries, block_keys, preferred_element_type=...  12 us
    ppermute x3, starting transfers between devices, group_route_pieces(): pieces.append(lax.ppermute(block, WIDE, route))  11.3 us
    all_gather x1, blocking collectives, shards(): all_heads = lax.all_gather(attended, 'narrow', axis=1, tiled=True)  10.6 us
    dot_general x1, matrix products, shards(): qkv_sum = jnp.dot(normed, qkv, preferred_element_type=jnp.float32)  4.81 us
    dot_general x1, matrix products, shards(): jnp.dot(all_heads, out_rows, preferred_element_type=jnp.float32)  4.3 us
  transfers between devices with their start and end apart: 3, of which 0 were waited for; matrix products, arithmetic and copies ran while one was open for 24% of the time, Pallas kernels for 0%

profile of v15, /device:TPU:1, one launch (start us, length us, event | category | flops | bytes accessed | tf_op | source)
XLA Modules:
  0.0 167.0 jit_solution(5270107176838231682)
XLA Ops:
  2.3 2.0 %pad_maximum_fusion.1.cache_ref = bf16[320,1024]{1,0:T(8,128)(2,1)} fusion(bf16[160,1024]{1,0:T(8,128)(2,1)} %param.20, bf16[160,1024]{1,0:T(8,128)(2,1)} %param.19), kind=kLoop, calls=%fused_computation.59 | loop fusion | flops 1310720 | bytes 1310720 | tf_op jit(solution)/shard_map/concatenate | solution.py:346
  4.3 67.9 %shard_map.130 = (bf16[128,250,128]{2,1,0:T(8,128)(2,1)}, bf16[4,320,1024]{2,1,0:T(8,128)(2,1)}, bf16[4,128,640]{2,1,0:T(8,128)(2,1)}) custom-call(bf16[250,128]{1,0:T(8,128)(2,1)} %reshape.239.blk_ref, bf16[320,1024]{1,0:T(8,128)(2,1)} %pad_maximum_fusion.1.cache_ref, bf16[128,640]{1,0:T(8,128)(2,1)} %tok_ref.1), custom_call_target="tpu_custom_call" | custom-call | bytes 16384000 | tf_op jit(solution)/shard_map/pallas_call | solution.py:173
  72.2 15.3 %reshape.241 = bf16[2560,1600]{1,0:T(8,128)(2,1)} reshape(bf16[128,250,128]{2,1,0:T(8,128)(2,1)} %get-tuple-element.209) | data formatting | bytes 16384000 | tf_op jit(solution)/shard_map/reshape | solution.py:349
  87.8 4.8 %fusion.23 = f32[128,960]{0,1:T(8,128)S(1)} fusion(bf16[2560,1600]{1,0:T(8,128)(2,1)} %reshape.241, f32[2560]{0:T(1024)S(1)} %convert_element_type.43, f32[128]{0:T(128)S(1)} %add_rsqrt_fusion, bf16[128,640]{1,0:T(8,128)(2,1)S(1)} %get-tuple-element.282, bf16[128,640]{1,0:T(8,128)(2,1)S(1)} %get-tuple-element.283, ...), kind=kOutput, calls=%fused_computation.30 | convolution fusion | flops 632750080 | bytes 6400512 | tf_op jit(solution)/shard_map/dot_general | solution.py:360
  95.3 4.0 %collective-permute-start.2 = (bf16[128,320]{0,1:T(8,128)(2,1)}, bf16[128,320]{0,1:T(8,128)(2,1)}, u32[]{:S(2)}, u32[]{:S(2)}) collective-permute-start(bf16[128,320]{0,1:T(8,128)(2,1)} %get-tuple-element.298), channel_id=1, source_target_pairs={{0,12},{4,8},{8,4},{12,0},{16,28},{20,24},{24,20},{28,16},{32,44},... | collective-permute-start | bytes 245768 | tf_op jit(solution)/shard_map/ppermute | solution.py:337
  99.3 5.4 %collective-permute-start.1 = (bf16[128,320]{0,1:T(8,128)(2,1)}, bf16[128,320]{0,1:T(8,128)(2,1)}, u32[]{:S(2)}, u32[]{:S(2)}) collective-permute-start(bf16[128,320]{0,1:T(8,128)(2,1)} %get-tuple-element.298), channel_id=1, source_target_pairs={{0,8},{4,12},{8,0},{12,4},{16,24},{20,28},{24,16},{28,20},{32,40},... | collective-permute-start | bytes 245768 | tf_op jit(solution)/shard_map/ppermute | solution.py:337
  104.7 1.9 %collective-permute-start = (bf16[128,320]{0,1:T(8,128)(2,1)}, bf16[128,320]{0,1:T(8,128)(2,1)}, u32[]{:S(2)}, u32[]{:S(2)}) collective-permute-start(bf16[128,320]{0,1:T(8,128)(2,1)} %get-tuple-element.298), channel_id=1, source_target_pairs={{0,4},{4,0},{8,12},{12,8},{16,20},{20,16},{24,28},{28,24},{32,36},... | collective-permute-start | bytes 245768 | tf_op jit(solution)/shard_map/ppermute | solution.py:337
  107.9 1.3 dynamic_slice.61
  109.2 1.8 %broadcast_compare_fusion = pred[4096]{0:T(1024)(128)(4,1)S(1)} fusion(s32[]{:T(128)} %bitcast.2, s32[]{:T(128)} %bitcast.1, s32[]{:T(128)} %bitcast), kind=kLoop, calls=%fused_computation.123 | loop fusion | flops 163840 | bytes 4108 | tf_op jit(solution)/shard_map/lt | solution.py:398
  111.1 1.8 %add_select_fusion = s32[4096]{0:T(1024)S(1)} fusion(s32[]{:T(128)} %bitcast.2, s32[]{:T(128)} %bitcast.1, s32[]{:T(128)} %bitcast), kind=kLoop, calls=%fused_computation.104 | loop fusion | flops 159744 | bytes 16396 | tf_op jit(solution)/shard_map/jit(remainder)/select_n | solution.py:390
  115.4 1.7 %fusion.82 = (bf16[160,4096]{1,0:T(8,128)(2,1)}, bf16[160,4096]{1,0:T(8,128)(2,1)}) fusion(bf16[320,4096]{1,0:T(8,128)(2,1)S(1)} %pad_maximum_fusion), kind=kLoop, calls=%fused_computation.146 | loop fusion | bytes 5242880 | tf_op jit(solution)/shard_map/slice | solution.py:382
  117.2 30.5 %while.5 = (s32[]{:T(128)}, f32[128,2,4,80]{0,3,2,1:T(8,128)S(1)}, f32[128,2,4]{0,2,1:T(4,128)S(1)}, f32[128,2,4]{0,2,1:T(4,128)S(1)}, pred[4096]{0:T(1024)(128)...) while((s32[]{:T(128)}, f32[128,2,4,80]{0,3,2,1:T(8,128)S(1)}, ...), condition=%wide.region_4.5_spmd.clone, body=%wide.region_1.4_spmd.clone.sunk | while | flops 174118016 | bytes 7774939 | solution.py:278
  117.6 1.4 fusion.99
  119.5 1.5 fusion.102
  121.4 1.4 fusion.99
  123.3 1.5 fusion.102
  125.2 1.4 fusion.99
  127.2 1.5 fusion.102
  129.0 1.4 fusion.99
  131.0 1.5 fusion.102
  132.9 1.4 fusion.99
  134.8 1.5 fusion.102
  136.7 1.4 fusion.99
  138.6 1.5 fusion.102
  140.5 1.4 fusion.99
  142.4 1.5 fusion.102
  144.3 1.4 fusion.99
  146.2 1.5 fusion.102
  148.1 1.0 pad_maximum_fusion.3
  150.8 10.6 %all_gather.3 = bf16[128,2560]{0,1:T(8,128)(2,1)S(1)} all-gather(bf16[128,640]{0,1:T(8,128)(2,1)S(1)} %bitcast.142), channel_id=1, replica_groups=mesh['z'=16,'x'=4,'c'=2,'narrow'=4] {'narrow'}, dimensions={1}, use_global_device_ids=true | all-gather | bytes 819200 | tf_op jit(solution)/shard_map/all_gather | solution.py:417
  161.3 4.3 %fusion.38 = bf16[128,640]{1,0:T(8,128)(2,1)} fusion(bf16[128,2560]{0,1:T(8,128)(2,1)S(1)} %all_gather.3, bf16[2560,1600]{1,0:T(8,128)(2,1)} %reshape.241), kind=kOutput, calls=%fused_computation.55 | convolution fusion | flops 419512320 | bytes 4096000 | tf_op jit(solution)/shard_map/dot_general | solution.py:418
  165.6 1.4 fusion.51
  (123 shorter events, 15.1 us)
Async XLA Ops:
  72.2 15.3 %copy-start.5 = (bf16[2560]{0:T(1024)(128)(2,1)S(1)}, bf16[2560]{0:T(1024)(128)(2,1)}, u32[]{:S(2)}) copy-start(bf16[2560]{0:T(1024)(128)(2,1)} %param.14) | copy-start | bytes 15364
  72.2 15.3 %copy-start.3 = (bf16[4,128,640]{2,1,0:T(8,128)(2,1)S(1)}, bf16[4,128,640]{2,1,0:T(8,128)(2,1)}, u32[]{:S(2)}) copy-start(bf16[4,128,640]{2,1,0:T(8,128)(2,1)} %get-tuple-element.208) | copy-start | bytes 1966084
  87.7 4.9 %copy-start.6 = (s32[32]{0:T(128)S(1)}, s32[32]{0:T(128)}, u32[]{:S(2)}) copy-start(s32[32]{0:T(128)} %param.21) | copy-start | bytes 388
  87.8 19.6 %copy-start.7 = (s32[32]{0:T(128)S(1)}, s32[32]{0:T(128)}, u32[]{:S(2)}) copy-start(s32[32]{0:T(128)} %param.22) | copy-start | bytes 388
  87.8 27.1 %copy-start = (bf16[4,320,1024]{2,1,0:T(8,128)(2,1)S(1)}, bf16[4,320,1024]{2,1,0:T(8,128)(2,1)}, u32[]{:S(2)}) copy-start(bf16[4,320,1024]{2,1,0:T(8,128)(2,1)} %get-tuple-element.207) | copy-start | bytes 7864324
  94.1 0.6 copy-start.4
  95.3 52.7 %collective-permute-start.2 = (bf16[128,320]{0,1:T(8,128)(2,1)}, bf16[128,320]{0,1:T(8,128)(2,1)}, u32[]{:S(2)}, u32[]{:S(2)}) collective-permute-start(bf16[128,320]{0,1:T(8,128)(2,1)} %get-tuple-element.298), channel_id=1, source_target_pairs={{0,12},{4,8},{8,4},{12,0},{16,28},{20,24},{24,20},{28,16},{32,44},... | collective-permute-start | bytes 245768 | tf_op jit(solution)/shard_map/ppermute | solution.py:337
  99.3 48.7 %collective-permute-start.1 = (bf16[128,320]{0,1:T(8,128)(2,1)}, bf16[128,320]{0,1:T(8,128)(2,1)}, u32[]{:S(2)}, u32[]{:S(2)}) collective-permute-start(bf16[128,320]{0,1:T(8,128)(2,1)} %get-tuple-element.298), channel_id=1, source_target_pairs={{0,8},{4,12},{8,0},{12,4},{16,24},{20,28},{24,16},{28,20},{32,40},... | collective-permute-start | bytes 245768 | tf_op jit(solution)/shard_map/ppermute | solution.py:337
  104.7 43.4 %collective-permute-start = (bf16[128,320]{0,1:T(8,128)(2,1)}, bf16[128,320]{0,1:T(8,128)(2,1)}, u32[]{:S(2)}, u32[]{:S(2)}) collective-permute-start(bf16[128,320]{0,1:T(8,128)(2,1)} %get-tuple-element.298), channel_id=1, source_target_pairs={{0,4},{4,0},{8,12},{12,8},{16,20},{20,16},{24,28},{28,24},{32,36},... | collective-permute-start | bytes 245768 | tf_op jit(solution)/shard_map/ppermute | solution.py:337
  115.4 1.8 %copy-start.8 = (f32[128,2,4,80]{0,3,2,1:T(8,128)S(1)}, f32[128,2,4,80]{0,3,2,1:T(8,128)}, u32[]{:S(2)}) copy-start(f32[128,2,4,80]{0,3,2,1:T(8,128)} %custom-call) | copy-start | bytes 983044
  161.3 4.3 %copy-start.1 = (bf16[160,1024]{1,0:T(8,128)(2,1)S(1)}, bf16[160,1024]{1,0:T(8,128)(2,1)}, u32[]{:S(2)}) copy-start(bf16[160,1024]{1,0:T(8,128)(2,1)} %param.20) | copy-start | bytes 983044
  161.3 4.3 %copy-start.2 = (bf16[160,1024]{1,0:T(8,128)(2,1)S(1)}, bf16[160,1024]{1,0:T(8,128)(2,1)}, u32[]{:S(2)}) copy-start(bf16[160,1024]{1,0:T(8,128)(2,1)} %param.19) | copy-start | bytes 983044

commit v16 on v12

--- a/solution.py
+++ b/solution.py
@@ -85,21 +85,6 @@
         cp.start()
         sends.append(cp)
     locals_[0].wait()
-    for k in range(1, 2 * nc):
-        cp = pltpu.make_async_remote_copy(
-            src_ref=cache_ref, dst_ref=cache_out.at[place],
-            send_sem=cache_send.at[k], recv_sem=cache_recv.at[k],
-            device_id=group_dev(place ^ k), device_id_type=MESH_ID)
-        cp.start()
-        sends.append(cp)
-    for k in range(1, nn):
-        cp = pltpu.make_async_remote_copy(
-            src_ref=tok_ref, dst_ref=tok_out.at[n],
-            send_sem=tok_send.at[k], recv_sem=tok_recv.at[k],
-            device_id=(z, x, c, lax.rem(n + k, nn)), device_id_type=MESH_ID)
-        cp.start()
-        sends.append(cp)
-
     subs = RING_SUBS
     sub_len = per_plane // subs
 
@@ -141,6 +126,21 @@
             cp = ring_copy(s, j, send_z, (dst_z, x, c, n))
             cp.start()
             sends.append(cp)
+        if s == 1:
+            for k in range(1, 2 * nc):
+                cp = pltpu.make_async_remote_copy(
+                    src_ref=cache_ref, dst_ref=cache_out.at[place],
+                    send_sem=cache_send.at[k], recv_sem=cache_recv.at[k],
+                    device_id=group_dev(place ^ k), device_id_type=MESH_ID)
+                cp.start()
+                sends.append(cp)
+            for k in range(1, nn):
+                cp = pltpu.make_async_remote_copy(
+                    src_ref=tok_ref, dst_ref=tok_out.at[n],
+                    send_sem=tok_send.at[k], recv_sem=tok_recv.at[k],
+                    device_id=(z, x, c, lax.rem(n + k, nn)), device_id_type=MESH_ID)
+                cp.start()
+                sends.append(cp)
     last_z = lax.rem(z - step_dir * half + 2 * nz, nz)
     for j in range(subs):
         ring_copy(half, j, last_z, (src_z, x, c, n)).wait_recv()

time: 168 us -> 168 us (level)
  the two profiles are of different devices: /device:TPU:12 before, /device:TPU:1 now
where the time goes in v16:
time: 168 us; the launch traced here: 165 us
  Pallas kernels  65.2 us (39%)
  matrix products  33.4 us (20%)
  local copies, waits for them, and re-layouts  23.5 us (14%)
  other arithmetic  16.9 us (10%)
  starting transfers between devices  11.2 us (7%)
  blocking collectives  11.1 us (7%)
  between operations  2.94 us (2%)
    pallas_call x1, Pallas kernels, gather_wide(): pl.pallas_call(functools.partial(gather_kernel, nz, nx, nc, nn), out_shap...  65.2 us
    reshape x1, local copies, waits for them, and re-layouts, shards(): all_weights = gathered.reshape(-1, joined_width)  15.3 us
    dot_general x9, matrix products, step(): jnp.einsum('tgrk,gdk->tgrd', weights.astype(jnp.bfloat16), block_values,...  12.2 us
    dot_general x9, matrix products, step(): jnp.einsum('tgrd,gdk->tgrk', queries, block_keys, preferred_element_type=...  12 us
    ppermute x3, starting transfers between devices, group_route_pieces(): pieces.append(lax.ppermute(block, WIDE, route))  11.2 us
    all_gather x1, blocking collectives, shards(): all_heads = lax.all_gather(attended, 'narrow', axis=1, tiled=True)  11.1 us
    dot_general x1, matrix products, shards(): qkv_sum = jnp.dot(normed, qkv, preferred_element_type=jnp.float32)  4.81 us
    dot_general x1, matrix products, shards(): jnp.dot(all_heads, out_rows, preferred_element_type=jnp.float32)  4.3 us
  transfers between devices with their start and end apart: 3, of which 0 were waited for; matrix products, arithmetic and copies ran while one was open for 24% of the time, Pallas kernels for 0%

profile of v16, /device:TPU:1, one launch (start us, length us, event | category | flops | bytes accessed | tf_op | source)
XLA Modules:
  0.0 164.9 jit_solution(3783227034797301169)
XLA Ops:
  2.3 2.0 %pad_maximum_fusion.1.cache_ref = bf16[320,1024]{1,0:T(8,128)(2,1)} fusion(bf16[160,1024]{1,0:T(8,128)(2,1)} %param.20, bf16[160,1024]{1,0:T(8,128)(2,1)} %param.19), kind=kLoop, calls=%fused_computation.59 | loop fusion | flops 1310720 | bytes 1310720 | tf_op jit(solution)/shard_map/concatenate | solution.py:346
  4.3 65.2 %shard_map.130 = (bf16[128,250,128]{2,1,0:T(8,128)(2,1)}, bf16[4,320,1024]{2,1,0:T(8,128)(2,1)}, bf16[4,128,640]{2,1,0:T(8,128)(2,1)}) custom-call(bf16[250,128]{1,0:T(8,128)(2,1)} %reshape.239.blk_ref, bf16[320,1024]{1,0:T(8,128)(2,1)} %pad_maximum_fusion.1.cache_ref, bf16[128,640]{1,0:T(8,128)(2,1)} %tok_ref.1), custom_call_target="tpu_custom_call" | custom-call | bytes 16384000 | tf_op jit(solution)/shard_map/pallas_call | solution.py:173
  69.5 15.3 %reshape.241 = bf16[2560,1600]{1,0:T(8,128)(2,1)} reshape(bf16[128,250,128]{2,1,0:T(8,128)(2,1)} %get-tuple-element.209) | data formatting | bytes 16384000 | tf_op jit(solution)/shard_map/reshape | solution.py:349
  85.1 4.8 %fusion.23 = f32[128,960]{0,1:T(8,128)S(1)} fusion(bf16[2560,1600]{1,0:T(8,128)(2,1)} %reshape.241, f32[2560]{0:T(1024)S(1)} %convert_element_type.43, f32[128]{0:T(128)S(1)} %add_rsqrt_fusion, bf16[128,640]{1,0:T(8,128)(2,1)S(1)} %get-tuple-element.282, bf16[128,640]{1,0:T(8,128)(2,1)S(1)} %get-tuple-element.283, ...), kind=kOutput, calls=%fused_computation.30 | convolution fusion | flops 632750080 | bytes 6400512 | tf_op jit(solution)/shard_map/dot_general | solution.py:360
  92.7 5.7 %collective-permute-start.2 = (bf16[128,320]{0,1:T(8,128)(2,1)}, bf16[128,320]{0,1:T(8,128)(2,1)}, u32[]{:S(2)}, u32[]{:S(2)}) collective-permute-start(bf16[128,320]{0,1:T(8,128)(2,1)} %get-tuple-element.298), channel_id=1, source_target_pairs={{0,12},{4,8},{8,4},{12,0},{16,28},{20,24},{24,20},{28,16},{32,44},... | collective-permute-start | bytes 245768 | tf_op jit(solution)/shard_map/ppermute | solution.py:337
  98.4 3.6 %collective-permute-start.1 = (bf16[128,320]{0,1:T(8,128)(2,1)}, bf16[128,320]{0,1:T(8,128)(2,1)}, u32[]{:S(2)}, u32[]{:S(2)}) collective-permute-start(bf16[128,320]{0,1:T(8,128)(2,1)} %get-tuple-element.298), channel_id=1, source_target_pairs={{0,8},{4,12},{8,0},{12,4},{16,24},{20,28},{24,16},{28,20},{32,40},... | collective-permute-start | bytes 245768 | tf_op jit(solution)/shard_map/ppermute | solution.py:337
  102.0 1.9 %collective-permute-start = (bf16[128,320]{0,1:T(8,128)(2,1)}, bf16[128,320]{0,1:T(8,128)(2,1)}, u32[]{:S(2)}, u32[]{:S(2)}) collective-permute-start(bf16[128,320]{0,1:T(8,128)(2,1)} %get-tuple-element.298), channel_id=1, source_target_pairs={{0,4},{4,0},{8,12},{12,8},{16,20},{20,16},{24,28},{28,24},{32,36},... | collective-permute-start | bytes 245768 | tf_op jit(solution)/shard_map/ppermute | solution.py:337
  105.2 1.3 dynamic_slice.61
  106.5 1.8 %broadcast_compare_fusion = pred[4096]{0:T(1024)(128)(4,1)S(1)} fusion(s32[]{:T(128)} %bitcast.2, s32[]{:T(128)} %bitcast.1, s32[]{:T(128)} %bitcast), kind=kLoop, calls=%fused_computation.123 | loop fusion | flops 163840 | bytes 4108 | tf_op jit(solution)/shard_map/lt | solution.py:398
  108.4 1.8 %add_select_fusion = s32[4096]{0:T(1024)S(1)} fusion(s32[]{:T(128)} %bitcast.2, s32[]{:T(128)} %bitcast.1, s32[]{:T(128)} %bitcast), kind=kLoop, calls=%fused_computation.104 | loop fusion | flops 159744 | bytes 16396 | tf_op jit(solution)/shard_map/jit(remainder)/select_n | solution.py:390
  112.7 1.7 %fusion.82 = (bf16[160,4096]{1,0:T(8,128)(2,1)}, bf16[160,4096]{1,0:T(8,128)(2,1)}) fusion(bf16[320,4096]{1,0:T(8,128)(2,1)S(1)} %pad_maximum_fusion), kind=kLoop, calls=%fused_computation.146 | loop fusion | bytes 5242880 | tf_op jit(solution)/shard_map/slice | solution.py:382
  114.5 30.5 %while.5 = (s32[]{:T(128)}, f32[128,2,4,80]{0,3,2,1:T(8,128)S(1)}, f32[128,2,4]{0,2,1:T(4,128)S(1)}, f32[128,2,4]{0,2,1:T(4,128)S(1)}, pred[4096]{0:T(1024)(128)...) while((s32[]{:T(128)}, f32[128,2,4,80]{0,3,2,1:T(8,128)S(1)}, ...), condition=%wide.region_4.5_spmd.clone, body=%wide.region_1.4_spmd.clone.sunk | while | flops 174118016 | bytes 7774939 | solution.py:278
  114.9 1.4 fusion.99
  116.8 1.5 fusion.102
  118.7 1.4 fusion.99
  120.6 1.5 fusion.102
  122.5 1.4 fusion.99
  124.4 1.5 fusion.102
  126.3 1.4 fusion.99
  128.2 1.5 fusion.102
  130.1 1.4 fusion.99
  132.1 1.5 fusion.102
  133.9 1.4 fusion.99
  135.9 1.5 fusion.102
  137.8 1.4 fusion.99
  139.7 1.5 fusion.102
  141.6 1.4 fusion.99
  143.5 1.5 fusion.102
  145.3 1.0 pad_maximum_fusion.3
  148.0 11.1 %all_gather.3 = bf16[128,2560]{0,1:T(8,128)(2,1)S(1)} all-gather(bf16[128,640]{0,1:T(8,128)(2,1)S(1)} %bitcast.142), channel_id=1, replica_groups=mesh['z'=16,'x'=4,'c'=2,'narrow'=4] {'narrow'}, dimensions={1}, use_global_device_ids=true | all-gather | bytes 819200 | tf_op jit(solution)/shard_map/all_gather | solution.py:417
  159.2 4.3 %fusion.38 = bf16[128,640]{1,0:T(8,128)(2,1)} fusion(bf16[128,2560]{0,1:T(8,128)(2,1)S(1)} %all_gather.3, bf16[2560,1600]{1,0:T(8,128)(2,1)} %reshape.241), kind=kOutput, calls=%fused_computation.55 | convolution fusion | flops 419512320 | bytes 4096000 | tf_op jit(solution)/shard_map/dot_general | solution.py:418
  163.5 1.4 fusion.51
  (123 shorter events, 15.1 us)
Async XLA Ops:
  69.5 15.3 %copy-start.5 = (bf16[2560]{0:T(1024)(128)(2,1)S(1)}, bf16[2560]{0:T(1024)(128)(2,1)}, u32[]{:S(2)}) copy-start(bf16[2560]{0:T(1024)(128)(2,1)} %param.14) | copy-start | bytes 15364
  69.5 15.3 %copy-start.3 = (bf16[4,128,640]{2,1,0:T(8,128)(2,1)S(1)}, bf16[4,128,640]{2,1,0:T(8,128)(2,1)}, u32[]{:S(2)}) copy-start(bf16[4,128,640]{2,1,0:T(8,128)(2,1)} %get-tuple-element.208) | copy-start | bytes 1966084
  85.1 4.9 %copy-start.6 = (s32[32]{0:T(128)S(1)}, s32[32]{0:T(128)}, u32[]{:S(2)}) copy-start(s32[32]{0:T(128)} %param.21) | copy-start | bytes 388
  85.1 19.5 %copy-start.7 = (s32[32]{0:T(128)S(1)}, s32[32]{0:T(128)}, u32[]{:S(2)}) copy-start(s32[32]{0:T(128)} %param.22) | copy-start | bytes 388
  85.1 27.1 %copy-start = (bf16[4,320,1024]{2,1,0:T(8,128)(2,1)S(1)}, bf16[4,320,1024]{2,1,0:T(8,128)(2,1)}, u32[]{:S(2)}) copy-start(bf16[4,320,1024]{2,1,0:T(8,128)(2,1)} %get-tuple-element.207) | copy-start | bytes 7864324
  91.4 0.6 copy-start.4
  92.7 52.6 %collective-permute-start.2 = (bf16[128,320]{0,1:T(8,128)(2,1)}, bf16[128,320]{0,1:T(8,128)(2,1)}, u32[]{:S(2)}, u32[]{:S(2)}) collective-permute-start(bf16[128,320]{0,1:T(8,128)(2,1)} %get-tuple-element.298), channel_id=1, source_target_pairs={{0,12},{4,8},{8,4},{12,0},{16,28},{20,24},{24,20},{28,16},{32,44},... | collective-permute-start | bytes 245768 | tf_op jit(solution)/shard_map/ppermute | solution.py:337
  98.4 46.9 %collective-permute-start.1 = (bf16[128,320]{0,1:T(8,128)(2,1)}, bf16[128,320]{0,1:T(8,128)(2,1)}, u32[]{:S(2)}, u32[]{:S(2)}) collective-permute-start(bf16[128,320]{0,1:T(8,128)(2,1)} %get-tuple-element.298), channel_id=1, source_target_pairs={{0,8},{4,12},{8,0},{12,4},{16,24},{20,28},{24,16},{28,20},{32,40},... | collective-permute-start | bytes 245768 | tf_op jit(solution)/shard_map/ppermute | solution.py:337
  102.0 43.4 %collective-permute-start = (bf16[128,320]{0,1:T(8,128)(2,1)}, bf16[128,320]{0,1:T(8,128)(2,1)}, u32[]{:S(2)}, u32[]{:S(2)}) collective-permute-start(bf16[128,320]{0,1:T(8,128)(2,1)} %get-tuple-element.298), channel_id=1, source_target_pairs={{0,4},{4,0},{8,12},{12,8},{16,20},{20,16},{24,28},{28,24},{32,36},... | collective-permute-start | bytes 245768 | tf_op jit(solution)/shard_map/ppermute | solution.py:337
  112.7 1.8 %copy-start.8 = (f32[128,2,4,80]{0,3,2,1:T(8,128)S(1)}, f32[128,2,4,80]{0,3,2,1:T(8,128)}, u32[]{:S(2)}) copy-start(f32[128,2,4,80]{0,3,2,1:T(8,128)} %custom-call) | copy-start | bytes 983044
  159.2 4.3 %copy-start.1 = (bf16[160,1024]{1,0:T(8,128)(2,1)S(1)}, bf16[160,1024]{1,0:T(8,128)(2,1)}, u32[]{:S(2)}) copy-start(bf16[160,1024]{1,0:T(8,128)(2,1)} %param.20) | copy-start | bytes 983044
  159.2 4.3 %copy-start.2 = (bf16[160,1024]{1,0:T(8,128)(2,1)S(1)}, bf16[160,1024]{1,0:T(8,128)(2,1)}, u32[]{:S(2)}) copy-start(bf16[160,1024]{1,0:T(8,128)(2,1)} %param.19) | copy-start | bytes 983044
